TPU v7x, 128 devices: a whole 4x4x4 slice. The times are simulated.
128 devices in a mesh: gx: 4 (over z), gy: 32 (over y, x, core).
Axes of the slice: x: 4, y: 4, z: 4, core: 2. Of those that a mesh axis runs over, the one named last changes fastest.
Arguments:
- densities: float32 [2048, 2, 128, 128], P(('gx', 'gy')), may hold values from -6 to 6
- hamiltonian: float32 [2, 128, 128], replicated, may hold values from -3 to 3, as said below
- couplings: float32 [4, 128, 128], replicated, may hold values from -1 to 1, as said below
- decay_rates: float32 [4], replicated, may hold values from 0.5 to 2
- correlation: float32 [2, 4], replicated, may hold values from 0.25 to 1.5
- upper_link: int32 [2048, 4], P(('gx', 'gy')), may hold values from 0 to 2048, as said below
- lower_link: int32 [2048, 4], P(('gx', 'gy')), may hold values from 0 to 2048, as said below
- occupation: int32 [2048, 4], P(('gx', 'gy')), may hold values from 0 to 3
Outputs:
- advanced: float32 [2048, 2, 128, 128], P(('gx', 'gy'))
Inputs may be any that keep to these rules, and one draw needn't show every extreme that they name: For every bath b, upper_link[g,b] = h with h < 2048 exactly when lower_link[h,b] = g, and then occupation[h,b] = occupation[g,b] + 1; the value 2048 means no link. Matrix g is held by device g // 16, devices numbered in the order gx+gy. lower_link[g,b] < 2048 exactly when occupation[g,b] > 0. Links of the first two baths join two matrices of one device. Links of the third bath join matrices of two devices with the same gx index, and at most one matrix of a device is linked to matrices of any one other device; this bound is reached. Links of the fourth bath join matrices of two devices with the same gy index, and at most 2 matrices of a device are linked to matrices of any one other device; this bound is reached. hamiltonian[0] is symmetric and hamiltonian[1] antisymmetric. Each couplings[b] is symmetric.
All inputs are finite; a program needn't handle non-finite values.
Results may differ from a plain program's by a relative error of at most 0.0001.
Values sent between devices are 32-bit elements; how exact they have to be, the bound alone decides.
No kernel may reach another device: no remote copies, remote signals or barrier semaphores. Data moves between devices by JAX's collectives and lax.ppermute only.
A program may use at most 192 MiB of HBM per device.

v0:
```python
import jax
import jax.numpy as jnp
from jax import lax
from jax.sharding import PartitionSpec as P

XCAP = 2


step_size = 0.1
highest = lax.Precision.HIGHEST


def left_apply(matrix, operand):
    return jnp.einsum("ij,...jk->...ik", matrix, operand, precision=highest)


def right_apply(operand, matrix):
    return jnp.einsum("...ij,jk->...ik", operand, matrix, precision=highest)


def select_table(index, live, pool_rows):
    pool_ids = jnp.arange(pool_rows, dtype=jnp.int32)
    return ((index[:, None] == pool_ids[None, :]) & live[:, None]).astype(jnp.float32)


def select_rows(table, pool):
    return jnp.einsum("rp,pcij->rcij", table, pool, precision=highest)


def link_plan(targets, usable, partner, sources, partner_count, capacity):
    entry_ids = jnp.arange(targets.shape[0], dtype=jnp.int32)
    same_partner = (partner[:, None] == partner[None, :]) & usable[:, None] & usable[None, :]
    earlier = entry_ids[None, :] < entry_ids[:, None]
    repeated = jnp.any((targets[:, None] == targets[None, :]) & earlier & usable[None, :], axis=1)
    first_seen = usable & jnp.logical_not(repeated)
    recv_rank = jnp.sum(
        same_partner & first_seen[None, :] & (targets[None, :] < targets[:, None]), axis=1
    )
    recv_place = partner * capacity + recv_rank
    pair_repeat = jnp.any(same_partner & (sources[:, None] == sources[None, :]) & earlier, axis=1)
    pair_first = usable & jnp.logical_not(pair_repeat)
    send_rank = jnp.sum(
        same_partner & pair_first[None, :] & (sources[None, :] < sources[:, None]), axis=1
    )
    send_place = partner * capacity + send_rank
    slot_ids = jnp.arange(partner_count * capacity, dtype=jnp.int32)
    matches = (send_place[None, :] == slot_ids[:, None]) & pair_first[None, :]
    send_index = jnp.sum(jnp.where(matches, sources[None, :], 0), axis=1)
    send_live = jnp.any(matches, axis=1)
    return (recv_place, send_index, send_live)


def local(
    densities, hamiltonian, couplings, decay_rates, correlation, upper_link, lower_link, occupation
):
    per_device = densities.shape[0]
    matrix_order = densities.shape[-1]
    bath_count = couplings.shape[0]
    along_y = lax.axis_size("gy")
    along_x = lax.axis_size("gx")
    index_x = lax.axis_index("gx")
    index_y = lax.axis_index("gy")
    own_device = index_x * along_y + index_y
    missing = per_device * along_y * along_x
    targets = jnp.concatenate([upper_link, lower_link], axis=1).reshape(-1)
    sources = jnp.repeat(jnp.arange(per_device, dtype=jnp.int32), 2 * bath_count)
    usable = targets < missing
    holder = targets // per_device
    holder_x = holder // along_y
    holder_y = holder % along_y
    on_device = usable & (holder == own_device)
    in_row = usable & (holder_x == index_x) & (holder != own_device)
    in_column = usable & (holder_y == index_y) & (holder != own_device)
    row_place, row_index, row_live = link_plan(targets, in_row, holder_y, sources, along_y, 1)
    column_place, column_index, column_live = link_plan(
        targets, in_column, holder_x, sources, along_x, XCAP
    )
    local_place = targets - own_device * per_device
    column_start = per_device + along_y
    blank_place = column_start + along_x * XCAP
    row_slot = per_device + row_place
    pool_rows = blank_place + 1
    positions = jnp.where(
        on_device,
        local_place,
        jnp.where(in_row, row_slot, jnp.where(in_column, column_start + column_place, blank_place)),
    )
    positions = positions.reshape(per_device, 2, bath_count)
    always = jnp.ones((per_device,), jnp.bool_)
    upper_tables = [
        select_table(positions[:, 0, bath_index], always, pool_rows)
        for bath_index in range(bath_count)
    ]
    lower_tables = [
        select_table(positions[:, 1, bath_index], always, pool_rows)
        for bath_index in range(bath_count)
    ]
    row_table = select_table(row_index, row_live, per_device)
    column_table = select_table(column_index, column_live, per_device)
    damping = jnp.sum(occupation.astype(jnp.float32) * decay_rates[None, :], axis=1)[:, None, None]
    zero_block = jnp.zeros((1, 2, matrix_order, matrix_order), jnp.float32)

    def neighbour_parts(pooled, bath_index):
        upper_part = select_rows(upper_tables[bath_index], pooled)
        lower_part = select_rows(lower_tables[bath_index], pooled)
        level_weight = occupation[:, bath_index].astype(jnp.float32)[:, None, None]
        real_weight = correlation[0, bath_index] * level_weight
        imag_weight = correlation[1, bath_index] * level_weight
        forward = jnp.stack(
            [
                upper_part[:, 0] + real_weight * lower_part[:, 0] - imag_weight * lower_part[:, 1],
                upper_part[:, 1] + real_weight * lower_part[:, 1] + imag_weight * lower_part[:, 0],
            ],
            axis=1,
        )
        backward = jnp.stack(
            [
                upper_part[:, 0] + real_weight * lower_part[:, 0] + imag_weight * lower_part[:, 1],
                upper_part[:, 1] + real_weight * lower_part[:, 1] - imag_weight * lower_part[:, 0],
            ],
            axis=1,
        )
        return (forward, backward)

    def bath_terms(pooled, pooled_baths):
        operand_pairs = [neighbour_parts(pooled, bath_index) for bath_index in pooled_baths]
        mixed_sum = jnp.zeros((per_device, 2, matrix_order, matrix_order), jnp.float32)
        for bath_index, pair_item in zip(pooled_baths, operand_pairs):
            mixed_sum = mixed_sum + left_apply(couplings[bath_index], pair_item[0])
            mixed_sum = mixed_sum - right_apply(pair_item[1], couplings[bath_index])
        return mixed_sum

    def derive(section_input):
        row_out = select_rows(row_table, section_input)
        column_out = select_rows(column_table, section_input)
        column_in = lax.all_to_all(column_out, "gx", split_axis=0, concat_axis=0, tiled=True)
        row_in = lax.all_to_all(row_out, "gy", split_axis=0, concat_axis=0, tiled=True)
        pooled = jnp.concatenate([section_input, row_in, column_in, zero_block], axis=0)
        mixed = bath_terms(pooled, list(range(bath_count)))
        left_real = left_apply(hamiltonian[0], section_input)
        left_imag = left_apply(hamiltonian[1], section_input)
        right_real = right_apply(section_input, hamiltonian[0])
        right_imag = right_apply(section_input, hamiltonian[1])
        commutator_real = left_real[:, 0] - left_imag[:, 1] - (right_real[:, 0] - right_imag[:, 1])
        commutator_imag = left_real[:, 1] + left_imag[:, 0] - (right_imag[:, 0] + right_real[:, 1])
        out_real = commutator_imag + mixed[:, 1] - damping * section_input[:, 0]
        out_imag = -commutator_real - mixed[:, 0] - damping * section_input[:, 1]
        return jnp.stack([out_real, out_imag], axis=1)

    slope_one = derive(densities)
    slope_two = derive(densities + 0.5 * step_size * slope_one)
    slope_three = derive(densities + 0.5 * step_size * slope_two)
    slope_four = derive(densities + step_size * slope_three)
    return densities + step_size / 6.0 * (
        slope_one + 2.0 * slope_two + 2.0 * slope_three + slope_four
    )


def solution(mesh):
    return jax.shard_map(
        local,
        mesh=mesh,
        in_specs=(
            P(("gx", "gy"), None, None, None),
            P(),
            P(),
            P(),
            P(),
            P(("gx", "gy"), None),
            P(("gx", "gy"), None),
            P(("gx", "gy"), None),
        ),
        out_specs=P(("gx", "gy"), None, None, None),
        check_vma=False,
    )
```

profile of v0, /device:TPU:0, one launch (start us, length us, event | category | flops | bytes accessed | tf_op | source)
XLA Modules:
  0.0 592.8 jit_solution(15777966566923114636)
XLA Ops:
  6.5 5.4 all-to-all-start.1
  15.1 4.4 copy.315
  19.6 7.5 %all-to-all-done.1 = f32[8,2,128,128]{3,2,1,0:T(8,128)S(1)} async-done(((f32[8,2,128,128]{3,2,1,0:T(8,128)}), f32[8,2,128,128]{3,2,1,0:T(8,128)S(1)}, u32[]{:S(2)}, u32[]{:S(2)}) %all-to-all-start.1) | async-done | bytes 1048608 | tf_op jit(solution)/shard_map/all_to_all | solution.py:136
  27.0 7.5 %all-to-all-start = ((f32[32,2,128,128]{3,2,1,0:T(8,128)}), f32[32,2,128,128]{3,2,1,0:T(8,128)}, u32[]{:S(2)}, u32[]{:S(2)}) async-start(f32[32,2,128,128]{3,2,1,0:T(8,128)} %copy.315), calls=%async_computation | async-start | bytes 8388608 | tf_op jit(solution)/shard_map/all_to_all | solution.py:137
  41.5 5.4 multiply_bitcast_fusion.7
  46.9 4.8 convolution_bitcast_fusion.6
  51.7 4.8 convolution_bitcast_fusion.7
  65.0 23.5 %all-to-all-done = f32[32,2,128,128]{3,2,1,0:T(8,128)} async-done(((f32[32,2,128,128]{3,2,1,0:T(8,128)}), f32[32,2,128,128]{3,2,1,0:T(8,128)}, u32[]{:S(2)}, u32[]{:S(2)}) %all-to-all-start) | async-done | bytes 4194336 | tf_op jit(solution)/shard_map/all_to_all | solution.py:137
  88.5 4.6 copy.319
  144.8 4.5 fusion.11
  165.2 4.5 copy.343
  169.7 4.5 all-to-all-done.3
  174.2 6.2 %all-to-all-start.2 = ((f32[32,2,128,128]{3,2,1,0:T(8,128)}), f32[32,2,128,128]{3,2,1,0:T(8,128)}, u32[]{:S(2)}, u32[]{:S(2)}) async-start(f32[32,2,128,128]{3,2,1,0:T(8,128)} %copy.343), calls=%async_computation.2 | async-start | bytes 8388608 | tf_op jit(solution)/shard_map/all_to_all | solution.py:137
  195.0 39.0 %all-to-all-done.2 = f32[32,2,128,128]{3,2,1,0:T(8,128)} async-done(((f32[32,2,128,128]{3,2,1,0:T(8,128)}), f32[32,2,128,128]{3,2,1,0:T(8,128)}, u32[]{:S(2)}, u32[]{:S(2)}) %all-to-all-start.2) | async-done | bytes 4194336 | tf_op jit(solution)/shard_map/all_to_all | solution.py:137
  234.0 4.8 copy.347
  275.4 4.3 fusion.52
  290.6 4.4 fusion.8
  310.7 4.5 copy.369
  315.2 4.5 all-to-all-done.5
  319.7 6.0 %all-to-all-start.4 = ((f32[32,2,128,128]{3,2,1,0:T(8,128)}), f32[32,2,128,128]{3,2,1,0:T(8,128)}, u32[]{:S(2)}, u32[]{:S(2)}) async-start(f32[32,2,128,128]{3,2,1,0:T(8,128)} %copy.369), calls=%async_computation.4 | async-start | bytes 8388608 | tf_op jit(solution)/shard_map/all_to_all | solution.py:137
  340.3 39.2 %all-to-all-done.4 = f32[32,2,128,128]{3,2,1,0:T(8,128)} async-done(((f32[32,2,128,128]{3,2,1,0:T(8,128)}), f32[32,2,128,128]{3,2,1,0:T(8,128)}, u32[]{:S(2)}, u32[]{:S(2)}) %all-to-all-start.4) | async-done | bytes 4194336 | tf_op jit(solution)/shard_map/all_to_all | solution.py:137
  379.5 4.8 copy.373
  420.9 4.5 fusion.36
  436.1 4.4 fusion.5
  449.0 4.3 all-to-all-start.7
  456.7 4.5 copy.395
  461.2 4.6 all-to-all-done.7
  465.8 6.2 %all-to-all-start.6 = ((f32[32,2,128,128]{3,2,1,0:T(8,128)}), f32[32,2,128,128]{3,2,1,0:T(8,128)}, u32[]{:S(2)}, u32[]{:S(2)}) async-start(f32[32,2,128,128]{3,2,1,0:T(8,128)} %copy.395), calls=%async_computation.6 | async-start | bytes 8388608 | tf_op jit(solution)/shard_map/all_to_all | solution.py:137
  487.8 37.8 %all-to-all-done.6 = f32[32,2,128,128]{3,2,1,0:T(8,128)} async-done(((f32[32,2,128,128]{3,2,1,0:T(8,128)}), f32[32,2,128,128]{3,2,1,0:T(8,128)}, u32[]{:S(2)}, u32[]{:S(2)}) %all-to-all-start.6) | async-done | bytes 4194336 | tf_op jit(solution)/shard_map/all_to_all | solution.py:137
  525.6 4.8 copy.399
  567.0 4.3 fusion.20
  582.0 4.4 fusion.2
  (386 shorter events, 311.1 us)
Async XLA Ops:
  1.8 4.8 copy-start.64
  5.4 6.8 %copy-start = (f32[16,2,128,128]{3,2,1,0:T(8,128)S(1)}, f32[16,2,128,128]{3,2,1,0:T(8,128)}, u32[]{:S(2)}) copy-start(f32[16,2,128,128]{3,2,1,0:T(8,128)} %param.8) | copy-start | bytes 6291460
  6.5 20.5 %all-to-all-start.1 = ((f32[8,2,128,128]{3,2,1,0:T(8,128)}), f32[8,2,128,128]{3,2,1,0:T(8,128)S(1)}, u32[]{:S(2)}, u32[]{:S(2)}) async-start(f32[8,2,128,128]{3,2,1,0:T(8,128)} %copy.317), calls=%async_computation.1 | async-start | bytes 2097152 | tf_op jit(solution)/shard_map/all_to_all | solution.py:136
  27.0 61.4 %all-to-all-start = ((f32[32,2,128,128]{3,2,1,0:T(8,128)}), f32[32,2,128,128]{3,2,1,0:T(8,128)}, u32[]{:S(2)}, u32[]{:S(2)}) async-start(f32[32,2,128,128]{3,2,1,0:T(8,128)} %copy.315), calls=%async_computation | async-start | bytes 8388608 | tf_op jit(solution)/shard_map/all_to_all | solution.py:137
  37.0 9.9 %copy-start.19 = (f32[2,128,128]{2,1,0:T(8,128)S(1)}, f32[2,128,128]{2,1,0:T(8,128)}, u32[]{:S(2)}) copy-start(f32[2,128,128]{2,1,0:T(8,128)} %param.9) | copy-start | bytes 393220
  39.5 62.7 %copy-start.100 = (f32[57]{0:T(128)}, f32[57]{0:T(128)S(1)}, u32[]{:S(2)}) copy-start(f32[57]{0:T(128)S(1)} %pad.87.clone) | copy-start | bytes 688
  41.5 51.6 %copy-start.95 = (s32[16]{0:T(128)}, s32[16]{0:T(128)S(1)}, u32[]{:S(2)}) copy-start(s32[16]{0:T(128)S(1)} %get-tuple-element.92) | copy-start | bytes 196
  41.5 54.7 %copy-start.91 = (s32[16]{0:T(128)}, s32[16]{0:T(128)S(1)}, u32[]{:S(2)}) copy-start(s32[16]{0:T(128)S(1)} %get-tuple-element.99) | copy-start | bytes 196
  41.5 57.7 %copy-start.87 = (s32[16]{0:T(128)}, s32[16]{0:T(128)S(1)}, u32[]{:S(2)}) copy-start(s32[16]{0:T(128)S(1)} %get-tuple-element.98) | copy-start | bytes 196
  41.5 60.7 %copy-start.83 = (s32[16]{0:T(128)}, s32[16]{0:T(128)S(1)}, u32[]{:S(2)}) copy-start(s32[16]{0:T(128)S(1)} %get-tuple-element.97) | copy-start | bytes 196
  46.9 58.7 %copy-start.50 = (f32[16]{0:T(128)}, f32[16]{0:T(128)S(1)}, u32[]{:S(2)}) copy-start(f32[16]{0:T(128)S(1)} %get-tuple-element.100) | copy-start | bytes 196
  46.9 58.7 %copy-start.54 = (f32[16]{0:T(128)}, f32[16]{0:T(128)S(1)}, u32[]{:S(2)}) copy-start(f32[16]{0:T(128)S(1)} %get-tuple-element.101) | copy-start | bytes 196
  64.8 28.3 %copy-start.36 = (f32[16,2,128,128]{3,0,2,1:T(8,128)S(1)}, f32[16,2,128,128]{3,0,2,1:T(8,128)}, u32[]{:S(2)}) copy-start(f32[16,2,128,128]{3,0,2,1:T(8,128)} %copy.318) | copy-start | bytes 6291460
  64.8 28.3 %copy-start.37 = (f32[8,2,128,128]{3,0,2,1:T(8,128)S(1)}, f32[8,2,128,128]{3,0,2,1:T(8,128)}, u32[]{:S(2)}) copy-start(f32[8,2,128,128]{3,0,2,1:T(8,128)} %copy.320) | copy-start | bytes 3145732
  158.3 15.9 %all-to-all-start.3 = ((f32[8,2,128,128]{3,2,1,0:T(8,128)}), f32[8,2,128,128]{3,2,1,0:T(8,128)S(1)}, u32[]{:S(2)}, u32[]{:S(2)}) async-start(f32[8,2,128,128]{3,2,1,0:T(8,128)} %copy.345), calls=%async_computation.3 | async-start | bytes 2097152 | tf_op jit(solution)/shard_map/all_to_all | solution.py:136
  174.2 59.8 %all-to-all-start.2 = ((f32[32,2,128,128]{3,2,1,0:T(8,128)}), f32[32,2,128,128]{3,2,1,0:T(8,128)}, u32[]{:S(2)}, u32[]{:S(2)}) async-start(f32[32,2,128,128]{3,2,1,0:T(8,128)} %copy.343), calls=%async_computation.2 | async-start | bytes 8388608 | tf_op jit(solution)/shard_map/all_to_all | solution.py:137
  195.0 43.8 %copy-start.39 = (f32[8,2,128,128]{3,0,2,1:T(8,128)S(1)}, f32[8,2,128,128]{3,0,2,1:T(8,128)}, u32[]{:S(2)}) copy-start(f32[8,2,128,128]{3,0,2,1:T(8,128)} %copy.348) | copy-start | bytes 3145732
  234.0 4.8 copy-start.6
  234.0 4.8 copy-start.96
  234.0 4.8 copy-start.102
  303.8 15.9 %all-to-all-start.5 = ((f32[8,2,128,128]{3,2,1,0:T(8,128)}), f32[8,2,128,128]{3,2,1,0:T(8,128)S(1)}, u32[]{:S(2)}, u32[]{:S(2)}) async-start(f32[8,2,128,128]{3,2,1,0:T(8,128)} %copy.371), calls=%async_computation.5 | async-start | bytes 2097152 | tf_op jit(solution)/shard_map/all_to_all | solution.py:136
  319.7 59.8 %all-to-all-start.4 = ((f32[32,2,128,128]{3,2,1,0:T(8,128)}), f32[32,2,128,128]{3,2,1,0:T(8,128)}, u32[]{:S(2)}, u32[]{:S(2)}) async-start(f32[32,2,128,128]{3,2,1,0:T(8,128)} %copy.369), calls=%async_computation.4 | async-start | bytes 8388608 | tf_op jit(solution)/shard_map/all_to_all | solution.py:137
  340.3 44.0 %copy-start.40 = (f32[8,2,128,128]{3,0,2,1:T(8,128)S(1)}, f32[8,2,128,128]{3,0,2,1:T(8,128)}, u32[]{:S(2)}) copy-start(f32[8,2,128,128]{3,0,2,1:T(8,128)} %copy.374) | copy-start | bytes 3145732
  379.5 4.8 copy-start.7
  379.5 4.8 copy-start.97
  379.5 4.8 copy-start.103
  449.0 16.8 %all-to-all-start.7 = ((f32[8,2,128,128]{3,2,1,0:T(8,128)}), f32[8,2,128,128]{3,2,1,0:T(8,128)}, u32[]{:S(2)}, u32[]{:S(2)}) async-start(f32[8,2,128,128]{3,2,1,0:T(8,128)} %copy.397), calls=%async_computation.7 | async-start | bytes 2097152 | tf_op jit(solution)/shard_map/all_to_all | solution.py:136
  465.8 59.8 %all-to-all-start.6 = ((f32[32,2,128,128]{3,2,1,0:T(8,128)}), f32[32,2,128,128]{3,2,1,0:T(8,128)}, u32[]{:S(2)}, u32[]{:S(2)}) async-start(f32[32,2,128,128]{3,2,1,0:T(8,128)} %copy.395), calls=%async_computation.6 | async-start | bytes 8388608 | tf_op jit(solution)/shard_map/all_to_all | solution.py:137
  487.8 42.6 %copy-start.98 = (s32[16]{0:T(128)S(1)}, s32[16]{0:T(128)}, u32[]{:S(2)}) copy-start(s32[16]{0:T(128)} %copy-done.95) | copy-start | bytes 196
  487.8 42.6 %copy-start.104 = (f32[57]{0:T(128)S(1)}, f32[57]{0:T(128)}, u32[]{:S(2)}) copy-start(f32[57]{0:T(128)} %copy-done.100) | copy-start | bytes 688
  525.6 4.8 copy-start.5
  525.6 4.8 copy-start.38
  (81 other events, 261.3 us)
where the time goes:
time: 601 us; the launch traced here: 593 us
  matrix products  288 us (48%)
  waiting for transfers between devices  161 us (27%)
  local copies, waits for them, and re-layouts  69.7 us (12%)
  starting transfers between devices  42.7 us (7%)
  other arithmetic  28.7 us (5%)
    all_to_all x4, waiting for transfers between devices, derive(): lax.all_to_all(row_out, 'gy', split_axis=0, concat_axis=0, tiled=True)  140 us
    dot_general x40, matrix products, select_rows(): return jnp.einsum('rp,pcij->rcij', table, pool, precision=highest)  122 us
    dot_general x24, matrix products, left_apply(): return jnp.einsum('ij,...jk->...ik', matrix, operand, precision=highest)  96.3 us
    dot_general x24, matrix products, right_apply(): return jnp.einsum('...ij,jk->...ik', operand, matrix, precision=highest)  70.1 us
    all_to_all x4, starting transfers between devices, derive(): lax.all_to_all(row_out, 'gy', split_axis=0, concat_axis=0, tiled=True)  25.9 us
    dot_general x8, local copies, waits for them, and re-layouts, select_rows(): return jnp.einsum('rp,pcij->rcij', table, pool, precision=highest)  22.5 us
    all_to_all x4, waiting for transfers between devices, derive(): lax.all_to_all(column_out, 'gx', split_axis=0, concat_axis=0, tiled=True)  21.2 us
    all_to_all x4, local copies, waits for them, and re-layouts, derive(): lax.all_to_all(row_out, 'gy', split_axis=0, concat_axis=0, tiled=True)  18.9 us
  transfers between devices with their start and end apart: 8, of which 8 were waited for; matrix products, arithmetic and copies ran while one was open for 18% of the time, Pallas kernels for 0%

commit v1 on v0

v1 whole, which is shorter than its diff:
```python
import functools

import jax
import jax.numpy as jnp
from jax import lax
from jax.experimental import pallas as pl
from jax.experimental.pallas import tpu as pltpu
from jax.sharding import PartitionSpec as P

XCAP = 2
step_size = 0.1
f32, bf16 = jnp.float32, jnp.bfloat16
HBM = pl.BlockSpec(memory_space=pltpu.HBM)
SMEM = pl.BlockSpec(memory_space=pltpu.SMEM)
VMEM = pl.BlockSpec(memory_space=pltpu.VMEM)


def split(value):
    high = value.astype(bf16)
    return high, (value - high.astype(f32)).astype(bf16)


def prepare_kernel(h_ref, v_ref, left_ref, right_ref, row_left_ref, row_right_ref):
    n = h_ref.shape[-1]

    def put(matrix, left, right, place):
        high, low = split(matrix)
        start = place * 2 * n
        for half in range(2):
            cols = slice(start + half * n, start + (half + 1) * n)
            left[0:n, cols] = high
            left[n : 2 * n, cols] = low
            right[cols, 0:n] = high
            right[cols, n : 2 * n] = low

    terms = [h_ref[1], h_ref[0], v_ref[0], v_ref[1], v_ref[3]]
    for place, matrix in enumerate(terms):
        put(matrix, left_ref, right_ref, place)
    put(v_ref[2], row_left_ref, row_right_ref, 0)


def sandwich(terms, left, right):
    n = terms[0][0][0].shape[-1]
    columns, rows = [], []
    for (la, lb), (ra, rb) in terms:
        columns += [jnp.concatenate(pair, axis=1) for pair in zip(split(la), split(lb))]
        rows += [jnp.concatenate(pair, axis=0) for pair in zip(split(ra), split(rb))]
    stacked = jnp.concatenate(columns, axis=0)
    beside = jnp.concatenate(rows, axis=1)
    ahead = jnp.dot(left, stacked, preferred_element_type=f32)
    behind = jnp.dot(beside, right, preferred_element_type=f32)
    ahead = ahead[0:n] + ahead[n:]
    behind = behind[:, 0:n] + behind[:, n:]
    return ahead[:, 0:n] - behind[0:n], ahead[:, n:] - behind[n:]


def bath_term(ur, ui, lr, li, wr, wi):
    arr, ari, air, aii = wr * lr, wi * lr, wr * li, wi * li
    real, imag = ur + arr, ui + air
    return ((imag + ari, aii - real), (imag - ari, -real - aii))


def local_kernel(tab, wts, z_ref, c1, c2, c3, left, right, *rest, with_sum, last_scale):
    if with_sum:
        acc_ref, *rest = rest
    if last_scale is None and with_sum:
        out_ref, sum_ref, cbuf, sems = rest
    else:
        out_ref, cbuf, sems = rest
    g = pl.program_id(0)

    @pl.when(g == 0)
    def _():
        copies = [
            pltpu.make_async_copy(c, cbuf.at[pl.ds(2 * k, 2)], sems.at[k])
            for k, c in enumerate((c1, c2, c3))
        ]
        for copy in copies:
            copy.start()
        for copy in copies:
            copy.wait()

    yr, yi = z_ref[g, 0], z_ref[g, 1]
    terms = [((yr, yi), (yr, yi)), ((yi, -yr), (yi, -yr))]
    for k, (ref, bath) in enumerate(((z_ref, 0), (z_ref, 1), (cbuf, 3))):
        up, low = tab[g * 8 + 2 + 2 * k], tab[g * 8 + 3 + 2 * k]
        u, l = jnp.maximum(up, 0), jnp.maximum(low, 0)
        ur, ui = (jnp.where(up >= 0, ref[u, part], 0.0) for part in range(2))
        lr, li = (jnp.where(low >= 0, ref[l, part], 0.0) for part in range(2))
        terms.append(bath_term(ur, ui, lr, li, wts[g * 9 + 2 * bath], wts[g * 9 + 2 * bath + 1]))
    out_r, out_i = sandwich(terms, left[...], right[...])
    damp = wts[g * 9 + 8]
    out_r, out_i = out_r - damp * yr, out_i - damp * yi
    if with_sum:
        sum_r, sum_i = acc_ref[0, 0] + yr, acc_ref[0, 1] + yi
    if last_scale is not None:
        out_r, out_i = sum_r + last_scale * out_r, sum_i + last_scale * out_i
    out_ref[0, 0], out_ref[0, 1] = out_r, out_i
    if last_scale is None and with_sum:
        sum_ref[0, 0], sum_ref[0, 1] = sum_r, sum_i


def local_part(tab, wts, z, cols, left, right, acc, last_scale):
    count, _, n, _ = z.shape
    block = pl.BlockSpec((1, 2, n, n), lambda g: (g, 0, 0, 0))
    whole = lambda a: pl.BlockSpec(a.shape, lambda g: (0,) * a.ndim)
    with_sum = acc is not None
    outs = 2 if with_sum and last_scale is None else 1
    shape = pltpu.HBM(z.shape, f32)
    return pl.pallas_call(
        functools.partial(local_kernel, with_sum=with_sum, last_scale=last_scale),
        grid=(count,),
        out_shape=[shape] * outs,
        in_specs=[SMEM, SMEM, whole(z), HBM, HBM, HBM, whole(left), whole(right)]
        + [block] * with_sum,
        out_specs=[block] * outs,
        scratch_shapes=[
            pltpu.VMEM((6, 2, n, n), f32),
            pltpu.SemaphoreType.DMA((3,)),
        ],
        compiler_params=pltpu.CompilerParams(vmem_limit_bytes=16 << 20),
        cost_estimate=pl.CostEstimate(
            flops=count * 20 * 2 * (2 * n) * (2 * n) * n * 4, bytes_accessed=8 << 20, transcendentals=0
        ),
        name="local_part",
    )(tab, wts, z, *cols, left, right, *([acc] if with_sum else []))


def send_rows(tab, g, source, row_out, sem_u, sem_l, go):
    for k, sem in ((0, sem_u), (1, sem_l)):
        slot = tab[g * 8 + k]

        @pl.when(slot >= 0)
        def _():
            copy = pltpu.make_async_copy(source.at[g], row_out.at[jnp.maximum(slot, 0)], sem.at[g])
            copy.start() if go else copy.wait()


def send_columns(ctab, source, outs, sem, go):
    for k in range(6):
        g = ctab[k]

        @pl.when(g >= 0)
        def _():
            copy = pltpu.make_async_copy(
                source.at[jnp.maximum(g, 0)], outs[k // 2].at[k % 2], sem.at[k]
            )
            copy.start() if go else copy.wait()


def pack_rows_kernel(tab, z_ref, row_out, buf, sem_in, sem_u, sem_l):
    count = z_ref.shape[0]
    load = lambda g: pltpu.make_async_copy(z_ref.at[g], buf.at[g], sem_in.at[g])

    @pl.loop(0, count)
    def _(g):
        load(g).start()

    @pl.loop(0, count)
    def _(g):
        load(g).wait()
        send_rows(tab, g, buf, row_out, sem_u, sem_l, True)

    @pl.loop(0, count)
    def _(g):
        send_rows(tab, g, buf, row_out, sem_u, sem_l, False)


def pack_columns_kernel(ctab, z_ref, o1, o2, o3, sem):
    send_columns(ctab, z_ref, (o1, o2, o3), sem, True)
    send_columns(ctab, z_ref, (o1, o2, o3), sem, False)


def row_kernel(tab, ctab, wts, recv, part, left, right, *rest, scale, last):
    count, _, n, _ = part.shape
    if last:
        z_out, ubuf, lbuf, gbuf, zbuf, sem_u, sem_l, sem_g, sem_z = rest
    else:
        (z_out, row_out, o1, o2, o3, ubuf, lbuf, gbuf, zbuf) = rest[:9]
        (sem_u, sem_l, sem_g, sem_z, sem_ru, sem_rl, sem_c) = rest[9:]

    def fetch(g, go):
        for k, buf, sem in ((0, ubuf, sem_u), (1, lbuf, sem_l)):
            slot = tab[g * 8 + k]

            @pl.when(slot >= 0)
            def _():
                copy = pltpu.make_async_copy(recv.at[jnp.maximum(slot, 0)], buf.at[g], sem.at[g])
                copy.start() if go else copy.wait()

        copy = pltpu.make_async_copy(part.at[g], gbuf.at[g], sem_g.at[g])
        copy.start() if go else copy.wait()

    def keep(g):
        return pltpu.make_async_copy(zbuf.at[g], z_out.at[g], sem_z.at[g])

    @pl.loop(0, count)
    def _(g):
        fetch(g, True)

    def one(g):
        up, low = tab[g * 8], tab[g * 8 + 1]
        ur, ui = (jnp.where(up >= 0, ubuf[g, p], 0.0) for p in range(2))
        lr, li = (jnp.where(low >= 0, lbuf[g, p], 0.0) for p in range(2))
        term = bath_term(ur, ui, lr, li, wts[g * 9 + 4], wts[g * 9 + 5])
        out_r, out_i = sandwich([term], left[...], right[...])
        if last:
            zbuf[g, 0] = gbuf[g, 0] + scale * out_r
            zbuf[g, 1] = gbuf[g, 1] + scale * out_i
        else:
            zbuf[g, 0] = scale * (gbuf[g, 0] + out_r)
            zbuf[g, 1] = scale * (gbuf[g, 1] + out_i)

    width = 4

    @pl.loop(0, count // width)
    def _(step):
        for k in range(width):
            fetch(step * width + k, False)
        for k in range(width):
            one(step * width + k)
        for k in range(width):
            g = step * width + k
            keep(g).start()
            if not last:
                send_rows(tab, g, zbuf, row_out, sem_ru, sem_rl, True)

    if not last:
        send_columns(ctab, zbuf, (o1, o2, o3), sem_c, True)

    @pl.loop(0, count)
    def _(g):
        keep(g).wait()
        if not last:
            send_rows(tab, g, zbuf, row_out, sem_ru, sem_rl, False)

    if not last:
        send_columns(ctab, zbuf, (o1, o2, o3), sem_c, False)


def row_part(tab, ctab, wts, recv, part, left, right, scale, last):
    count, _, n, _ = part.shape
    shape = lambda rows: pltpu.HBM((rows, 2, n, n), f32)
    outs = [jax.ShapeDtypeStruct(part.shape, f32) if last else shape(count)]
    if not last:
        outs += [shape(recv.shape[0])] + [shape(XCAP)] * 3
    sems = [pltpu.SemaphoreType.DMA((count,))] * (4 if last else 6)
    if not last:
        sems = sems + [pltpu.SemaphoreType.DMA((6,))]
    return pl.pallas_call(
        functools.partial(row_kernel, scale=scale, last=last),
        out_shape=outs,
        in_specs=[SMEM, SMEM, SMEM, HBM, HBM, VMEM, VMEM],
        out_specs=[HBM] * len(outs),
        scratch_shapes=[pltpu.VMEM((count, 2, n, n), f32)] * 4 + sems,
        compiler_params=pltpu.CompilerParams(vmem_limit_bytes=16 << 20),
        cost_estimate=pl.CostEstimate(
            flops=count * 16 * 2 * n * n * n, bytes_accessed=10 << 20, transcendentals=0
        ),
        name="row_part",
    )(tab, ctab, wts, *(pltpu.with_memory_space_constraint(a, pltpu.HBM) for a in (recv, part)), left, right)


def local(
    densities, hamiltonian, couplings, decay_rates, correlation, upper_link, lower_link, occupation
):
    count, _, n, _ = densities.shape
    along_y, along_x = lax.axis_size("gy"), lax.axis_size("gx")
    index_x, index_y = lax.axis_index("gx"), lax.axis_index("gy")
    own = index_x * along_y + index_y
    missing = count * along_y * along_x

    links = jnp.stack([upper_link, lower_link], axis=2)
    live = links < missing
    near = jnp.where(live[:, 0:2], links[:, 0:2] - own * count, -1).reshape(count, 4)
    rows = jnp.where(live[:, 2], (links[:, 2] // count) % along_y, -1)

    targets, usable = links[:, 3].reshape(-1), live[:, 3].reshape(-1)
    sources = jnp.repeat(jnp.arange(count, dtype=jnp.int32), 2)
    relative = (targets // count // along_y - index_x) % along_x
    same = usable[:, None] & usable[None, :] & (relative[:, None] == relative[None, :])
    start = (relative - 1) * XCAP
    recv_slot = start + jnp.any(same & (targets[None, :] < targets[:, None]), axis=1)
    send_slot = start + jnp.any(same & (sources[None, :] < sources[:, None]), axis=1)
    recv_slot = jnp.where(usable, recv_slot, -1).reshape(count, 2)
    hit = (send_slot[None, :] == jnp.arange(6, dtype=jnp.int32)[:, None]) & usable[None, :]
    ctab = jnp.max(jnp.where(hit, sources[None, :], -1), axis=1)
    tab = jnp.concatenate([rows, near, recv_slot], axis=1).reshape(-1).astype(jnp.int32)

    level = occupation.astype(f32)
    damping = jnp.sum(level * decay_rates[None, :], axis=1, keepdims=True)
    pairs = (level[:, :, None] * correlation.T[None, :, :]).reshape(count, 8)
    wts = jnp.concatenate([pairs, damping], axis=1).reshape(-1)

    mats = lambda rows, cols: jax.ShapeDtypeStruct((rows, cols), bf16)
    left, right, row_left, row_right = pl.pallas_call(
        prepare_kernel,
        out_shape=[mats(2 * n, 10 * n), mats(10 * n, 2 * n), mats(2 * n, 2 * n), mats(2 * n, 2 * n)],
        in_specs=[VMEM, VMEM],
        out_specs=[VMEM] * 4,
        name="prepare",
    )(hamiltonian, couplings)

    row_send = pl.pallas_call(
        pack_rows_kernel,
        out_shape=pltpu.HBM((along_y, 2, n, n), f32),
        in_specs=[SMEM, HBM],
        out_specs=HBM,
        scratch_shapes=[pltpu.VMEM((count, 2, n, n), f32)]
        + [pltpu.SemaphoreType.DMA((count,))] * 3,
        name="pack_rows",
    )(tab, densities)
    col_send = pl.pallas_call(
        pack_columns_kernel,
        out_shape=[pltpu.HBM((XCAP, 2, n, n), f32)] * 3,
        in_specs=[SMEM, VMEM],
        out_specs=[HBM] * 3,
        scratch_shapes=[pltpu.SemaphoreType.DMA((6,))],
        name="pack_columns",
    )(ctab, densities)

    z, acc = densities, None
    for stage in range(1, 5):
        recv = lax.all_to_all(row_send, "gy", split_axis=0, concat_axis=0, tiled=True)
        arrived = [
            lax.ppermute(col_send[s - 1], "gx", [(x, (x + s) % along_x) for x in range(along_x)])
            for s in range(1, along_x)
        ]
        cols = arrived[::-1]
        scale, last = step_size / stage, stage == 4
        part = local_part(
            tab, wts, z, cols, left, right, acc, scale if last else None
        )
        if stage == 1:
            acc = densities
        elif not last:
            acc = part[1]
        outs = row_part(tab, ctab, wts, recv, part[0], row_left, row_right, scale, last)
        if last:
            return outs[0]
        z, row_send, *col_send = outs


def solution(mesh):
    return jax.shard_map(
        local,
        mesh=mesh,
        in_specs=(
            P(("gx", "gy"), None, None, None),
            P(),
            P(),
            P(),
            P(),
            P(("gx", "gy"), None),
            P(("gx", "gy"), None),
            P(("gx", "gy"), None),
        ),
        out_specs=P(("gx", "gy"), None, None, None),
        check_vma=False,
    )
```

time: 601 us -> 270 us (0.45); the launches traced: 593 us -> 269 us
  matrix products: 288 us -> 0 us
  Pallas kernels: 0 us -> 75.1 us
  local copies, waits for them, and re-layouts: 69.7 us -> 11.9 us
  waiting for transfers between devices: 161 us -> 135 us
  other arithmetic: 28.7 us -> 3.32 us
    dot_general x88 -> x0, matrix products: 288 us -> none  [the longest x40 122 us: select_rows(): return jnp.einsum('rp,pcij->rcij', table, pool, precision=highest)]
    all_to_all x8 -> x4, waiting for transfers between devices: 161 us -> 82.5 us  [local(): lax.all_to_all(row_send, 'gy', split_axis=0, concat_axis=0, tiled=True)]
    pallas_call x0 -> x11, Pallas kernels: none -> 75.1 us  [the longest x4 43.4 us: local_part(): pl.pallas_call(functools.partial(local_kernel, with_sum=with_sum, last_sc...]
    ppermute x0 -> x12, waiting for transfers between devices: none -> 52.4 us  [local(): lax.ppermute(col_send[s - 1], 'gx', [(x, (x + s) % along_x) for x in rang...]
    all_to_all x8 -> x0, local copies, waits for them, and re-layouts: 26.6 us -> none  [the longest x4 18.9 us: derive(): lax.all_to_all(row_out, 'gy', split_axis=0, concat_axis=0, tiled=True)]
    dot_general x8 -> x0, local copies, waits for them, and re-layouts: 22.5 us -> none  [select_rows(): return jnp.einsum('rp,pcij->rcij', table, pool, precision=highest)]
    ppermute x0 -> x12, starting transfers between devices: none -> 21.2 us  [local(): lax.ppermute(col_send[s - 1], 'gx', [(x, (x + s) % along_x) for x in rang...]
    all_to_all x8 -> x4, starting transfers between devices: 42.7 us -> 22.7 us  [local(): lax.all_to_all(row_send, 'gy', split_axis=0, concat_axis=0, tiled=True)]
  transfers between devices with their start and end apart: 8 -> 16, of which waited for: 8 -> 12; matrix products, arithmetic and copies ran while one was open for 18% -> 0% of each run, Pallas kernels for 0% -> 18%
where the time goes in v1:
time: 270 us; the launch traced here: 269 us
  waiting for transfers between devices  135 us (50%)
  Pallas kernels  75.1 us (28%)
  starting transfers between devices  43.9 us (16%)
  local copies, waits for them, and re-layouts  11.9 us (4%)
  other arithmetic  3.32 us (1%)
    all_to_all x4, waiting for transfers between devices, local(): lax.all_to_all(row_send, 'gy', split_axis=0, concat_axis=0, tiled=True)  82.5 us
    ppermute x12, waiting for transfers between devices, local(): lax.ppermute(col_send[s - 1], 'gx', [(x, (x + s) % along_x) for x in rang...  52.4 us
    pallas_call x4, Pallas kernels, local_part(): pl.pallas_call(functools.partial(local_kernel, with_sum=with_sum, last_sc...  43.4 us
    pallas_call x4, Pallas kernels, row_part(): pl.pallas_call(functools.partial(row_kernel, scale=scale, last=last), out...  23.5 us
    all_to_all x4, starting transfers between devices, local(): lax.all_to_all(row_send, 'gy', split_axis=0, concat_axis=0, tiled=True)  22.7 us
    ppermute x12, starting transfers between devices, local(): lax.ppermute(col_send[s - 1], 'gx', [(x, (x + s) % along_x) for x in rang...  21.2 us
    unnamed x50, local copies, waits for them, and re-layouts  10.3 us
  transfers between devices with their start and end apart: 16, of which 12 were waited for; matrix products, arithmetic and copies ran while one was open for 0% of the time, Pallas kernels for 18%

profile of v1, /device:TPU:0, one launch (start us, length us, event | category | flops | bytes accessed | tf_op | source)
XLA Modules:
  0.0 269.4 jit_solution(18069229596810614780)
XLA Ops:
  3.8 3.4 %pack_rows.1 = f32[32,2,128,128]{3,2,1,0:T(8,128)} custom-call(s32[128]{0:T(128)} %reshape.154.tab, f32[16,2,128,128]{3,2,1,0:T(8,128)} %rest_0_.1), custom_call_target="tpu_custom_call" | custom-call | tf_op jit(solution)/shard_map/pack_rows/pallas_call | solution.py:304
  7.3 7.6 %all-to-all-start = ((f32[32,2,128,128]{3,2,1,0:T(8,128)}), f32[32,2,128,128]{3,2,1,0:T(8,128)}, u32[]{:S(2)}, u32[]{:S(2)}) async-start(f32[32,2,128,128]{3,2,1,0:T(8,128)} %pack_rows.1), calls=%async_computation | async-start | bytes 8388608 | tf_op jit(solution)/shard_map/all_to_all | solution.py:324
  15.6 2.4 pack_columns.1
  18.1 4.1 %collective-permute-start = (f32[2,2,128,128]{3,2,1,0:T(8,128)}, f32[2,2,128,128]{3,2,1,0:T(8,128)S(1)}, u32[]{:S(2)}, u32[]{:S(2)}) collective-permute-start(f32[2,2,128,128]{3,2,1,0:T(8,128)} %get-tuple-element.31), channel_id=1, source_target_pairs={{0,96},{32,0},{64,32},{96,64},{1,97},{33,1},{65,33},{97,65},{2,98}... | collective-permute-start | bytes 786440 | tf_op jit(solution)/shard_map/ppermute | solution.py:326
  23.9 2.3 prepare.1
  26.3 7.8 %collective-permute-done.c1 = f32[2,2,128,128]{3,2,1,0:T(8,128)S(1)} collective-permute-done((f32[2,2,128,128]{3,2,1,0:T(8,128)}, f32[2,2,128,128]{3,2,1,0:T(8,128)S(1)}, u32[]{:S(2)}, u32[]{:S(2)}) %collective-permute-start) | collective-permute-done | bytes 262176 | tf_op jit(solution)/shard_map/ppermute | solution.py:326
  34.1 3.3 %collective-permute-done.2.c3 = f32[2,2,128,128]{3,2,1,0:T(8,128)S(1)} collective-permute-done((f32[2,2,128,128]{3,2,1,0:T(8,128)}, f32[2,2,128,128]{3,2,1,0:T(8,128)S(1)}, u32[]{:S(2)}, u32[]{:S(2)}) %collective-permute-start.2) | collective-permute-done | bytes 262176 | tf_op jit(solution)/shard_map/ppermute | solution.py:326
  39.5 10.7 %local_part.4.part = f32[16,2,128,128]{3,2,1,0:T(8,128)} custom-call(s32[128]{0:T(128)S(1)} %copy-done.3, f32[144]{0:T(256)S(1)} %reshape.155.wts, f32[16,2,128,128]{3,2,1,0:T(8,128)S(1)} %copy-done, f32[2,2,128,128]{3,2,1,0:T(8,128)S(1)} %collective-permute-done.c1, f32[2,2,128,128]{3,2,1,0:T(8,128)S(1)} %collective-permute-done.1.c2, ...), custom_call_target="tpu_custom_call" | custom-call | flops 21474836480 | bytes 8388608 | tf_op jit(solution)/shard_map/local_part/pallas_call | solution.py:110
  50.3 18.6 %all-to-all-done.recv = f32[32,2,128,128]{3,2,1,0:T(8,128)} async-done(((f32[32,2,128,128]{3,2,1,0:T(8,128)}), f32[32,2,128,128]{3,2,1,0:T(8,128)}, u32[]{:S(2)}, u32[]{:S(2)}) %all-to-all-start) | async-done | bytes 4194336 | tf_op jit(solution)/shard_map/all_to_all | solution.py:324
  68.9 6.1 %row_part.4 = (f32[16,2,128,128]{3,2,1,0:T(8,128)}, f32[32,2,128,128]{3,2,1,0:T(8,128)}, f32[2,2,128,128]{3,2,1,0:T(8,128)}, f32[2,2,128,128]{3,2,1,0:T(8,128)}, f32[2,2,128,128]{3,2,1,0:T(8,128)}) custom-call(s32[128]{0:T(128)S(1)} %copy-done.3, s32[6]{0:T(128)S(1)} %copy-done.4, f32[144]{0:T(256)S(1)} %reshape.155.wts, ...), custom_call_target="tpu_custom_call" | custom-call | flops 1073741824 | bytes 10485760 | tf_op jit(solution)/shard_map/row_part/pallas_call | solution.py:250
  75.0 5.0 %all-to-all-start.1 = ((f32[32,2,128,128]{3,2,1,0:T(8,128)}), f32[32,2,128,128]{3,2,1,0:T(8,128)}, u32[]{:S(2)}, u32[]{:S(2)}) async-start(f32[32,2,128,128]{3,2,1,0:T(8,128)} %get-tuple-element.38), calls=%async_computation.1 | async-start | bytes 8388608 | tf_op jit(solution)/shard_map/all_to_all | solution.py:324
  80.0 4.1 %collective-permute-start.3 = (f32[2,2,128,128]{3,2,1,0:T(8,128)}, f32[2,2,128,128]{3,2,1,0:T(8,128)S(1)}, u32[]{:S(2)}, u32[]{:S(2)}) collective-permute-start(f32[2,2,128,128]{3,2,1,0:T(8,128)} %get-tuple-element.40), channel_id=1, source_target_pairs={{0,96},{32,0},{64,32},{96,64},{1,97},{33,1},{65,33},{97,65},{2,98}... | collective-permute-start | bytes 786440 | tf_op jit(solution)/shard_map/ppermute | solution.py:326
  85.3 10.6 %collective-permute-done.3.c1 = f32[2,2,128,128]{3,2,1,0:T(8,128)S(1)} collective-permute-done((f32[2,2,128,128]{3,2,1,0:T(8,128)}, f32[2,2,128,128]{3,2,1,0:T(8,128)S(1)}, u32[]{:S(2)}, u32[]{:S(2)}) %collective-permute-start.3) | collective-permute-done | bytes 262176 | tf_op jit(solution)/shard_map/ppermute | solution.py:326
  95.9 3.2 %collective-permute-done.5.c3 = f32[2,2,128,128]{3,2,1,0:T(8,128)S(1)} collective-permute-done((f32[2,2,128,128]{3,2,1,0:T(8,128)S(1)}, f32[2,2,128,128]{3,2,1,0:T(8,128)S(1)}, u32[]{:S(2)}, u32[]{:S(2)}) %collective-permute-start.5) | collective-permute-done | bytes 262176 | tf_op jit(solution)/shard_map/ppermute | solution.py:326
  99.1 1.6 copy-done.7
  101.7 10.9 %local_part.5 = (f32[16,2,128,128]{3,2,1,0:T(8,128)}, f32[16,2,128,128]{3,2,1,0:T(8,128)}) custom-call(s32[128]{0:T(128)S(1)} %copy-done.3, f32[144]{0:T(256)S(1)} %reshape.155.wts, f32[16,2,128,128]{3,2,1,0:T(8,128)S(1)} %copy-done.7, f32[2,2,128,128]{3,2,1,0:T(8,128)S(1)} %collective-permute-done.3.c1, f32[2,2,128,128]{3,2,1,0:T(8,128)S(1)} %collective-permute-done.4.c2, ...), custom_call_target="tpu_custom_call" | custom-call | flops 21474836480 | bytes 8388608 | tf_op jit(solution)/shard_map/local_part/pallas_call | solution.py:110
  112.6 21.3 %all-to-all-done.1.recv = f32[32,2,128,128]{3,2,1,0:T(8,128)} async-done(((f32[32,2,128,128]{3,2,1,0:T(8,128)}), f32[32,2,128,128]{3,2,1,0:T(8,128)}, u32[]{:S(2)}, u32[]{:S(2)}) %all-to-all-start.1) | async-done | bytes 4194336 | tf_op jit(solution)/shard_map/all_to_all | solution.py:324
  134.0 6.1 %row_part.5 = (f32[16,2,128,128]{3,2,1,0:T(8,128)}, f32[32,2,128,128]{3,2,1,0:T(8,128)}, f32[2,2,128,128]{3,2,1,0:T(8,128)}, f32[2,2,128,128]{3,2,1,0:T(8,128)}, f32[2,2,128,128]{3,2,1,0:T(8,128)}) custom-call(s32[128]{0:T(128)S(1)} %copy-done.3, s32[6]{0:T(128)S(1)} %copy-done.4, f32[144]{0:T(256)S(1)} %reshape.155.wts, ...), custom_call_target="tpu_custom_call" | custom-call | flops 1073741824 | bytes 10485760 | tf_op jit(solution)/shard_map/row_part/pallas_call | solution.py:250
  140.1 5.0 %all-to-all-start.2 = ((f32[32,2,128,128]{3,2,1,0:T(8,128)}), f32[32,2,128,128]{3,2,1,0:T(8,128)}, u32[]{:S(2)}, u32[]{:S(2)}) async-start(f32[32,2,128,128]{3,2,1,0:T(8,128)} %get-tuple-element.44), calls=%async_computation.2 | async-start | bytes 8388608 | tf_op jit(solution)/shard_map/all_to_all | solution.py:324
  145.1 4.2 %collective-permute-start.6 = (f32[2,2,128,128]{3,2,1,0:T(8,128)}, f32[2,2,128,128]{3,2,1,0:T(8,128)S(1)}, u32[]{:S(2)}, u32[]{:S(2)}) collective-permute-start(f32[2,2,128,128]{3,2,1,0:T(8,128)} %get-tuple-element.46), channel_id=1, source_target_pairs={{0,96},{32,0},{64,32},{96,64},{1,97},{33,1},{65,33},{97,65},{2,98}... | collective-permute-start | bytes 786440 | tf_op jit(solution)/shard_map/ppermute | solution.py:326
  150.4 10.6 %collective-permute-done.6.c1 = f32[2,2,128,128]{3,2,1,0:T(8,128)S(1)} collective-permute-done((f32[2,2,128,128]{3,2,1,0:T(8,128)}, f32[2,2,128,128]{3,2,1,0:T(8,128)S(1)}, u32[]{:S(2)}, u32[]{:S(2)}) %collective-permute-start.6) | collective-permute-done | bytes 262176 | tf_op jit(solution)/shard_map/ppermute | solution.py:326
  161.0 3.2 %collective-permute-done.8.c3 = f32[2,2,128,128]{3,2,1,0:T(8,128)S(1)} collective-permute-done((f32[2,2,128,128]{3,2,1,0:T(8,128)S(1)}, f32[2,2,128,128]{3,2,1,0:T(8,128)S(1)}, u32[]{:S(2)}, u32[]{:S(2)}) %collective-permute-start.8) | collective-permute-done | bytes 262176 | tf_op jit(solution)/shard_map/ppermute | solution.py:326
  166.8 10.9 %local_part.6 = (f32[16,2,128,128]{3,2,1,0:T(8,128)}, f32[16,2,128,128]{3,2,1,0:T(8,128)}) custom-call(s32[128]{0:T(128)S(1)} %copy-done.3, f32[144]{0:T(256)S(1)} %reshape.155.wts, f32[16,2,128,128]{3,2,1,0:T(8,128)S(1)} %copy-done.5, f32[2,2,128,128]{3,2,1,0:T(8,128)S(1)} %collective-permute-done.6.c1, f32[2,2,128,128]{3,2,1,0:T(8,128)S(1)} %collective-permute-done.7.c2, ...), custom_call_target="tpu_custom_call" | custom-call | flops 21474836480 | bytes 8388608 | tf_op jit(solution)/shard_map/local_part/pallas_call | solution.py:110
  177.8 21.3 %all-to-all-done.2.recv = f32[32,2,128,128]{3,2,1,0:T(8,128)} async-done(((f32[32,2,128,128]{3,2,1,0:T(8,128)}), f32[32,2,128,128]{3,2,1,0:T(8,128)}, u32[]{:S(2)}, u32[]{:S(2)}) %all-to-all-start.2) | async-done | bytes 4194336 | tf_op jit(solution)/shard_map/all_to_all | solution.py:324
  199.0 6.1 %row_part.6 = (f32[16,2,128,128]{3,2,1,0:T(8,128)}, f32[32,2,128,128]{3,2,1,0:T(8,128)}, f32[2,2,128,128]{3,2,1,0:T(8,128)}, f32[2,2,128,128]{3,2,1,0:T(8,128)}, f32[2,2,128,128]{3,2,1,0:T(8,128)}) custom-call(s32[128]{0:T(128)S(1)} %copy-done.3, s32[6]{0:T(128)S(1)} %copy-done.4, f32[144]{0:T(256)S(1)} %reshape.155.wts, ...), custom_call_target="tpu_custom_call" | custom-call | flops 1073741824 | bytes 10485760 | tf_op jit(solution)/shard_map/row_part/pallas_call | solution.py:250
  205.1 5.0 %all-to-all-start.3 = ((f32[32,2,128,128]{3,2,1,0:T(8,128)}), f32[32,2,128,128]{3,2,1,0:T(8,128)}, u32[]{:S(2)}, u32[]{:S(2)}) async-start(f32[32,2,128,128]{3,2,1,0:T(8,128)} %get-tuple-element.51), calls=%async_computation.3 | async-start | bytes 8388608 | tf_op jit(solution)/shard_map/all_to_all | solution.py:324
  210.1 4.2 %collective-permute-start.9 = (f32[2,2,128,128]{3,2,1,0:T(8,128)}, f32[2,2,128,128]{3,2,1,0:T(8,128)S(1)}, u32[]{:S(2)}, u32[]{:S(2)}) collective-permute-start(f32[2,2,128,128]{3,2,1,0:T(8,128)} %get-tuple-element.53), channel_id=1, source_target_pairs={{0,96},{32,0},{64,32},{96,64},{1,97},{33,1},{65,33},{97,65},{2,98}... | collective-permute-start | bytes 786440 | tf_op jit(solution)/shard_map/ppermute | solution.py:326
  215.5 10.6 %collective-permute-done.9.c1 = f32[2,2,128,128]{3,2,1,0:T(8,128)S(1)} collective-permute-done((f32[2,2,128,128]{3,2,1,0:T(8,128)}, f32[2,2,128,128]{3,2,1,0:T(8,128)S(1)}, u32[]{:S(2)}, u32[]{:S(2)}) %collective-permute-start.9) | collective-permute-done | bytes 262176 | tf_op jit(solution)/shard_map/ppermute | solution.py:326
  226.1 3.2 %collective-permute-done.11.c3 = f32[2,2,128,128]{3,2,1,0:T(8,128)S(1)} collective-permute-done((f32[2,2,128,128]{3,2,1,0:T(8,128)S(1)}, f32[2,2,128,128]{3,2,1,0:T(8,128)S(1)}, u32[]{:S(2)}, u32[]{:S(2)}) %collective-permute-start.11) | collective-permute-done | bytes 262176 | tf_op jit(solution)/shard_map/ppermute | solution.py:326
  231.9 10.8 %local_part.7.part = f32[16,2,128,128]{3,2,1,0:T(8,128)} custom-call(s32[128]{0:T(128)S(1)} %copy-done.3, f32[144]{0:T(256)S(1)} %reshape.155.wts, f32[16,2,128,128]{3,2,1,0:T(8,128)S(1)} %copy-done.6, f32[2,2,128,128]{3,2,1,0:T(8,128)S(1)} %collective-permute-done.9.c1, f32[2,2,128,128]{3,2,1,0:T(8,128)S(1)} %collective-permute-done.10.c2, ...), custom_call_target="tpu_custom_call" | custom-call | flops 21474836480 | bytes 8388608 | tf_op jit(solution)/shard_map/local_part/pallas_call | solution.py:110
  242.8 21.3 %all-to-all-done.3.recv = f32[32,2,128,128]{3,2,1,0:T(8,128)} async-done(((f32[32,2,128,128]{3,2,1,0:T(8,128)}), f32[32,2,128,128]{3,2,1,0:T(8,128)}, u32[]{:S(2)}, u32[]{:S(2)}) %all-to-all-start.3) | async-done | bytes 4194336 | tf_op jit(solution)/shard_map/all_to_all | solution.py:324
  264.1 5.3 %row_part.7 = f32[16,2,128,128]{3,2,1,0:T(8,128)} custom-call(s32[128]{0:T(128)S(1)} %copy-done.3, s32[6]{0:T(128)S(1)} %copy-done.4, f32[144]{0:T(256)S(1)} %reshape.155.wts, f32[32,2,128,128]{3,2,1,0:T(8,128)} %all-to-all-done.3.recv, f32[16,2,128,128]{3,2,1,0:T(8,128)} %local_part.7.part, bf16[256,256]{1,0:T(8,128)(2,1)S(1)} %copy-done.1, ...), custom_call_target="tpu_custom_call" | custom-call | flops 1073741824 | bytes 10485760 | tf_op jit(solution)/shard_map/row_part/pallas_call | solution.py:250
  (92 shorter events, 18.3 us)
Async XLA Ops:
  7.3 61.6 %all-to-all-start = ((f32[32,2,128,128]{3,2,1,0:T(8,128)}), f32[32,2,128,128]{3,2,1,0:T(8,128)}, u32[]{:S(2)}, u32[]{:S(2)}) async-start(f32[32,2,128,128]{3,2,1,0:T(8,128)} %pack_rows.1), calls=%async_computation | async-start | bytes 8388608 | tf_op jit(solution)/shard_map/all_to_all | solution.py:324
  14.9 8.6 %copy-start.16 = (s32[16,4]{0,1:T(4,128)S(1)}, s32[16,4]{0,1:T(4,128)}, u32[]{:S(2)}) copy-start(s32[16,4]{0,1:T(4,128)} %param.15) | copy-start | bytes 772
  14.9 8.7 %copy-start.18 = (f32[4]{0:T(128)S(1)}, f32[4]{0:T(128)}, u32[]{:S(2)}) copy-start(f32[4]{0:T(128)} %param.11) | copy-start | bytes 52
  14.9 22.4 %copy-start = (f32[16,2,128,128]{3,2,1,0:T(8,128)S(1)}, f32[16,2,128,128]{3,2,1,0:T(8,128)}, u32[]{:S(2)}) copy-start(f32[16,2,128,128]{3,2,1,0:T(8,128)} %rest_0_.1) | copy-start | bytes 6291460
  14.9 22.4 %copy-start.3 = (s32[128]{0:T(128)S(1)}, s32[128]{0:T(128)}, u32[]{:S(2)}) copy-start(s32[128]{0:T(128)} %reshape.154.tab) | copy-start | bytes 1540
  18.1 16.0 %collective-permute-start = (f32[2,2,128,128]{3,2,1,0:T(8,128)}, f32[2,2,128,128]{3,2,1,0:T(8,128)S(1)}, u32[]{:S(2)}, u32[]{:S(2)}) collective-permute-start(f32[2,2,128,128]{3,2,1,0:T(8,128)} %get-tuple-element.31), channel_id=1, source_target_pairs={{0,96},{32,0},{64,32},{96,64},{1,97},{33,1},{65,33},{97,65},{2,98}... | collective-permute-start | bytes 786440 | tf_op jit(solution)/shard_map/ppermute | solution.py:326
  22.2 11.9 %collective-permute-start.1 = (f32[2,2,128,128]{3,2,1,0:T(8,128)}, f32[2,2,128,128]{3,2,1,0:T(8,128)S(1)}, u32[]{:S(2)}, u32[]{:S(2)}) collective-permute-start(f32[2,2,128,128]{3,2,1,0:T(8,128)} %get-tuple-element.32), channel_id=1, source_target_pairs={{0,64},{32,96},{64,0},{96,32},{1,65},{33,97},{65,1},{97,33},{2,66}... | collective-permute-start | bytes 786440 | tf_op jit(solution)/shard_map/ppermute | solution.py:326
  22.2 15.2 %collective-permute-start.2 = (f32[2,2,128,128]{3,2,1,0:T(8,128)}, f32[2,2,128,128]{3,2,1,0:T(8,128)S(1)}, u32[]{:S(2)}, u32[]{:S(2)}) collective-permute-start(f32[2,2,128,128]{3,2,1,0:T(8,128)} %get-tuple-element.33), channel_id=1, source_target_pairs={{0,32},{32,64},{64,96},{96,0},{1,33},{33,65},{65,97},{97,1},{2,34}... | collective-permute-start | bytes 786440 | tf_op jit(solution)/shard_map/ppermute | solution.py:326
  39.5 29.3 %copy-start.1 = (bf16[256,256]{1,0:T(8,128)(2,1)S(1)}, bf16[256,256]{1,0:T(8,128)(2,1)}, u32[]{:S(2)}) copy-start(bf16[256,256]{1,0:T(8,128)(2,1)} %get-tuple-element.36.left) | copy-start | bytes 393220
  39.5 29.3 %copy-start.2 = (bf16[256,256]{1,0:T(8,128)(2,1)S(1)}, bf16[256,256]{1,0:T(8,128)(2,1)}, u32[]{:S(2)}) copy-start(bf16[256,256]{1,0:T(8,128)(2,1)} %get-tuple-element.37.right) | copy-start | bytes 393220
  39.5 29.3 %copy-start.4 = (s32[6]{0:T(128)S(1)}, s32[6]{0:T(128)}, u32[]{:S(2)}) copy-start(s32[6]{0:T(128)} %select_reduce_fusion.ctab) | copy-start | bytes 76
  75.0 9.2 %copy-start.22 = (f32[2,2,128,128]{3,2,1,0:T(8,128)S(1)}, f32[2,2,128,128]{3,2,1,0:T(8,128)}, u32[]{:S(2)}) copy-start(f32[2,2,128,128]{3,2,1,0:T(8,128)} %get-tuple-element.41) | copy-start | bytes 786436
  75.0 9.2 %copy-start.19 = (f32[2,2,128,128]{3,2,1,0:T(8,128)S(1)}, f32[2,2,128,128]{3,2,1,0:T(8,128)}, u32[]{:S(2)}) copy-start(f32[2,2,128,128]{3,2,1,0:T(8,128)} %get-tuple-element.42) | copy-start | bytes 786436
  75.0 24.1 %copy-start.9 = (bf16[256,1280]{1,0:T(8,128)(2,1)S(1)}, bf16[256,1280]{1,0:T(8,128)(2,1)}, u32[]{:S(2)}) copy-start(bf16[256,1280]{1,0:T(8,128)(2,1)} %get-tuple-element.34.left) | copy-start | bytes 1966084
  75.0 59.0 %all-to-all-start.1 = ((f32[32,2,128,128]{3,2,1,0:T(8,128)}), f32[32,2,128,128]{3,2,1,0:T(8,128)}, u32[]{:S(2)}, u32[]{:S(2)}) async-start(f32[32,2,128,128]{3,2,1,0:T(8,128)} %get-tuple-element.38), calls=%async_computation.1 | async-start | bytes 8388608 | tf_op jit(solution)/shard_map/all_to_all | solution.py:324
  80.0 15.9 %collective-permute-start.3 = (f32[2,2,128,128]{3,2,1,0:T(8,128)}, f32[2,2,128,128]{3,2,1,0:T(8,128)S(1)}, u32[]{:S(2)}, u32[]{:S(2)}) collective-permute-start(f32[2,2,128,128]{3,2,1,0:T(8,128)} %get-tuple-element.40), channel_id=1, source_target_pairs={{0,96},{32,0},{64,32},{96,64},{1,97},{33,1},{65,33},{97,65},{2,98}... | collective-permute-start | bytes 786440 | tf_op jit(solution)/shard_map/ppermute | solution.py:326
  84.1 11.8 %collective-permute-start.4 = (f32[2,2,128,128]{3,2,1,0:T(8,128)S(1)}, f32[2,2,128,128]{3,2,1,0:T(8,128)S(1)}, u32[]{:S(2)}, u32[]{:S(2)}) collective-permute-start(f32[2,2,128,128]{3,2,1,0:T(8,128)S(1)} %copy-done.22), channel_id=1, source_target_pairs={{0,64},{32,96},{64,0},{96,32},{1,65},{33,97},{65,1},{97,33},{2,66}... | collective-permute-start | bytes 786440 | tf_op jit(solution)/shard_map/ppermute | solution.py:326
  84.1 14.9 %collective-permute-start.5 = (f32[2,2,128,128]{3,2,1,0:T(8,128)S(1)}, f32[2,2,128,128]{3,2,1,0:T(8,128)S(1)}, u32[]{:S(2)}, u32[]{:S(2)}) collective-permute-start(f32[2,2,128,128]{3,2,1,0:T(8,128)S(1)} %copy-done.19), channel_id=1, source_target_pairs={{0,32},{32,64},{64,96},{96,0},{1,33},{33,65},{65,97},{97,1},{2,34}... | collective-permute-start | bytes 786440 | tf_op jit(solution)/shard_map/ppermute | solution.py:326
  140.0 9.2 %copy-start.23 = (f32[2,2,128,128]{3,2,1,0:T(8,128)S(1)}, f32[2,2,128,128]{3,2,1,0:T(8,128)}, u32[]{:S(2)}) copy-start(f32[2,2,128,128]{3,2,1,0:T(8,128)} %get-tuple-element.47) | copy-start | bytes 786436
  140.0 9.2 %copy-start.20 = (f32[2,2,128,128]{3,2,1,0:T(8,128)S(1)}, f32[2,2,128,128]{3,2,1,0:T(8,128)}, u32[]{:S(2)}) copy-start(f32[2,2,128,128]{3,2,1,0:T(8,128)} %get-tuple-element.48) | copy-start | bytes 786436
  140.0 24.1 %copy-start.5 = (f32[16,2,128,128]{3,2,1,0:T(8,128)S(1)}, f32[16,2,128,128]{3,2,1,0:T(8,128)}, u32[]{:S(2)}) copy-start(f32[16,2,128,128]{3,2,1,0:T(8,128)} %get-tuple-element.45.z_ref) | copy-start | bytes 6291460
  140.1 59.0 %all-to-all-start.2 = ((f32[32,2,128,128]{3,2,1,0:T(8,128)}), f32[32,2,128,128]{3,2,1,0:T(8,128)}, u32[]{:S(2)}, u32[]{:S(2)}) async-start(f32[32,2,128,128]{3,2,1,0:T(8,128)} %get-tuple-element.44), calls=%async_computation.2 | async-start | bytes 8388608 | tf_op jit(solution)/shard_map/all_to_all | solution.py:324
  145.1 15.9 %collective-permute-start.6 = (f32[2,2,128,128]{3,2,1,0:T(8,128)}, f32[2,2,128,128]{3,2,1,0:T(8,128)S(1)}, u32[]{:S(2)}, u32[]{:S(2)}) collective-permute-start(f32[2,2,128,128]{3,2,1,0:T(8,128)} %get-tuple-element.46), channel_id=1, source_target_pairs={{0,96},{32,0},{64,32},{96,64},{1,97},{33,1},{65,33},{97,65},{2,98}... | collective-permute-start | bytes 786440 | tf_op jit(solution)/shard_map/ppermute | solution.py:326
  149.2 11.8 %collective-permute-start.7 = (f32[2,2,128,128]{3,2,1,0:T(8,128)S(1)}, f32[2,2,128,128]{3,2,1,0:T(8,128)S(1)}, u32[]{:S(2)}, u32[]{:S(2)}) collective-permute-start(f32[2,2,128,128]{3,2,1,0:T(8,128)S(1)} %copy-done.23), channel_id=1, source_target_pairs={{0,64},{32,96},{64,0},{96,32},{1,65},{33,97},{65,1},{97,33},{2,66}... | collective-permute-start | bytes 786440 | tf_op jit(solution)/shard_map/ppermute | solution.py:326
  149.2 14.9 %collective-permute-start.8 = (f32[2,2,128,128]{3,2,1,0:T(8,128)S(1)}, f32[2,2,128,128]{3,2,1,0:T(8,128)S(1)}, u32[]{:S(2)}, u32[]{:S(2)}) collective-permute-start(f32[2,2,128,128]{3,2,1,0:T(8,128)S(1)} %copy-done.20), channel_id=1, source_target_pairs={{0,32},{32,64},{64,96},{96,0},{1,33},{33,65},{65,97},{97,1},{2,34}... | collective-permute-start | bytes 786440 | tf_op jit(solution)/shard_map/ppermute | solution.py:326
  205.1 9.2 %copy-start.24 = (f32[2,2,128,128]{3,2,1,0:T(8,128)S(1)}, f32[2,2,128,128]{3,2,1,0:T(8,128)}, u32[]{:S(2)}) copy-start(f32[2,2,128,128]{3,2,1,0:T(8,128)} %get-tuple-element.54) | copy-start | bytes 786436
  205.1 9.2 %copy-start.21 = (f32[2,2,128,128]{3,2,1,0:T(8,128)S(1)}, f32[2,2,128,128]{3,2,1,0:T(8,128)}, u32[]{:S(2)}) copy-start(f32[2,2,128,128]{3,2,1,0:T(8,128)} %get-tuple-element.55) | copy-start | bytes 786436
  205.1 24.1 %copy-start.6 = (f32[16,2,128,128]{3,2,1,0:T(8,128)S(1)}, f32[16,2,128,128]{3,2,1,0:T(8,128)}, u32[]{:S(2)}) copy-start(f32[16,2,128,128]{3,2,1,0:T(8,128)} %get-tuple-element.52.z_ref) | copy-start | bytes 6291460
  205.1 59.0 %all-to-all-start.3 = ((f32[32,2,128,128]{3,2,1,0:T(8,128)}), f32[32,2,128,128]{3,2,1,0:T(8,128)}, u32[]{:S(2)}, u32[]{:S(2)}) async-start(f32[32,2,128,128]{3,2,1,0:T(8,128)} %get-tuple-element.51), calls=%async_computation.3 | async-start | bytes 8388608 | tf_op jit(solution)/shard_map/all_to_all | solution.py:324
  210.1 15.9 %collective-permute-start.9 = (f32[2,2,128,128]{3,2,1,0:T(8,128)}, f32[2,2,128,128]{3,2,1,0:T(8,128)S(1)}, u32[]{:S(2)}, u32[]{:S(2)}) collective-permute-start(f32[2,2,128,128]{3,2,1,0:T(8,128)} %get-tuple-element.53), channel_id=1, source_target_pairs={{0,96},{32,0},{64,32},{96,64},{1,97},{33,1},{65,33},{97,65},{2,98}... | collective-permute-start | bytes 786440 | tf_op jit(solution)/shard_map/ppermute | solution.py:326
  214.3 11.8 %collective-permute-start.10 = (f32[2,2,128,128]{3,2,1,0:T(8,128)S(1)}, f32[2,2,128,128]{3,2,1,0:T(8,128)S(1)}, u32[]{:S(2)}, u32[]{:S(2)}) collective-permute-start(f32[2,2,128,128]{3,2,1,0:T(8,128)S(1)} %copy-done.24), channel_id=1, source_target_pairs={{0,64},{32,96},{64,0},{96,32},{1,65},{33,97},{65,1},{97,33},{2,66}... | collective-permute-start | bytes 786440 | tf_op jit(solution)/shard_map/ppermute | solution.py:326
  214.3 14.9 %collective-permute-start.11 = (f32[2,2,128,128]{3,2,1,0:T(8,128)S(1)}, f32[2,2,128,128]{3,2,1,0:T(8,128)S(1)}, u32[]{:S(2)}, u32[]{:S(2)}) collective-permute-start(f32[2,2,128,128]{3,2,1,0:T(8,128)S(1)} %copy-done.21), channel_id=1, source_target_pairs={{0,32},{32,64},{64,96},{96,0},{1,33},{33,65},{65,97},{97,1},{2,34}... | collective-permute-start | bytes 786440 | tf_op jit(solution)/shard_map/ppermute | solution.py:326
  (9 other events, 18.7 us)

commit v2 on v1

v2 whole, which is shorter than its diff:
```python
import functools

import jax
import jax.numpy as jnp
from jax import lax
from jax.experimental import pallas as pl
from jax.experimental.pallas import tpu as pltpu
from jax.sharding import PartitionSpec as P

XCAP = 2
step_size = 0.1
f32, bf16 = jnp.float32, jnp.bfloat16
LIMIT = 24 << 20
WIDTH = 4
HBM = pl.BlockSpec(memory_space=pltpu.HBM)
SMEM = pl.BlockSpec(memory_space=pltpu.SMEM)
VMEM = pl.BlockSpec(memory_space=pltpu.VMEM)


def split(value):
    high = value.astype(bf16)
    return high, (value - high.astype(f32)).astype(bf16)


def prepare_kernel(h_ref, v_ref, left_ref, right_ref, row_left_ref, row_right_ref):
    n = h_ref.shape[-1]

    def put(matrix, left, right, place):
        high, low = split(matrix)
        start = place * 2 * n
        for half in range(2):
            cols = slice(start + half * n, start + (half + 1) * n)
            left[0:n, cols] = high
            left[n : 2 * n, cols] = low
            right[cols, 0:n] = high
            right[cols, n : 2 * n] = low

    terms = [h_ref[1], h_ref[0], v_ref[0], v_ref[1], v_ref[3]]
    for place, matrix in enumerate(terms):
        put(matrix, left_ref, right_ref, place)
    put(v_ref[2], row_left_ref, row_right_ref, 0)


def sandwich(terms, left, right):
    n = terms[0][0][0].shape[-1]
    columns, rows = [], []
    for (la, lb), (ra, rb) in terms:
        columns += [jnp.concatenate(pair, axis=1) for pair in zip(split(la), split(lb))]
        rows += [jnp.concatenate(pair, axis=0) for pair in zip(split(ra), split(rb))]
    stacked = jnp.concatenate(columns, axis=0)
    beside = jnp.concatenate(rows, axis=1)
    ahead = jnp.dot(left, stacked, preferred_element_type=f32)
    behind = jnp.dot(beside, right, preferred_element_type=f32)
    ahead = ahead[0:n] + ahead[n:]
    behind = behind[:, 0:n] + behind[:, n:]
    return ahead[:, 0:n] - behind[0:n], ahead[:, n:] - behind[n:]


def bath_term(ur, ui, lr, li, wr, wi):
    arr, ari, air, aii = wr * lr, wi * lr, wr * li, wi * li
    real, imag = ur + arr, ui + air
    return ((imag + ari, aii - real), (imag - ari, -real - aii))


def first_slot(tab, g):
    up, low = tab[g * 8], tab[g * 8 + 1]
    return jnp.where(up >= 0, up, low)


def when_copy(live, source, target, sem, go):
    @pl.when(live)
    def _():
        copy = pltpu.make_async_copy(source, target, sem)
        copy.start() if go else copy.wait()


def load_state(tab, g, state, buf, sem, go):
    if len(state) == 1:
        when_copy(g >= 0, state[0].at[jnp.maximum(g, 0)], buf, sem, go)
        return
    slot = first_slot(tab, jnp.maximum(g, 0))
    when_copy((g >= 0) & (slot >= 0), state[1].at[jnp.maximum(slot, 0)], buf, sem, go)
    when_copy((g >= 0) & (slot < 0), state[0].at[jnp.maximum(g, 0)], buf, sem, go)


def local_kernel(tab, wts, c1, c2, c3, left, right, *rest, states, with_sum, last_scale):
    state, rest = rest[:states], rest[states:]
    count = state[0].shape[0]
    if with_sum:
        acc_ref, *rest = rest
    keep_sum = with_sum and last_scale is None
    if keep_sum:
        out_ref, sum_ref, z_ref, cbuf, sem_z, sems = rest
    else:
        out_ref, z_ref, cbuf, sem_z, sems = rest

    @pl.loop(0, count)
    def _(g):
        load_state(tab, g, state, z_ref.at[g], sem_z.at[g], True)

    copies = [
        pltpu.make_async_copy(c, cbuf.at[pl.ds(XCAP * k, XCAP)], sems.at[k])
        for k, c in enumerate((c1, c2, c3))
    ]
    for copy in copies:
        copy.start()
    for copy in copies:
        copy.wait()

    @pl.loop(0, count)
    def _(g):
        load_state(tab, g, state, z_ref.at[g], sem_z.at[g], False)

    def one(g):
        yr, yi = z_ref[g, 0], z_ref[g, 1]
        terms = [((yr, yi), (yr, yi)), ((yi, -yr), (yi, -yr))]
        for k, (ref, bath) in enumerate(((z_ref, 0), (z_ref, 1), (cbuf, 3))):
            up, low = tab[g * 8 + 2 + 2 * k], tab[g * 8 + 3 + 2 * k]
            u, l = jnp.maximum(up, 0), jnp.maximum(low, 0)
            ur, ui = (jnp.where(up >= 0, ref[u, part], 0.0) for part in range(2))
            lr, li = (jnp.where(low >= 0, ref[l, part], 0.0) for part in range(2))
            wr, wi = wts[g * 9 + 2 * bath], wts[g * 9 + 2 * bath + 1]
            terms.append(bath_term(ur, ui, lr, li, wr, wi))
        out_r, out_i = sandwich(terms, left[...], right[...])
        damp = wts[g * 9 + 8]
        out_r, out_i = out_r - damp * yr, out_i - damp * yi
        if with_sum:
            sum_r, sum_i = acc_ref[g, 0] + yr, acc_ref[g, 1] + yi
        if last_scale is not None:
            out_r, out_i = sum_r + last_scale * out_r, sum_i + last_scale * out_i
        out_ref[g, 0], out_ref[g, 1] = out_r, out_i
        if keep_sum:
            sum_ref[g, 0], sum_ref[g, 1] = sum_r, sum_i

    width = 2

    @pl.loop(0, count // width)
    def _(step):
        for k in range(width):
            one(step * width + k)


def in_hbm(*arrays):
    return [pltpu.with_memory_space_constraint(a, pltpu.HBM) for a in arrays]


def local_part(tab, wts, state, cols, left, right, acc, last_scale):
    count, _, n, _ = state[0].shape
    with_sum = acc is not None
    outs = 2 if with_sum and last_scale is None else 1
    return pl.pallas_call(
        functools.partial(
            local_kernel, states=len(state), with_sum=with_sum, last_scale=last_scale
        ),
        out_shape=[jax.ShapeDtypeStruct(state[0].shape, f32)] * outs,
        in_specs=[SMEM, SMEM, HBM, HBM, HBM, VMEM, VMEM]
        + [HBM] * len(state)
        + [VMEM] * with_sum,
        out_specs=[VMEM] * outs,
        scratch_shapes=[
            pltpu.VMEM((count, 2, n, n), f32),
            pltpu.VMEM((3 * XCAP, 2, n, n), f32),
            pltpu.SemaphoreType.DMA((count,)),
            pltpu.SemaphoreType.DMA((3,)),
        ],
        compiler_params=pltpu.CompilerParams(vmem_limit_bytes=LIMIT),
        cost_estimate=pl.CostEstimate(
            flops=count * 160 * n * n * n, bytes_accessed=8 << 20, transcendentals=0
        ),
        name="local_part",
    )(tab, wts, *cols, left, right, *in_hbm(*state), *([acc] if with_sum else []))


def pack_columns_kernel(tab, ctab, *rest, states):
    state, (o1, o2, o3, buf, sem) = rest[:states], rest[states:]
    outs = (o1, o2, o3)
    slots = len(outs) * XCAP
    for go in (True, False):
        for k in range(slots):
            load_state(tab, ctab[k], state, buf.at[k], sem.at[k], go)
    for go in (True, False):
        for k in range(slots):
            when_copy(ctab[k] >= 0, buf.at[k], outs[k // XCAP].at[k % XCAP], sem.at[k], go)


def pack_columns(tab, ctab, state):
    count, _, n, _ = state[0].shape
    return pl.pallas_call(
        functools.partial(pack_columns_kernel, states=len(state)),
        out_shape=[pltpu.HBM((XCAP, 2, n, n), f32)] * 3,
        in_specs=[SMEM, SMEM] + [HBM] * len(state),
        out_specs=[HBM] * 3,
        scratch_shapes=[
            pltpu.VMEM((3 * XCAP, 2, n, n), f32),
            pltpu.SemaphoreType.DMA((3 * XCAP,)),
        ],
        cost_estimate=pl.CostEstimate(flops=0, bytes_accessed=1 << 20, transcendentals=0),
        name="pack_columns",
    )(tab, ctab, *in_hbm(*state))


def pack_rows_kernel(up_ref, low_ref, z_ref, row_out, buf, sem_in, sem_u, sem_l, *, missing, bath):
    count, along_y = z_ref.shape[0], row_out.shape[0]
    links = ((up_ref, sem_u), (low_ref, sem_l))

    def load(g, go):
        linked = (up_ref[g, bath] < missing) | (low_ref[g, bath] < missing)
        when_copy(linked, z_ref.at[g], buf.at[g], sem_in.at[g], go)

    def send(g, go):
        for ref, sem in links:
            target = ref[g, bath]
            slot = lax.rem(lax.div(target, count), along_y)
            when_copy(target < missing, buf.at[g], row_out.at[slot], sem.at[g], go)

    @pl.loop(0, count)
    def _(g):
        load(g, True)

    @pl.loop(0, count)
    def _(g):
        load(g, False)
        send(g, True)

    @pl.loop(0, count)
    def _(g):
        send(g, False)


def row_kernel(tab, wts, recv, part, left, right, *rest, scale, last):
    count, _, n, _ = part.shape
    if last:
        z_out, xbuf, ybuf, zbuf, sem_x, sem_y, sem_g, sem_z = rest
    else:
        z_out, row_out, xbuf, ybuf, zbuf, sem_x, sem_y, sem_g, sem_z, sem_u, sem_l = rest

    def both(g):
        return (tab[g * 8] >= 0) & (tab[g * 8 + 1] >= 0)

    def fetch(g, go):
        slot, low = first_slot(tab, g), tab[g * 8 + 1]
        when_copy(slot >= 0, recv.at[jnp.maximum(slot, 0)], xbuf.at[g], sem_x.at[g], go)
        when_copy(both(g), recv.at[jnp.maximum(low, 0)], ybuf.at[g], sem_y.at[g], go)
        if go:

            @pl.when(slot < 0)
            def _():
                xbuf[g] = jnp.zeros_like(xbuf[g])

    def fetch_part(step):
        group = pl.ds(step * WIDTH, WIDTH)
        return pltpu.make_async_copy(part.at[group], zbuf.at[group], sem_g.at[step])

    def send(g, go):
        if last:
            when_copy(g >= 0, zbuf.at[g], z_out.at[g], sem_z.at[g], go)
            return
        for k, sem in ((0, sem_u), (1, sem_l)):
            slot = tab[g * 8 + k]
            when_copy(slot >= 0, zbuf.at[g], row_out.at[jnp.maximum(slot, 0)], sem.at[g], go)
        when_copy(first_slot(tab, g) < 0, zbuf.at[g], z_out.at[g], sem_z.at[g], go)

    @pl.loop(0, count // WIDTH)
    def _(step):
        for k in range(WIDTH):
            fetch(step * WIDTH + k, True)
        fetch_part(step).start()

    def product(buf, group, reals, imags):
        ahead, beside = [], []
        for g in group:
            (hr, tr), (hi, ti) = split(buf[g, 0]), split(buf[g, 1])
            high, tail = jnp.concatenate([hr, hi], 1), jnp.concatenate([tr, ti], 1)
            stacked = jnp.concatenate([high, tail], 0)
            both_rows = jnp.dot(left[...], stacked, preferred_element_type=f32)
            ahead.append(both_rows[0:n] + both_rows[n:])
            beside.append(jnp.concatenate([hr, tr], 1))
            beside.append(jnp.concatenate([hi, ti], 1))
        behind = jnp.dot(jnp.concatenate(beside, 0), right[...], preferred_element_type=f32)
        behind = behind[:, 0:n] + behind[:, n:]
        for k, (real, imag) in enumerate(zip(reals, imags)):
            ar, ai = ahead[k][:, 0:n], ahead[k][:, n:]
            br, bi = (behind[(2 * k + p) * n : (2 * k + p + 1) * n] for p in range(2))
            yield real * (ai - bi) + imag * (ar + br), imag * (ai + bi) - real * (ar - br)

    def weights(g):
        return wts[g * 9 + 4], wts[g * 9 + 5]

    @pl.loop(0, count // WIDTH)
    def _(step):
        group = [step * WIDTH + k for k in range(WIDTH)]
        for g in group:
            fetch(g, False)
        fetch_part(step).wait()
        above = [tab[g * 8] >= 0 for g in group]
        reals = [jnp.where(a, 1.0, weights(g)[0]) for a, g in zip(above, group)]
        imags = [jnp.where(a, 0.0, weights(g)[1]) for a, g in zip(above, group)]
        for g, term in zip(group, product(xbuf, group, reals, imags)):
            for p in range(2):
                if last:
                    zbuf[g, p] = zbuf[g, p] + scale * term[p]
                else:
                    zbuf[g, p] = scale * (zbuf[g, p] + term[p])
        for g in group:

            @pl.when(both(g))
            def _():
                wr, wi = weights(g)
                (term,) = product(ybuf, [g], [wr], [wi])
                for p in range(2):
                    zbuf[g, p] = zbuf[g, p] + scale * term[p]

        for g in group:
            send(g, True)

    @pl.loop(0, count)
    def _(g):
        send(g, False)


def row_part(tab, wts, recv, part, left, right, scale, last):
    count, _, n, _ = part.shape
    outs = [jax.ShapeDtypeStruct(part.shape, f32) if last else pltpu.HBM(part.shape, f32)]
    if not last:
        outs += [pltpu.HBM(recv.shape, f32)]
    return pl.pallas_call(
        functools.partial(row_kernel, scale=scale, last=last),
        out_shape=outs,
        in_specs=[SMEM, SMEM, HBM, HBM, VMEM, VMEM],
        out_specs=[HBM] * len(outs),
        scratch_shapes=[pltpu.VMEM((count, 2, n, n), f32)] * 3
        + [pltpu.SemaphoreType.DMA((count,))] * (4 if last else 6),
        compiler_params=pltpu.CompilerParams(vmem_limit_bytes=LIMIT),
        cost_estimate=pl.CostEstimate(
            flops=count * 32 * n * n * n, bytes_accessed=10 << 20, transcendentals=0
        ),
        name="row_part",
    )(tab, wts, *in_hbm(recv, part), left, right)


def local(
    densities, hamiltonian, couplings, decay_rates, correlation, upper_link, lower_link, occupation
):
    count, _, n, _ = densities.shape
    along_y, along_x = lax.axis_size("gy"), lax.axis_size("gx")
    index_x, index_y = lax.axis_index("gx"), lax.axis_index("gy")
    own = index_x * along_y + index_y
    missing = count * along_y * along_x

    row_send = pl.pallas_call(
        functools.partial(pack_rows_kernel, missing=missing, bath=2),
        out_shape=pltpu.HBM((along_y, 2, n, n), f32),
        in_specs=[SMEM, SMEM, HBM],
        out_specs=HBM,
        scratch_shapes=[pltpu.VMEM((count, 2, n, n), f32)]
        + [pltpu.SemaphoreType.DMA((count,))] * 3,
        name="pack_rows",
    )(upper_link, lower_link, densities)

    links = jnp.stack([upper_link, lower_link], axis=2)
    live = links < missing
    near = jnp.where(live[:, 0:2], links[:, 0:2] - own * count, -1).reshape(count, 4)
    rows = jnp.where(live[:, 2], (links[:, 2] // count) % along_y, -1)

    targets, usable = links[:, 3].reshape(-1), live[:, 3].reshape(-1)
    sources = jnp.repeat(jnp.arange(count, dtype=jnp.int32), 2)
    relative = (targets // count // along_y - index_x) % along_x
    same = usable[:, None] & usable[None, :] & (relative[:, None] == relative[None, :])
    start = (relative - 1) * XCAP
    recv_slot = start + jnp.any(same & (targets[None, :] < targets[:, None]), axis=1)
    send_slot = start + jnp.any(same & (sources[None, :] < sources[:, None]), axis=1)
    recv_slot = jnp.where(usable, recv_slot, -1).reshape(count, 2)
    hit = (send_slot[None, :] == jnp.arange(6, dtype=jnp.int32)[:, None]) & usable[None, :]
    ctab = jnp.max(jnp.where(hit, sources[None, :], -1), axis=1)
    tab = jnp.concatenate([rows, near, recv_slot], axis=1).reshape(-1).astype(jnp.int32)

    level = occupation.astype(f32)
    damping = jnp.sum(level * decay_rates[None, :], axis=1, keepdims=True)
    pairs = (level[:, :, None] * correlation.T[None, :, :]).reshape(count, 8)
    wts = jnp.concatenate([pairs, damping], axis=1).reshape(-1)

    mats = lambda rows, cols: jax.ShapeDtypeStruct((rows, cols), bf16)
    left, right, row_left, row_right = pl.pallas_call(
        prepare_kernel,
        out_shape=[mats(2 * n, 10 * n), mats(10 * n, 2 * n), mats(2 * n, 2 * n), mats(2 * n, 2 * n)],
        in_specs=[VMEM, VMEM],
        out_specs=[VMEM] * 4,
        name="prepare",
    )(hamiltonian, couplings)

    state, acc = [densities], None
    for stage in range(1, 5):
        recv = lax.all_to_all(row_send, "gy", split_axis=0, concat_axis=0, tiled=True)
        col_send = pack_columns(tab, ctab, state)
        arrived = [
            lax.ppermute(col_send[s - 1], "gx", [(x, (x + s) % along_x) for x in range(along_x)])
            for s in range(1, along_x)
        ]
        scale, last = step_size / stage, stage == 4
        part = local_part(
            tab, wts, state, arrived[::-1], left, right, acc, scale if last else None
        )
        if stage == 1:
            acc = densities
        elif not last:
            acc = part[1]
        outs = row_part(tab, wts, recv, part[0], row_left, row_right, scale, last)
        if last:
            return outs[0]
        state, row_send = outs, outs[1]


def solution(mesh):
    return jax.shard_map(
        local,
        mesh=mesh,
        in_specs=(
            P(("gx", "gy"), None, None, None),
            P(),
            P(),
            P(),
            P(),
            P(("gx", "gy"), None),
            P(("gx", "gy"), None),
            P(("gx", "gy"), None),
        ),
        out_specs=P(("gx", "gy"), None, None, None),
        check_vma=False,
    )
```

time: 270 us -> 268 us (level)
  waiting for transfers between devices: 135 us -> 124 us
  local copies, waits for them, and re-layouts: 11.9 us -> 18.8 us
    all_to_all x4, waiting for transfers between devices: 82.5 us -> 74.6 us  [local(): lax.all_to_all(row_send, 'gy', split_axis=0, concat_axis=0, tiled=True)]
    unnamed x50 -> x52, local copies, waits for them, and re-layouts: 10.3 us -> 17.1 us
    pallas_call x6 -> x9, Pallas kernels: 49.2 us -> 52.7 us  [the longest x4 38.4 us: local_part(): pl.pallas_call(functools.partial(local_kernel, states=len(state), with_su...]
    ppermute x12, waiting for transfers between devices: 52.4 us -> 49.1 us  [local(): lax.ppermute(col_send[s - 1], 'gx', [(x, (x + s) % along_x) for x in rang...]
  transfers between devices with their start and end apart: 16 -> 16, of which waited for: 12 -> 13; matrix products, arithmetic and copies ran while one was open for 0% -> 1% of each run, Pallas kernels for 18% -> 19%
where the time goes in v2:
time: 268 us; the launch traced here: 267 us
  waiting for transfers between devices  124 us (46%)
  Pallas kernels  77.6 us (29%)
  starting transfers between devices  45.4 us (17%)
  local copies, waits for them, and re-layouts  18.8 us (7%)
    all_to_all x4, waiting for transfers between devices, local(): lax.all_to_all(row_send, 'gy', split_axis=0, concat_axis=0, tiled=True)  74.6 us
    ppermute x12, waiting for transfers between devices, local(): lax.ppermute(col_send[s - 1], 'gx', [(x, (x + s) % along_x) for x in rang...  49.1 us
    pallas_call x4, Pallas kernels, local_part(): pl.pallas_call(functools.partial(local_kernel, states=len(state), with_su...  38.4 us
    ppermute x12, starting transfers between devices, local(): lax.ppermute(col_send[s - 1], 'gx', [(x, (x + s) % along_x) for x in rang...  23 us
    pallas_call x4, Pallas kernels, row_part(): pl.pallas_call(functools.partial(row_kernel, scale=scale, last=last), out...  22.5 us
    all_to_all x4, starting transfers between devices, local(): lax.all_to_all(row_send, 'gy', split_axis=0, concat_axis=0, tiled=True)  22.3 us
    unnamed x52, local copies, waits for them, and re-layouts  17.1 us
    pallas_call x4, Pallas kernels, pack_columns(): pl.pallas_call(functools.partial(pack_columns_kernel, states=len(state)),...  10.7 us
  transfers between devices with their start and end apart: 16, of which 13 were waited for; matrix products, arithmetic and copies ran while one was open for 1% of the time, Pallas kernels for 19%

profile of v2, /device:TPU:0, one launch (start us, length us, event | category | flops | bytes accessed | tf_op | source)
XLA Modules:
  0.0 267.2 jit_solution(12738529656520187627)
XLA Ops:
  2.7 3.6 %pack_rows.1 = f32[32,2,128,128]{3,2,1,0:T(8,128)} custom-call(s32[16,4]{1,0:T(8,128)} %copy.33.up_ref, s32[16,4]{1,0:T(8,128)} %copy.34.low_ref, f32[16,2,128,128]{3,2,1,0:T(8,128)} %rest_2_.1), custom_call_target="tpu_custom_call" | custom-call | tf_op jit(solution)/shard_map/pack_rows/pallas_call | solution.py:350
  6.3 7.7 %all-to-all-start = ((f32[32,2,128,128]{3,2,1,0:T(8,128)}), f32[32,2,128,128]{3,2,1,0:T(8,128)}, u32[]{:S(2)}, u32[]{:S(2)}) async-start(f32[32,2,128,128]{3,2,1,0:T(8,128)} %pack_rows.1), calls=%async_computation | async-start | bytes 8388608 | tf_op jit(solution)/shard_map/all_to_all | solution.py:393
  19.1 4.1 %collective-permute-start = (f32[2,2,128,128]{3,2,1,0:T(8,128)}, f32[2,2,128,128]{3,2,1,0:T(8,128)S(1)}, u32[]{:S(2)}, u32[]{:S(2)}) collective-permute-start(f32[2,2,128,128]{3,2,1,0:T(8,128)} %get-tuple-element.31), channel_id=1, source_target_pairs={{0,96},{32,0},{64,32},{96,64},{1,97},{33,1},{65,33},{97,65},{2,98}... | collective-permute-start | bytes 786440 | tf_op jit(solution)/shard_map/ppermute | solution.py:396
  27.3 7.8 %collective-permute-done.c1 = f32[2,2,128,128]{3,2,1,0:T(8,128)S(1)} collective-permute-done((f32[2,2,128,128]{3,2,1,0:T(8,128)}, f32[2,2,128,128]{3,2,1,0:T(8,128)S(1)}, u32[]{:S(2)}, u32[]{:S(2)}) %collective-permute-start) | collective-permute-done | bytes 262176 | tf_op jit(solution)/shard_map/ppermute | solution.py:396
  35.1 3.3 %collective-permute-done.2.c3 = f32[2,2,128,128]{3,2,1,0:T(8,128)S(1)} collective-permute-done((f32[2,2,128,128]{3,2,1,0:T(8,128)}, f32[2,2,128,128]{3,2,1,0:T(8,128)S(1)}, u32[]{:S(2)}, u32[]{:S(2)}) %collective-permute-start.2) | collective-permute-done | bytes 262176 | tf_op jit(solution)/shard_map/ppermute | solution.py:396
  40.6 9.2 %local_part.4.part = f32[16,2,128,128]{3,2,1,0:T(8,128)S(1)} custom-call(s32[128]{0:T(128)S(1)} %copy-done.7, f32[144]{0:T(256)S(1)} %reshape.155.wts, f32[2,2,128,128]{3,2,1,0:T(8,128)S(1)} %collective-permute-done.c1, f32[2,2,128,128]{3,2,1,0:T(8,128)S(1)} %collective-permute-done.1.c2, f32[2,2,128,128]{3,2,1,0:T(8,128)S(1)} %collective-permute-done.2.c3, ...), custom_call_target="tpu_custom_call" | custom-call | flops 5368709120 | bytes 8388608 | tf_op jit(solution)/shard_map/local_part/pallas_call | solution.py:151
  51.1 16.9 %all-to-all-done.recv = f32[32,2,128,128]{3,2,1,0:T(8,128)} async-done(((f32[32,2,128,128]{3,2,1,0:T(8,128)}), f32[32,2,128,128]{3,2,1,0:T(8,128)}, u32[]{:S(2)}, u32[]{:S(2)}) %all-to-all-start) | async-done | bytes 4194336 | tf_op jit(solution)/shard_map/all_to_all | solution.py:393
  68.0 5.7 %row_part.4 = (f32[16,2,128,128]{3,2,1,0:T(8,128)}, f32[32,2,128,128]{3,2,1,0:T(8,128)}) custom-call(s32[128]{0:T(128)S(1)} %copy-done.7, f32[144]{0:T(256)S(1)} %reshape.155.wts, f32[32,2,128,128]{3,2,1,0:T(8,128)} %all-to-all-done.recv, f32[16,2,128,128]{3,2,1,0:T(8,128)} %copy-done.6, bf16[256,256]{1,0:T(8,128)(2,1)S(1)} %copy-done.1, ...), custom_call_target="tpu_custom_call" | custom-call | flops 1073741824 | bytes 10485760 | tf_op jit(solution)/shard_map/row_part/pallas_call | solution.py:326
  73.8 4.9 %all-to-all-start.1 = ((f32[32,2,128,128]{3,2,1,0:T(8,128)}), f32[32,2,128,128]{3,2,1,0:T(8,128)}, u32[]{:S(2)}, u32[]{:S(2)}) async-start(f32[32,2,128,128]{3,2,1,0:T(8,128)} %get-tuple-element.38.rest_1_), calls=%async_computation.1 | async-start | bytes 8388608 | tf_op jit(solution)/shard_map/all_to_all | solution.py:393
  78.7 2.7 %pack_columns.5 = (f32[2,2,128,128]{3,2,1,0:T(8,128)}, f32[2,2,128,128]{3,2,1,0:T(8,128)}, f32[2,2,128,128]{3,2,1,0:T(8,128)}) custom-call(s32[128]{0:T(128)} %reshape.154.tab, s32[6]{0:T(128)} %select_reduce_fusion.ctab, f32[16,2,128,128]{3,2,1,0:T(8,128)} %get-tuple-element.39.rest_0_, f32[32,2,128,128]{3,2,1,0:T(8,128)} %get-tuple-element.38.rest_1_), custom_call_target="tpu_custom_call" | custom-call | bytes 1048576 | tf_op jit(solution)/shard_map/pack_columns/pallas_call | solution.py:188
  81.4 4.1 %collective-permute-start.3 = (f32[2,2,128,128]{3,2,1,0:T(8,128)}, f32[2,2,128,128]{3,2,1,0:T(8,128)S(1)}, u32[]{:S(2)}, u32[]{:S(2)}) collective-permute-start(f32[2,2,128,128]{3,2,1,0:T(8,128)} %get-tuple-element.40), channel_id=1, source_target_pairs={{0,96},{32,0},{64,32},{96,64},{1,97},{33,1},{65,33},{97,65},{2,98}... | collective-permute-start | bytes 786440 | tf_op jit(solution)/shard_map/ppermute | solution.py:396
  86.7 10.6 %collective-permute-done.3.c1 = f32[2,2,128,128]{3,2,1,0:T(8,128)S(1)} collective-permute-done((f32[2,2,128,128]{3,2,1,0:T(8,128)}, f32[2,2,128,128]{3,2,1,0:T(8,128)S(1)}, u32[]{:S(2)}, u32[]{:S(2)}) %collective-permute-start.3) | collective-permute-done | bytes 262176 | tf_op jit(solution)/shard_map/ppermute | solution.py:396
  97.3 3.3 %collective-permute-done.5.c3 = f32[2,2,128,128]{3,2,1,0:T(8,128)S(1)} collective-permute-done((f32[2,2,128,128]{3,2,1,0:T(8,128)}, f32[2,2,128,128]{3,2,1,0:T(8,128)S(1)}, u32[]{:S(2)}, u32[]{:S(2)}) %collective-permute-start.5) | collective-permute-done | bytes 262176 | tf_op jit(solution)/shard_map/ppermute | solution.py:396
  101.7 9.6 %local_part.5 = (f32[16,2,128,128]{3,2,1,0:T(8,128)S(1)}, f32[16,2,128,128]{3,2,1,0:T(8,128)S(1)}) custom-call(s32[128]{0:T(128)S(1)} %copy-done.8, f32[144]{0:T(256)S(1)} %reshape.155.wts, f32[2,2,128,128]{3,2,1,0:T(8,128)S(1)} %collective-permute-done.3.c1, f32[2,2,128,128]{3,2,1,0:T(8,128)S(1)} %collective-permute-done.4.c2, ...), custom_call_target="tpu_custom_call" | custom-call | flops 5368709120 | bytes 8388608 | tf_op jit(solution)/shard_map/local_part/pallas_call | solution.py:151
  114.0 18.6 %all-to-all-done.1.recv = f32[32,2,128,128]{3,2,1,0:T(8,128)} async-done(((f32[32,2,128,128]{3,2,1,0:T(8,128)}), f32[32,2,128,128]{3,2,1,0:T(8,128)}, u32[]{:S(2)}, u32[]{:S(2)}) %all-to-all-start.1) | async-done | bytes 4194336 | tf_op jit(solution)/shard_map/all_to_all | solution.py:393
  132.6 5.7 %row_part.5 = (f32[16,2,128,128]{3,2,1,0:T(8,128)}, f32[32,2,128,128]{3,2,1,0:T(8,128)}) custom-call(s32[128]{0:T(128)S(1)} %copy-done.8, f32[144]{0:T(256)S(1)} %reshape.155.wts, f32[32,2,128,128]{3,2,1,0:T(8,128)} %all-to-all-done.1.recv, f32[16,2,128,128]{3,2,1,0:T(8,128)} %copy-done.5, bf16[256,256]{1,0:T(8,128)(2,1)S(1)} %copy-done.1, ...), custom_call_target="tpu_custom_call" | custom-call | flops 1073741824 | bytes 10485760 | tf_op jit(solution)/shard_map/row_part/pallas_call | solution.py:326
  138.3 4.9 %all-to-all-start.2 = ((f32[32,2,128,128]{3,2,1,0:T(8,128)}), f32[32,2,128,128]{3,2,1,0:T(8,128)}, u32[]{:S(2)}, u32[]{:S(2)}) async-start(f32[32,2,128,128]{3,2,1,0:T(8,128)} %get-tuple-element.44.rest_1_), calls=%async_computation.2 | async-start | bytes 8388608 | tf_op jit(solution)/shard_map/all_to_all | solution.py:393
  143.2 2.7 %pack_columns.6 = (f32[2,2,128,128]{3,2,1,0:T(8,128)}, f32[2,2,128,128]{3,2,1,0:T(8,128)}, f32[2,2,128,128]{3,2,1,0:T(8,128)}) custom-call(s32[128]{0:T(128)} %reshape.154.tab, s32[6]{0:T(128)} %select_reduce_fusion.ctab, f32[16,2,128,128]{3,2,1,0:T(8,128)} %get-tuple-element.45.rest_0_, f32[32,2,128,128]{3,2,1,0:T(8,128)} %get-tuple-element.44.rest_1_), custom_call_target="tpu_custom_call" | custom-call | bytes 1048576 | tf_op jit(solution)/shard_map/pack_columns/pallas_call | solution.py:188
  146.0 4.2 %collective-permute-start.6 = (f32[2,2,128,128]{3,2,1,0:T(8,128)}, f32[2,2,128,128]{3,2,1,0:T(8,128)S(1)}, u32[]{:S(2)}, u32[]{:S(2)}) collective-permute-start(f32[2,2,128,128]{3,2,1,0:T(8,128)} %get-tuple-element.46), channel_id=1, source_target_pairs={{0,96},{32,0},{64,32},{96,64},{1,97},{33,1},{65,33},{97,65},{2,98}... | collective-permute-start | bytes 786440 | tf_op jit(solution)/shard_map/ppermute | solution.py:396
  151.3 10.7 %collective-permute-done.6.c1 = f32[2,2,128,128]{3,2,1,0:T(8,128)S(1)} collective-permute-done((f32[2,2,128,128]{3,2,1,0:T(8,128)}, f32[2,2,128,128]{3,2,1,0:T(8,128)S(1)}, u32[]{:S(2)}, u32[]{:S(2)}) %collective-permute-start.6) | collective-permute-done | bytes 262176 | tf_op jit(solution)/shard_map/ppermute | solution.py:396
  162.0 3.3 %collective-permute-done.8.c3 = f32[2,2,128,128]{3,2,1,0:T(8,128)S(1)} collective-permute-done((f32[2,2,128,128]{3,2,1,0:T(8,128)}, f32[2,2,128,128]{3,2,1,0:T(8,128)S(1)}, u32[]{:S(2)}, u32[]{:S(2)}) %collective-permute-start.8) | collective-permute-done | bytes 262176 | tf_op jit(solution)/shard_map/ppermute | solution.py:396
  166.9 9.8 %local_part.6 = (f32[16,2,128,128]{3,2,1,0:T(8,128)S(1)}, f32[16,2,128,128]{3,2,1,0:T(8,128)S(1)}) custom-call(s32[128]{0:T(128)S(1)} %copy-done.9, f32[144]{0:T(256)S(1)} %reshape.155.wts, f32[2,2,128,128]{3,2,1,0:T(8,128)S(1)} %collective-permute-done.6.c1, f32[2,2,128,128]{3,2,1,0:T(8,128)S(1)} %collective-permute-done.7.c2, ...), custom_call_target="tpu_custom_call" | custom-call | flops 5368709120 | bytes 8388608 | tf_op jit(solution)/shard_map/local_part/pallas_call | solution.py:151
  179.3 17.9 %all-to-all-done.2.recv = f32[32,2,128,128]{3,2,1,0:T(8,128)} async-done(((f32[32,2,128,128]{3,2,1,0:T(8,128)}), f32[32,2,128,128]{3,2,1,0:T(8,128)}, u32[]{:S(2)}, u32[]{:S(2)}) %all-to-all-start.2) | async-done | bytes 4194336 | tf_op jit(solution)/shard_map/all_to_all | solution.py:393
  197.2 5.7 %row_part.6 = (f32[16,2,128,128]{3,2,1,0:T(8,128)}, f32[32,2,128,128]{3,2,1,0:T(8,128)}) custom-call(s32[128]{0:T(128)S(1)} %copy-done.9, f32[144]{0:T(256)S(1)} %reshape.155.wts, f32[32,2,128,128]{3,2,1,0:T(8,128)} %all-to-all-done.2.recv, f32[16,2,128,128]{3,2,1,0:T(8,128)} %copy-done.4, bf16[256,256]{1,0:T(8,128)(2,1)S(1)} %copy-done.1, ...), custom_call_target="tpu_custom_call" | custom-call | flops 1073741824 | bytes 10485760 | tf_op jit(solution)/shard_map/row_part/pallas_call | solution.py:326
  202.9 4.9 %all-to-all-start.3 = ((f32[32,2,128,128]{3,2,1,0:T(8,128)}), f32[32,2,128,128]{3,2,1,0:T(8,128)}, u32[]{:S(2)}, u32[]{:S(2)}) async-start(f32[32,2,128,128]{3,2,1,0:T(8,128)} %get-tuple-element.51.rest_1_), calls=%async_computation.3 | async-start | bytes 8388608 | tf_op jit(solution)/shard_map/all_to_all | solution.py:393
  207.8 2.7 %pack_columns.7 = (f32[2,2,128,128]{3,2,1,0:T(8,128)}, f32[2,2,128,128]{3,2,1,0:T(8,128)}, f32[2,2,128,128]{3,2,1,0:T(8,128)}) custom-call(s32[128]{0:T(128)} %reshape.154.tab, s32[6]{0:T(128)} %select_reduce_fusion.ctab, f32[16,2,128,128]{3,2,1,0:T(8,128)} %get-tuple-element.52.rest_0_, f32[32,2,128,128]{3,2,1,0:T(8,128)} %get-tuple-element.51.rest_1_), custom_call_target="tpu_custom_call" | custom-call | bytes 1048576 | tf_op jit(solution)/shard_map/pack_columns/pallas_call | solution.py:188
  210.5 3.9 %collective-permute-start.10 = (f32[2,2,128,128]{3,2,1,0:T(8,128)}, f32[2,2,128,128]{3,2,1,0:T(8,128)S(1)}, u32[]{:S(2)}, u32[]{:S(2)}) collective-permute-start(f32[2,2,128,128]{3,2,1,0:T(8,128)} %get-tuple-element.54), channel_id=1, source_target_pairs={{0,64},{32,96},{64,0},{96,32},{1,65},{33,97},{65,1},{97,33},{2,66}... | collective-permute-start | bytes 786440 | tf_op jit(solution)/shard_map/ppermute | solution.py:396
  217.6 4.2 %collective-permute-done.10.c2 = f32[2,2,128,128]{3,2,1,0:T(8,128)S(1)} collective-permute-done((f32[2,2,128,128]{3,2,1,0:T(8,128)}, f32[2,2,128,128]{3,2,1,0:T(8,128)S(1)}, u32[]{:S(2)}, u32[]{:S(2)}) %collective-permute-start.10) | collective-permute-done | bytes 262176 | tf_op jit(solution)/shard_map/ppermute | solution.py:396
  221.8 5.0 %collective-permute-done.11.c3 = f32[2,2,128,128]{3,2,1,0:T(8,128)S(1)} collective-permute-done((f32[2,2,128,128]{3,2,1,0:T(8,128)}, f32[2,2,128,128]{3,2,1,0:T(8,128)S(1)}, u32[]{:S(2)}, u32[]{:S(2)}) %collective-permute-start.11) | collective-permute-done | bytes 262176 | tf_op jit(solution)/shard_map/ppermute | solution.py:396
  229.4 9.7 %local_part.7.part = f32[16,2,128,128]{3,2,1,0:T(8,128)S(1)} custom-call(s32[128]{0:T(128)S(1)} %copy-done.10, f32[144]{0:T(256)S(1)} %reshape.155.wts, f32[2,2,128,128]{3,2,1,0:T(8,128)S(1)} %collective-permute-done.9.c1, f32[2,2,128,128]{3,2,1,0:T(8,128)S(1)} %collective-permute-done.10.c2, f32[2,2,128,128]{3,2,1,0:T(8,128)S(1)} %collective-permute-done.11.c3, ...), custom_call_target="tpu_custom_call" | custom-call | flops 5368709120 | bytes 8388608 | tf_op jit(solution)/shard_map/local_part/pallas_call | solution.py:151
  240.4 21.3 %all-to-all-done.3.recv = f32[32,2,128,128]{3,2,1,0:T(8,128)} async-done(((f32[32,2,128,128]{3,2,1,0:T(8,128)}), f32[32,2,128,128]{3,2,1,0:T(8,128)}, u32[]{:S(2)}, u32[]{:S(2)}) %all-to-all-start.3) | async-done | bytes 4194336 | tf_op jit(solution)/shard_map/all_to_all | solution.py:393
  261.7 5.3 %row_part.7 = f32[16,2,128,128]{3,2,1,0:T(8,128)} custom-call(s32[128]{0:T(128)S(1)} %copy-done.10, f32[144]{0:T(256)S(1)} %reshape.155.wts, f32[32,2,128,128]{3,2,1,0:T(8,128)} %all-to-all-done.3.recv, f32[16,2,128,128]{3,2,1,0:T(8,128)} %copy-done.3, bf16[256,256]{1,0:T(8,128)(2,1)S(1)} %copy-done.1, bf16[256,256]{1,0:T(8,128)(2,1)S(1)} %copy-done.2), custom_call_target="tpu_custom_call" | custom-call | flops 1073741824 | bytes 10485760 | tf_op jit(solution)/shard_map/row_part/pallas_call | solution.py:326
  (97 shorter events, 32.6 us)
Async XLA Ops:
  6.3 7.8 %copy-start.20 = (s32[16,4]{0,1:T(4,128)S(1)}, s32[16,4]{0,1:T(4,128)}, u32[]{:S(2)}) copy-start(s32[16,4]{0,1:T(4,128)} %param.14) | copy-start | bytes 772
  6.3 7.8 %copy-start.21 = (s32[16,4]{0,1:T(4,128)S(1)}, s32[16,4]{0,1:T(4,128)}, u32[]{:S(2)}) copy-start(s32[16,4]{0,1:T(4,128)} %param.13) | copy-start | bytes 772
  6.3 61.7 %all-to-all-start = ((f32[32,2,128,128]{3,2,1,0:T(8,128)}), f32[32,2,128,128]{3,2,1,0:T(8,128)}, u32[]{:S(2)}, u32[]{:S(2)}) async-start(f32[32,2,128,128]{3,2,1,0:T(8,128)} %pack_rows.1), calls=%async_computation | async-start | bytes 8388608 | tf_op jit(solution)/shard_map/all_to_all | solution.py:393
  14.1 10.4 %copy-start.22 = (s32[16,4]{0,1:T(4,128)S(1)}, s32[16,4]{0,1:T(4,128)}, u32[]{:S(2)}) copy-start(s32[16,4]{0,1:T(4,128)} %param.15) | copy-start | bytes 772
  14.1 10.4 %copy-start.23 = (f32[2,4]{1,0:T(2,128)S(1)}, f32[2,4]{1,0:T(2,128)}, u32[]{:S(2)}) copy-start(f32[2,4]{1,0:T(2,128)} %param.12) | copy-start | bytes 100
  14.1 10.6 %copy-start.24 = (f32[4]{0:T(128)S(1)}, f32[4]{0:T(128)}, u32[]{:S(2)}) copy-start(f32[4]{0:T(128)} %param.11) | copy-start | bytes 52
  15.8 22.6 %copy-start.7 = (s32[128]{0:T(128)S(1)}, s32[128]{0:T(128)}, u32[]{:S(2)}) copy-start(s32[128]{0:T(128)} %reshape.154.tab) | copy-start | bytes 1540
  19.1 15.9 %collective-permute-start = (f32[2,2,128,128]{3,2,1,0:T(8,128)}, f32[2,2,128,128]{3,2,1,0:T(8,128)S(1)}, u32[]{:S(2)}, u32[]{:S(2)}) collective-permute-start(f32[2,2,128,128]{3,2,1,0:T(8,128)} %get-tuple-element.31), channel_id=1, source_target_pairs={{0,96},{32,0},{64,32},{96,64},{1,97},{33,1},{65,33},{97,65},{2,98}... | collective-permute-start | bytes 786440 | tf_op jit(solution)/shard_map/ppermute | solution.py:396
  23.2 11.9 %collective-permute-start.1 = (f32[2,2,128,128]{3,2,1,0:T(8,128)}, f32[2,2,128,128]{3,2,1,0:T(8,128)S(1)}, u32[]{:S(2)}, u32[]{:S(2)}) collective-permute-start(f32[2,2,128,128]{3,2,1,0:T(8,128)} %get-tuple-element.32), channel_id=1, source_target_pairs={{0,64},{32,96},{64,0},{96,32},{1,65},{33,97},{65,1},{97,33},{2,66}... | collective-permute-start | bytes 786440 | tf_op jit(solution)/shard_map/ppermute | solution.py:396
  23.2 15.2 %collective-permute-start.2 = (f32[2,2,128,128]{3,2,1,0:T(8,128)}, f32[2,2,128,128]{3,2,1,0:T(8,128)S(1)}, u32[]{:S(2)}, u32[]{:S(2)}) collective-permute-start(f32[2,2,128,128]{3,2,1,0:T(8,128)} %get-tuple-element.33), channel_id=1, source_target_pairs={{0,32},{32,64},{64,96},{96,0},{1,33},{33,65},{65,97},{97,1},{2,34}... | collective-permute-start | bytes 786440 | tf_op jit(solution)/shard_map/ppermute | solution.py:396
  40.6 27.5 %copy-start.1 = (bf16[256,256]{1,0:T(8,128)(2,1)S(1)}, bf16[256,256]{1,0:T(8,128)(2,1)}, u32[]{:S(2)}) copy-start(bf16[256,256]{1,0:T(8,128)(2,1)} %get-tuple-element.36.left) | copy-start | bytes 393220
  40.6 27.5 %copy-start.2 = (bf16[256,256]{1,0:T(8,128)(2,1)S(1)}, bf16[256,256]{1,0:T(8,128)(2,1)}, u32[]{:S(2)}) copy-start(bf16[256,256]{1,0:T(8,128)(2,1)} %get-tuple-element.37.right) | copy-start | bytes 393220
  73.8 58.8 %all-to-all-start.1 = ((f32[32,2,128,128]{3,2,1,0:T(8,128)}), f32[32,2,128,128]{3,2,1,0:T(8,128)}, u32[]{:S(2)}, u32[]{:S(2)}) async-start(f32[32,2,128,128]{3,2,1,0:T(8,128)} %get-tuple-element.38.rest_1_), calls=%async_computation.1 | async-start | bytes 8388608 | tf_op jit(solution)/shard_map/all_to_all | solution.py:393
  78.6 22.0 %copy-start = (f32[16,2,128,128]{3,2,1,0:T(8,128)S(1)}, f32[16,2,128,128]{3,2,1,0:T(8,128)}, u32[]{:S(2)}) copy-start(f32[16,2,128,128]{3,2,1,0:T(8,128)} %rest_2_.1) | copy-start | bytes 6291460
  78.7 22.0 %copy-start.8 = (s32[128]{0:T(128)S(1)}, s32[128]{0:T(128)}, u32[]{:S(2)}) copy-start(s32[128]{0:T(128)} %reshape.154.tab) | copy-start | bytes 1540
  78.7 22.0 %copy-start.12 = (bf16[256,1280]{1,0:T(8,128)(2,1)S(1)}, bf16[256,1280]{1,0:T(8,128)(2,1)}, u32[]{:S(2)}) copy-start(bf16[256,1280]{1,0:T(8,128)(2,1)} %get-tuple-element.34.left) | copy-start | bytes 1966084
  81.4 15.9 %collective-permute-start.3 = (f32[2,2,128,128]{3,2,1,0:T(8,128)}, f32[2,2,128,128]{3,2,1,0:T(8,128)S(1)}, u32[]{:S(2)}, u32[]{:S(2)}) collective-permute-start(f32[2,2,128,128]{3,2,1,0:T(8,128)} %get-tuple-element.40), channel_id=1, source_target_pairs={{0,96},{32,0},{64,32},{96,64},{1,97},{33,1},{65,33},{97,65},{2,98}... | collective-permute-start | bytes 786440 | tf_op jit(solution)/shard_map/ppermute | solution.py:396
  85.6 11.8 %collective-permute-start.4 = (f32[2,2,128,128]{3,2,1,0:T(8,128)}, f32[2,2,128,128]{3,2,1,0:T(8,128)S(1)}, u32[]{:S(2)}, u32[]{:S(2)}) collective-permute-start(f32[2,2,128,128]{3,2,1,0:T(8,128)} %get-tuple-element.41), channel_id=1, source_target_pairs={{0,64},{32,96},{64,0},{96,32},{1,65},{33,97},{65,1},{97,33},{2,66}... | collective-permute-start | bytes 786440 | tf_op jit(solution)/shard_map/ppermute | solution.py:396
  85.6 15.1 %collective-permute-start.5 = (f32[2,2,128,128]{3,2,1,0:T(8,128)}, f32[2,2,128,128]{3,2,1,0:T(8,128)S(1)}, u32[]{:S(2)}, u32[]{:S(2)}) collective-permute-start(f32[2,2,128,128]{3,2,1,0:T(8,128)} %get-tuple-element.42), channel_id=1, source_target_pairs={{0,32},{32,64},{64,96},{96,0},{1,33},{33,65},{65,97},{97,1},{2,34}... | collective-permute-start | bytes 786440 | tf_op jit(solution)/shard_map/ppermute | solution.py:396
  138.3 58.8 %all-to-all-start.2 = ((f32[32,2,128,128]{3,2,1,0:T(8,128)}), f32[32,2,128,128]{3,2,1,0:T(8,128)}, u32[]{:S(2)}, u32[]{:S(2)}) async-start(f32[32,2,128,128]{3,2,1,0:T(8,128)} %get-tuple-element.44.rest_1_), calls=%async_computation.2 | async-start | bytes 8388608 | tf_op jit(solution)/shard_map/all_to_all | solution.py:393
  143.2 22.1 %copy-start.9 = (s32[128]{0:T(128)S(1)}, s32[128]{0:T(128)}, u32[]{:S(2)}) copy-start(s32[128]{0:T(128)} %reshape.154.tab) | copy-start | bytes 1540
  143.2 22.1 %copy-start.15 = (bf16[1280,256]{1,0:T(8,128)(2,1)S(1)}, bf16[1280,256]{1,0:T(8,128)(2,1)}, u32[]{:S(2)}) copy-start(bf16[1280,256]{1,0:T(8,128)(2,1)} %get-tuple-element.35.right) | copy-start | bytes 1966084
  146.0 16.0 %collective-permute-start.6 = (f32[2,2,128,128]{3,2,1,0:T(8,128)}, f32[2,2,128,128]{3,2,1,0:T(8,128)S(1)}, u32[]{:S(2)}, u32[]{:S(2)}) collective-permute-start(f32[2,2,128,128]{3,2,1,0:T(8,128)} %get-tuple-element.46), channel_id=1, source_target_pairs={{0,96},{32,0},{64,32},{96,64},{1,97},{33,1},{65,33},{97,65},{2,98}... | collective-permute-start | bytes 786440 | tf_op jit(solution)/shard_map/ppermute | solution.py:396
  150.2 11.8 %collective-permute-start.7 = (f32[2,2,128,128]{3,2,1,0:T(8,128)}, f32[2,2,128,128]{3,2,1,0:T(8,128)S(1)}, u32[]{:S(2)}, u32[]{:S(2)}) collective-permute-start(f32[2,2,128,128]{3,2,1,0:T(8,128)} %get-tuple-element.47), channel_id=1, source_target_pairs={{0,64},{32,96},{64,0},{96,32},{1,65},{33,97},{65,1},{97,33},{2,66}... | collective-permute-start | bytes 786440 | tf_op jit(solution)/shard_map/ppermute | solution.py:396
  150.2 15.1 %collective-permute-start.8 = (f32[2,2,128,128]{3,2,1,0:T(8,128)}, f32[2,2,128,128]{3,2,1,0:T(8,128)S(1)}, u32[]{:S(2)}, u32[]{:S(2)}) collective-permute-start(f32[2,2,128,128]{3,2,1,0:T(8,128)} %get-tuple-element.48), channel_id=1, source_target_pairs={{0,32},{32,64},{64,96},{96,0},{1,33},{33,65},{65,97},{97,1},{2,34}... | collective-permute-start | bytes 786440 | tf_op jit(solution)/shard_map/ppermute | solution.py:396
  165.3 1.6 copy-start.19
  202.9 58.8 %all-to-all-start.3 = ((f32[32,2,128,128]{3,2,1,0:T(8,128)}), f32[32,2,128,128]{3,2,1,0:T(8,128)}, u32[]{:S(2)}, u32[]{:S(2)}) async-start(f32[32,2,128,128]{3,2,1,0:T(8,128)} %get-tuple-element.51.rest_1_), calls=%async_computation.3 | async-start | bytes 8388608 | tf_op jit(solution)/shard_map/all_to_all | solution.py:393
  207.8 20.0 %copy-start.10 = (s32[128]{0:T(128)S(1)}, s32[128]{0:T(128)}, u32[]{:S(2)}) copy-start(s32[128]{0:T(128)} %reshape.154.tab) | copy-start | bytes 1540
  210.5 11.3 %collective-permute-start.10 = (f32[2,2,128,128]{3,2,1,0:T(8,128)}, f32[2,2,128,128]{3,2,1,0:T(8,128)S(1)}, u32[]{:S(2)}, u32[]{:S(2)}) collective-permute-start(f32[2,2,128,128]{3,2,1,0:T(8,128)} %get-tuple-element.54), channel_id=1, source_target_pairs={{0,64},{32,96},{64,0},{96,32},{1,65},{33,97},{65,1},{97,33},{2,66}... | collective-permute-start | bytes 786440 | tf_op jit(solution)/shard_map/ppermute | solution.py:396
  214.4 12.4 %collective-permute-start.11 = (f32[2,2,128,128]{3,2,1,0:T(8,128)}, f32[2,2,128,128]{3,2,1,0:T(8,128)S(1)}, u32[]{:S(2)}, u32[]{:S(2)}) collective-permute-start(f32[2,2,128,128]{3,2,1,0:T(8,128)} %get-tuple-element.55), channel_id=1, source_target_pairs={{0,32},{32,64},{64,96},{96,0},{1,33},{33,65},{65,97},{97,1},{2,34}... | collective-permute-start | bytes 786440 | tf_op jit(solution)/shard_map/ppermute | solution.py:396
  215.6 12.1 %collective-permute-start.9 = (f32[2,2,128,128]{3,2,1,0:T(8,128)}, f32[2,2,128,128]{3,2,1,0:T(8,128)S(1)}, u32[]{:S(2)}, u32[]{:S(2)}) collective-permute-start(f32[2,2,128,128]{3,2,1,0:T(8,128)} %get-tuple-element.53), channel_id=1, source_target_pairs={{0,96},{32,0},{64,32},{96,64},{1,97},{33,1},{65,33},{97,65},{2,98}... | collective-permute-start | bytes 786440 | tf_op jit(solution)/shard_map/ppermute | solution.py:396
  227.8 1.6 copy-start.17
  (9 other events, 11.2 us)

commit v3 on v2

v3 whole, which is shorter than its diff:
```python
import functools

import jax
import jax.numpy as jnp
from jax import lax
from jax.experimental import pallas as pl
from jax.experimental.pallas import tpu as pltpu
from jax.sharding import PartitionSpec as P

XCAP = 2
step_size = 0.1
f32, bf16 = jnp.float32, jnp.bfloat16
LIMIT = 24 << 20
WIDTH = 4
SCALARS = 11
HBM = pl.BlockSpec(memory_space=pltpu.HBM)
SMEM = pl.BlockSpec(memory_space=pltpu.SMEM)
VMEM = pl.BlockSpec(memory_space=pltpu.VMEM)


def split(value):
    high = value.astype(bf16)
    return high, (value - high.astype(f32)).astype(bf16)


def prepare_kernel(h_ref, v_ref, left_ref, right_ref, row_left_ref, row_right_ref):
    n = h_ref.shape[-1]

    def put(matrix, left, right, place):
        high, low = split(matrix)
        start = place * 2 * n
        for half in range(2):
            cols = slice(start + half * n, start + (half + 1) * n)
            left[0:n, cols] = high
            left[n : 2 * n, cols] = low
            right[cols, 0:n] = high
            right[cols, n : 2 * n] = low

    terms = [h_ref[1], h_ref[0], v_ref[0], v_ref[1], v_ref[3]]
    for place, matrix in enumerate(terms):
        put(matrix, left_ref, right_ref, place)
    put(v_ref[2], row_left_ref, row_right_ref, 0)


def sandwich(terms, left, right):
    n = terms[0][0][0].shape[-1]
    columns, rows = [], []
    for (la, lb), (ra, rb) in terms:
        columns += [jnp.concatenate(pair, axis=1) for pair in zip(split(la), split(lb))]
        rows += [jnp.concatenate(pair, axis=0) for pair in zip(split(ra), split(rb))]
    stacked = jnp.concatenate(columns, axis=0)
    beside = jnp.concatenate(rows, axis=1)
    ahead = jnp.dot(left, stacked, preferred_element_type=f32)
    behind = jnp.dot(beside, right, preferred_element_type=f32)
    ahead = ahead[0:n] + ahead[n:]
    behind = behind[:, 0:n] + behind[:, n:]
    return ahead[:, 0:n] - behind[0:n], ahead[:, n:] - behind[n:]


def bath_term(ur, ui, lr, li, wr, wi):
    arr, ari, air, aii = wr * lr, wi * lr, wr * li, wi * li
    real, imag = ur + arr, ui + air
    return ((imag + ari, aii - real), (imag - ari, -real - aii))


def first_slot(tab, g):
    up, low = tab[g * 8], tab[g * 8 + 1]
    return jnp.where(up >= 0, up, low)


def when_copy(live, source, target, sem, go):
    @pl.when(live)
    def _():
        copy = pltpu.make_async_copy(source, target, sem)
        copy.start() if go else copy.wait()


def send_slots(tab, g, buf, row_out, sem_u, sem_l, go):
    for k, sem in ((0, sem_u), (1, sem_l)):
        slot = tab[g * 8 + k]
        when_copy(slot >= 0, buf.at[g], row_out.at[jnp.maximum(slot, 0)], sem.at[g], go)


def local_kernel(tab, wts, z_ref, c1, c2, c3, left, right, *rest, with_sum, last_scale):
    count = z_ref.shape[0]
    if with_sum:
        acc_ref, *rest = rest
    last = last_scale is not None
    keep_sum = with_sum and not last
    out_ref, *rest = rest
    if not last:
        row_out, *rest = rest
    if keep_sum:
        sum_ref, *rest = rest
    cbuf, sems, sem_u, sem_l = rest

    copies = [
        pltpu.make_async_copy(c, cbuf.at[pl.ds(XCAP * k, XCAP)], sems.at[k])
        for k, c in enumerate((c1, c2, c3))
    ]
    for copy in copies:
        copy.start()
    for copy in copies:
        copy.wait()

    def one(g):
        yr, yi = z_ref[g, 0], z_ref[g, 1]
        terms = [((yr, yi), (yr, yi)), ((yi, -yr), (yi, -yr))]
        for k, (ref, bath) in enumerate(((z_ref, 0), (z_ref, 1), (cbuf, 3))):
            up, low = tab[g * 8 + 2 + 2 * k], tab[g * 8 + 3 + 2 * k]
            u, l = jnp.maximum(up, 0), jnp.maximum(low, 0)
            ur, ui = (jnp.where(up >= 0, ref[u, part], 0.0) for part in range(2))
            lr, li = (jnp.where(low >= 0, ref[l, part], 0.0) for part in range(2))
            wr, wi = wts[g * SCALARS + 2 * bath], wts[g * SCALARS + 2 * bath + 1]
            terms.append(bath_term(ur, ui, lr, li, wr, wi))
        out_r, out_i = sandwich(terms, left[...], right[...])
        damp = wts[g * SCALARS + 8]
        out_r, out_i = out_r - damp * yr, out_i - damp * yi
        if with_sum:
            sum_r, sum_i = acc_ref[g, 0] + yr, acc_ref[g, 1] + yi
        if last_scale is not None:
            out_r, out_i = sum_r + last_scale * out_r, sum_i + last_scale * out_i
        out_ref[g, 0], out_ref[g, 1] = out_r, out_i
        if keep_sum:
            sum_ref[g, 0], sum_ref[g, 1] = sum_r, sum_i

    width = 2

    @pl.loop(0, count // width)
    def _(step):
        for k in range(width):
            one(step * width + k)
        if not last:
            for k in range(width):
                send_slots(tab, step * width + k, out_ref, row_out, sem_u, sem_l, True)

    if not last:

        @pl.loop(0, count)
        def _(g):
            send_slots(tab, g, out_ref, row_out, sem_u, sem_l, False)


def in_hbm(*arrays):
    return [pltpu.with_memory_space_constraint(a, pltpu.HBM) for a in arrays]


def local_part(tab, wts, z, cols, left, right, acc, slots, last_scale):
    count, _, n, _ = z.shape
    with_sum, last = acc is not None, last_scale is not None
    outs, places = [jax.ShapeDtypeStruct(z.shape, f32)], [VMEM]
    if not last:
        outs, places = outs + [pltpu.HBM((slots, 2, n, n), f32)], places + [HBM]
    if with_sum and not last:
        outs, places = outs + [jax.ShapeDtypeStruct(z.shape, f32)], places + [VMEM]
    return pl.pallas_call(
        functools.partial(local_kernel, with_sum=with_sum, last_scale=last_scale),
        out_shape=outs,
        in_specs=[SMEM, SMEM, VMEM, HBM, HBM, HBM, VMEM, VMEM] + [VMEM] * with_sum,
        out_specs=places,
        scratch_shapes=[
            pltpu.VMEM((3 * XCAP, 2, n, n), f32),
            pltpu.SemaphoreType.DMA((3,)),
            pltpu.SemaphoreType.DMA((count,)),
            pltpu.SemaphoreType.DMA((count,)),
        ],
        compiler_params=pltpu.CompilerParams(vmem_limit_bytes=LIMIT),
        cost_estimate=pl.CostEstimate(
            flops=count * 160 * n * n * n, bytes_accessed=8 << 20, transcendentals=0
        ),
        name="local_part",
    )(tab, wts, z, *cols, left, right, *([acc] if with_sum else []))


def pack_columns_kernel(ctab, z_ref, o1, o2, o3, buf, sem):
    outs = (o1, o2, o3)
    slots = len(outs) * XCAP
    for go in (True, False):
        for k in range(slots):
            g = ctab[k]
            when_copy(g >= 0, z_ref.at[jnp.maximum(g, 0)], buf.at[k], sem.at[k], go)
    for go in (True, False):
        for k in range(slots):
            when_copy(ctab[k] >= 0, buf.at[k], outs[k // XCAP].at[k % XCAP], sem.at[k], go)


def pack_columns(ctab, z):
    count, _, n, _ = z.shape
    return pl.pallas_call(
        pack_columns_kernel,
        out_shape=[pltpu.HBM((XCAP, 2, n, n), f32)] * 3,
        in_specs=[SMEM, HBM],
        out_specs=[HBM] * 3,
        scratch_shapes=[
            pltpu.VMEM((3 * XCAP, 2, n, n), f32),
            pltpu.SemaphoreType.DMA((3 * XCAP,)),
        ],
        cost_estimate=pl.CostEstimate(flops=0, bytes_accessed=1 << 20, transcendentals=0),
        name="pack_columns",
    )(ctab, *in_hbm(z))


def pack_rows_kernel(up_ref, low_ref, z_ref, row_out, buf, sem_in, sem_u, sem_l, *, missing, bath):
    count, along_y = z_ref.shape[0], row_out.shape[0]
    links = ((up_ref, sem_u), (low_ref, sem_l))

    def load(g, go):
        linked = (up_ref[bath, g] < missing) | (low_ref[bath, g] < missing)
        when_copy(linked, z_ref.at[g], buf.at[g], sem_in.at[g], go)

    def send(g, go):
        for ref, sem in links:
            target = ref[bath, g]
            slot = lax.rem(lax.div(target, count), along_y)
            when_copy(target < missing, buf.at[g], row_out.at[slot], sem.at[g], go)

    @pl.loop(0, count)
    def _(g):
        load(g, True)

    @pl.loop(0, count)
    def _(g):
        load(g, False)
        send(g, True)

    @pl.loop(0, count)
    def _(g):
        send(g, False)


def product(left, right, values, reals, imags):
    n = values[0][0].shape[-1]
    ahead, beside = [], []
    for xr, xi in values:
        (hr, tr), (hi, ti) = split(xr), split(xi)
        high, tail = jnp.concatenate([hr, hi], 1), jnp.concatenate([tr, ti], 1)
        rows = jnp.dot(left, jnp.concatenate([high, tail], 0), preferred_element_type=f32)
        ahead.append(rows[0:n] + rows[n:])
        beside.append(jnp.concatenate([hr, tr], 1))
        beside.append(jnp.concatenate([hi, ti], 1))
    behind = jnp.dot(jnp.concatenate(beside, 0), right, preferred_element_type=f32)
    behind = behind[:, 0:n] + behind[:, n:]
    results = []
    for k, (real, imag) in enumerate(zip(reals, imags)):
        ar, ai = ahead[k][:, 0:n], ahead[k][:, n:]
        br, bi = (behind[(2 * k + p) * n : (2 * k + p + 1) * n] for p in range(2))
        results.append((real * (ai - bi) + imag * (ar + br), imag * (ai + bi) - real * (ar - br)))
    return results


def weights(wts, g, above):
    nr, ni = wts[g * SCALARS + 4], wts[g * SCALARS + 5]
    cr, ci = wts[g * SCALARS + 9], wts[g * SCALARS + 10]
    here = jnp.where(above, 1.0, nr), jnp.where(above, 0.0, ni)
    there = jnp.where(above, nr + cr, 1.0), jnp.where(above, ni + ci, 0.0)
    return here, there


def two_links(tab, g):
    return (tab[g * 8] >= 0) & (tab[g * 8 + 1] >= 0)


def fix_kernel(tab, wts, recv, part, slots_in, left, right, *rest, back):
    del slots_in
    if back is not None:
        prev, *rest = rest
    slots_out, token, rbuf, wbuf, pbuf, obuf, sem = rest
    count = part.shape[0]
    token[0] = 0

    @pl.loop(0, count)
    def _(g):
        @pl.when(two_links(tab, g))
        def _():
            slots = [jnp.maximum(tab[g * 8 + k], 0) for k in range(2)]
            copies = [
                pltpu.make_async_copy(recv.at[slots[k]], rbuf.at[k], sem.at[k]) for k in range(2)
            ]
            copies.append(pltpu.make_async_copy(part.at[g], pbuf, sem.at[2]))
            if back is not None:
                copies.append(pltpu.make_async_copy(prev.at[g], wbuf, sem.at[3]))
            for copy in copies:
                copy.start()
            for copy in copies:
                copy.wait()
            for k, above in enumerate((True, False)):
                here, there = weights(wts, g, above)
                x = rbuf[k, 0], rbuf[k, 1]
                if back is not None:
                    own = wbuf[0], wbuf[1]
                    (term,) = product(left[...], right[...], [own], there[:1], there[1:])
                    x = back * (x[0] + term[0]), back * (x[1] + term[1])
                (term,) = product(left[...], right[...], [x], here[:1], here[1:])
                for p in range(2):
                    obuf[1 - k, p] = pbuf[p] + term[p]
            copies = [
                pltpu.make_async_copy(obuf.at[k], slots_out.at[slots[k]], sem.at[4 + k])
                for k in range(2)
            ]
            for copy in copies:
                copy.start()
            for copy in copies:
                copy.wait()


def fix_slots(tab, wts, recv, part, slots, prev, left, right, back):
    count, _, n, _ = part.shape
    olds = [] if back is None else in_hbm(prev)
    return pl.pallas_call(
        functools.partial(fix_kernel, back=back),
        out_shape=[pltpu.HBM(slots.shape, f32), jax.ShapeDtypeStruct((1,), jnp.int32)],
        in_specs=[SMEM, SMEM, HBM, HBM, HBM, VMEM, VMEM] + [HBM] * len(olds),
        out_specs=[HBM, SMEM],
        scratch_shapes=[
            pltpu.VMEM((2, 2, n, n), f32),
            pltpu.VMEM((2, n, n), f32),
            pltpu.VMEM((2, n, n), f32),
            pltpu.VMEM((2, 2, n, n), f32),
            pltpu.SemaphoreType.DMA((6,)),
        ],
        input_output_aliases={4: 0},
        compiler_params=pltpu.CompilerParams(vmem_limit_bytes=LIMIT),
        cost_estimate=pl.CostEstimate(flops=0, bytes_accessed=1 << 10, transcendentals=0),
        name="fix_slots",
    )(tab, wts, *in_hbm(recv, part, slots), left, right, *olds)


def row_kernel(tab, wts, token, recv, part, left, right, *rest, scale, back, last):
    del token
    count, _, n, _ = part.shape
    if back is not None:
        prev, *rest = rest
    z_out, xbuf, ybuf, wbuf, zbuf, sem_x, sem_y, sem_w, sem_g, sem_z = rest

    def fetch(g, go):
        slot, low = first_slot(tab, g), tab[g * 8 + 1]
        when_copy(slot >= 0, recv.at[jnp.maximum(slot, 0)], xbuf.at[g], sem_x.at[g], go)
        when_copy(two_links(tab, g), recv.at[jnp.maximum(low, 0)], ybuf.at[g], sem_y.at[g], go)
        if go:

            @pl.when(slot < 0)
            def _():
                xbuf[g] = jnp.zeros_like(xbuf[g])

    def fetch_own(step, go):
        group = pl.ds(step * WIDTH, WIDTH)
        copies = [pltpu.make_async_copy(part.at[group], zbuf.at[group], sem_g.at[step])]
        if back is not None:
            copies.append(pltpu.make_async_copy(prev.at[group], wbuf.at[group], sem_w.at[step]))
        for copy in copies:
            copy.start() if go else copy.wait()

    def keep(step):
        group = pl.ds(step * WIDTH, WIDTH)
        return pltpu.make_async_copy(zbuf.at[group], z_out.at[group], sem_z.at[step])

    @pl.loop(0, count // WIDTH)
    def _(step):
        for k in range(WIDTH):
            fetch(step * WIDTH + k, True)
        fetch_own(step, True)

    def linked(group, buf, above):
        both = [weights(wts, g, a) for g, a in zip(group, above)]
        values = [(buf[g, 0], buf[g, 1]) for g in group]
        if back is not None:
            own = [(wbuf[g, 0], wbuf[g, 1]) for g in group]
            terms = product(
                left[...], right[...], own, [b[1][0] for b in both], [b[1][1] for b in both]
            )
            values = [
                tuple(back * (v + t) for v, t in zip(value, term))
                for value, term in zip(values, terms)
            ]
        return product(
            left[...], right[...], values, [b[0][0] for b in both], [b[0][1] for b in both]
        )

    @pl.loop(0, count // WIDTH)
    def _(step):
        group = [step * WIDTH + k for k in range(WIDTH)]
        for g in group:
            fetch(g, False)
        fetch_own(step, False)
        above = [tab[g * 8] >= 0 for g in group]
        for g, term in zip(group, linked(group, xbuf, above)):
            for p in range(2):
                if last:
                    zbuf[g, p] = zbuf[g, p] + scale * term[p]
                else:
                    zbuf[g, p] = scale * (zbuf[g, p] + term[p])
        for g in group:

            @pl.when(two_links(tab, g))
            def _():
                (term,) = linked([g], ybuf, [False])
                for p in range(2):
                    zbuf[g, p] = zbuf[g, p] + scale * term[p]

        keep(step).start()

    @pl.loop(0, count // WIDTH)
    def _(step):
        keep(step).wait()


def row_part(tab, wts, token, recv, part, prev, left, right, scale, back, last):
    count, _, n, _ = part.shape
    out = jax.ShapeDtypeStruct(part.shape, f32) if last else pltpu.HBM(part.shape, f32)
    olds = [] if back is None else in_hbm(prev)
    return pl.pallas_call(
        functools.partial(row_kernel, scale=scale, back=back, last=last),
        out_shape=out,
        in_specs=[SMEM, SMEM, SMEM, HBM, HBM, VMEM, VMEM] + [HBM] * len(olds),
        out_specs=HBM,
        scratch_shapes=[pltpu.VMEM((count, 2, n, n), f32)] * 4
        + [pltpu.SemaphoreType.DMA((count,))] * 5,
        compiler_params=pltpu.CompilerParams(vmem_limit_bytes=LIMIT),
        cost_estimate=pl.CostEstimate(
            flops=count * 64 * n * n * n, bytes_accessed=10 << 20, transcendentals=0
        ),
        name="row_part",
    )(tab, wts, token, *in_hbm(recv, part), left, right, *olds)


def local(
    densities, hamiltonian, couplings, decay_rates, correlation, upper_link, lower_link, occupation
):
    count, _, n, _ = densities.shape
    along_y, along_x = lax.axis_size("gy"), lax.axis_size("gx")
    index_x, index_y = lax.axis_index("gx"), lax.axis_index("gy")
    own = index_x * along_y + index_y
    missing = count * along_y * along_x

    row_send = pl.pallas_call(
        functools.partial(pack_rows_kernel, missing=missing, bath=2),
        out_shape=pltpu.HBM((along_y, 2, n, n), f32),
        in_specs=[SMEM, SMEM, HBM],
        out_specs=HBM,
        scratch_shapes=[pltpu.VMEM((count, 2, n, n), f32)]
        + [pltpu.SemaphoreType.DMA((count,))] * 3,
        name="pack_rows",
    )(upper_link.T, lower_link.T, densities)

    links = jnp.stack([upper_link, lower_link], axis=2)
    live = links < missing
    near = jnp.where(live[:, 0:2], links[:, 0:2] - own * count, -1).reshape(count, 4)
    rows = jnp.where(live[:, 2], (links[:, 2] // count) % along_y, -1)

    targets, usable = links[:, 3].reshape(-1), live[:, 3].reshape(-1)
    sources = jnp.repeat(jnp.arange(count, dtype=jnp.int32), 2)
    relative = (targets // count // along_y - index_x) % along_x
    same = usable[:, None] & usable[None, :] & (relative[:, None] == relative[None, :])
    start = (relative - 1) * XCAP
    recv_slot = start + jnp.any(same & (targets[None, :] < targets[:, None]), axis=1)
    send_slot = start + jnp.any(same & (sources[None, :] < sources[:, None]), axis=1)
    recv_slot = jnp.where(usable, recv_slot, -1).reshape(count, 2)
    hit = (send_slot[None, :] == jnp.arange(6, dtype=jnp.int32)[:, None]) & usable[None, :]
    ctab = jnp.max(jnp.where(hit, sources[None, :], -1), axis=1)
    tab = jnp.concatenate([rows, near, recv_slot], axis=1).reshape(-1).astype(jnp.int32)

    level = occupation.astype(f32)
    damping = jnp.sum(level * decay_rates[None, :], axis=1, keepdims=True)
    pairs = (level[:, :, None] * correlation.T[None, :, :]).reshape(count, 8)
    third = jnp.broadcast_to(correlation[:, 2][None, :], (count, 2))
    wts = jnp.concatenate([pairs, damping, third], axis=1).reshape(-1)

    mats = lambda rows, cols: jax.ShapeDtypeStruct((rows, cols), bf16)
    left, right, row_left, row_right = pl.pallas_call(
        prepare_kernel,
        out_shape=[mats(2 * n, 10 * n), mats(10 * n, 2 * n), mats(2 * n, 2 * n), mats(2 * n, 2 * n)],
        in_specs=[VMEM, VMEM],
        out_specs=[VMEM] * 4,
        name="prepare",
    )(hamiltonian, couplings)

    exchange = lambda a: lax.all_to_all(a, "gy", split_axis=0, concat_axis=0, tiled=True)
    states, acc, parts = [densities], None, None
    token = jnp.zeros((1,), jnp.int32)
    recv = exchange(row_send)
    for level in range(4):
        z, last = states[level], level == 3
        col_send = pack_columns(ctab, z)
        arrived = [
            lax.ppermute(col_send[s - 1], "gx", [(x, (x + s) % along_x) for x in range(along_x)])
            for s in range(1, along_x)
        ]
        scale = step_size / (level + 1)
        parts = local_part(
            tab, wts, z, arrived[::-1], left, right, acc, along_y, scale if last else None
        )
        acc = densities if level == 0 else None if last else parts[2]
        back = step_size / level if level else None
        prev = states[level - 1] if level else None
        mats = (row_left, row_right)
        if not last:
            slots, token = fix_slots(tab, wts, recv, parts[0], parts[1], prev, *mats, back)
            following = exchange(slots)
        new = row_part(tab, wts, token, recv, parts[0], prev, *mats, scale, back, last)
        if last:
            return new
        states.append(new)
        recv = following


def solution(mesh):
    return jax.shard_map(
        local,
        mesh=mesh,
        in_specs=(
            P(("gx", "gy"), None, None, None),
            P(),
            P(),
            P(),
            P(),
            P(("gx", "gy"), None),
            P(("gx", "gy"), None),
            P(("gx", "gy"), None),
        ),
        out_specs=P(("gx", "gy"), None, None, None),
        check_vma=False,
    )
```

time: 268 us -> 255 us (0.951)
  waiting for transfers between devices: 124 us -> 102 us
  Pallas kernels: 77.6 us -> 84.9 us
    all_to_all x4, waiting for transfers between devices: 74.6 us -> 50.3 us  [local(): lax.all_to_all(a, 'gy', split_axis=0, concat_axis=0, tiled=True)]
    pallas_call x12 -> x15, Pallas kernels: 71.6 us -> 79.1 us  [the longest x4 34.7 us: local_part(): pl.pallas_call(functools.partial(local_kernel, with_sum=with_sum, last_sc...]
    unnamed x52 -> x48, local copies, waits for them, and re-layouts: 17.1 us -> 19.2 us
  transfers between devices with their start and end apart: 16 -> 16, of which waited for: 13 -> 12; matrix products, arithmetic and copies ran while one was open for 1% -> 1% of each run, Pallas kernels for 19% -> 27%
where the time goes in v3:
time: 255 us; the launch traced here: 254 us
  waiting for transfers between devices  102 us (40%)
  Pallas kernels  84.9 us (33%)
  starting transfers between devices  44.5 us (17%)
  local copies, waits for them, and re-layouts  20.6 us (8%)
    ppermute x12, waiting for transfers between devices, local(): lax.ppermute(col_send[s - 1], 'gx', [(x, (x + s) % along_x) for x in rang...  51.8 us
    all_to_all x4, waiting for transfers between devices, local(): lax.all_to_all(a, 'gy', split_axis=0, concat_axis=0, tiled=True)  50.3 us
    pallas_call x4, Pallas kernels, local_part(): pl.pallas_call(functools.partial(local_kernel, with_sum=with_sum, last_sc...  34.7 us
    pallas_call x4, Pallas kernels, row_part(): pl.pallas_call(functools.partial(row_kernel, scale=scale, back=back, last...  29.9 us
    all_to_all x4, starting transfers between devices, local(): lax.all_to_all(a, 'gy', split_axis=0, concat_axis=0, tiled=True)  22.3 us
    ppermute x12, starting transfers between devices, local(): lax.ppermute(col_send[s - 1], 'gx', [(x, (x + s) % along_x) for x in rang...  22.2 us
    unnamed x48, local copies, waits for them, and re-layouts  19.2 us
    pallas_call x4, Pallas kernels, pack_columns(): pl.pallas_call(pack_columns_kernel, out_shape=[pltpu.HBM((XCAP, 2, n, n),...  10.4 us
  transfers between devices with their start and end apart: 16, of which 12 were waited for; matrix products, arithmetic and copies ran while one was open for 1% of the time, Pallas kernels for 27%

profile of v3, /device:TPU:0, one launch (start us, length us, event | category | flops | bytes accessed | tf_op | source)
XLA Modules:
  0.0 253.8 jit_solution(8538230545656723028)
XLA Ops:
  0.0 3.4 %pack_rows.1 = f32[32,2,128,128]{3,2,1,0:T(8,128)} custom-call(s32[4,16]{1,0:T(4,128)} %bitcast.22, s32[4,16]{1,0:T(4,128)} %bitcast.18, f32[16,2,128,128]{3,2,1,0:T(8,128)} %rest_0_.5), custom_call_target="tpu_custom_call" | custom-call | tf_op jit(solution)/shard_map/pack_rows/pallas_call | solution.py:435
  3.5 7.7 %all-to-all-start = ((f32[32,2,128,128]{3,2,1,0:T(8,128)}), f32[32,2,128,128]{3,2,1,0:T(8,128)}, u32[]{:S(2)}, u32[]{:S(2)}) async-start(f32[32,2,128,128]{3,2,1,0:T(8,128)} %pack_rows.1), calls=%async_computation | async-start | bytes 8388608 | tf_op jit(solution)/shard_map/all_to_all | solution.py:477
  12.6 2.6 %pack_columns.4 = (f32[2,2,128,128]{3,2,1,0:T(8,128)}, f32[2,2,128,128]{3,2,1,0:T(8,128)}, f32[2,2,128,128]{3,2,1,0:T(8,128)}) custom-call(s32[6]{0:T(128)} %select_reduce_fusion.ctab, f32[16,2,128,128]{3,2,1,0:T(8,128)} %rest_0_.5), custom_call_target="tpu_custom_call" | custom-call | bytes 1048576 | tf_op jit(solution)/shard_map/pack_columns/pallas_call | solution.py:189
  15.2 4.2 %collective-permute-start = (f32[2,2,128,128]{3,2,1,0:T(8,128)}, f32[2,2,128,128]{3,2,1,0:T(8,128)S(1)}, u32[]{:S(2)}, u32[]{:S(2)}) collective-permute-start(f32[2,2,128,128]{3,2,1,0:T(8,128)} %get-tuple-element.35), channel_id=1, source_target_pairs={{0,96},{32,0},{64,32},{96,64},{1,97},{33,1},{65,33},{97,65},{2,98}... | collective-permute-start | bytes 786440 | tf_op jit(solution)/shard_map/ppermute | solution.py:485
  24.3 7.0 %collective-permute-done.c1 = f32[2,2,128,128]{3,2,1,0:T(8,128)S(1)} collective-permute-done((f32[2,2,128,128]{3,2,1,0:T(8,128)}, f32[2,2,128,128]{3,2,1,0:T(8,128)S(1)}, u32[]{:S(2)}, u32[]{:S(2)}) %collective-permute-start) | collective-permute-done | bytes 262176 | tf_op jit(solution)/shard_map/ppermute | solution.py:485
  31.3 3.3 %collective-permute-done.2.c3 = f32[2,2,128,128]{3,2,1,0:T(8,128)S(1)} collective-permute-done((f32[2,2,128,128]{3,2,1,0:T(8,128)}, f32[2,2,128,128]{3,2,1,0:T(8,128)S(1)}, u32[]{:S(2)}, u32[]{:S(2)}) %collective-permute-start.2) | collective-permute-done | bytes 262176 | tf_op jit(solution)/shard_map/ppermute | solution.py:485
  36.8 8.5 %local_part.4 = (f32[16,2,128,128]{3,2,1,0:T(8,128)S(1)}, f32[32,2,128,128]{3,2,1,0:T(8,128)}) custom-call(s32[128]{0:T(128)S(1)} %reshape.155.tab, f32[176]{0:T(256)S(1)} %reshape.156.wts, f32[16,2,128,128]{3,2,1,0:T(8,128)S(1)} %copy-done.1, f32[2,2,128,128]{3,2,1,0:T(8,128)S(1)} %collective-permute-done.c1, ...), custom_call_target="tpu_custom_call" | custom-call | flops 5368709120 | bytes 8388608 | tf_op jit(solution)/shard_map/local_part/pallas_call | solution.py:156
  46.6 18.5 %all-to-all-done.recv = f32[32,2,128,128]{3,2,1,0:T(8,128)} async-done(((f32[32,2,128,128]{3,2,1,0:T(8,128)}), f32[32,2,128,128]{3,2,1,0:T(8,128)}, u32[]{:S(2)}, u32[]{:S(2)}) %all-to-all-start) | async-done | bytes 4194336 | tf_op jit(solution)/shard_map/all_to_all | solution.py:477
  66.5 4.9 %all-to-all-start.1 = ((f32[32,2,128,128]{3,2,1,0:T(8,128)}), f32[32,2,128,128]{3,2,1,0:T(8,128)}, u32[]{:S(2)}, u32[]{:S(2)}) async-start(f32[32,2,128,128]{3,2,1,0:T(8,128)} %get-tuple-element.44), calls=%async_computation.1 | async-start | bytes 8388608 | tf_op jit(solution)/shard_map/all_to_all | solution.py:477
  71.4 6.2 %row_part.4.z_ref.rest_0_ = f32[16,2,128,128]{3,2,1,0:T(8,128)} custom-call(s32[128]{0:T(128)S(1)} %reshape.155.tab, f32[176]{0:T(256)S(1)} %reshape.156.wts, s32[1]{0:T(128)} %get-tuple-element.45.token, f32[32,2,128,128]{3,2,1,0:T(8,128)} %all-to-all-done.recv, f32[16,2,128,128]{3,2,1,0:T(8,128)} %copy-done.3, bf16[256,256]{1,0:T(8,128)(2,1)S(1)} %copy-done.7, ...), custom_call_target="tpu_custom_call" | custom-call | flops 2147483648 | bytes 10485760 | tf_op jit(solution)/shard_map/row_part/pallas_call | solution.py:411
  80.1 4.3 %collective-permute-start.3 = (f32[2,2,128,128]{3,2,1,0:T(8,128)}, f32[2,2,128,128]{3,2,1,0:T(8,128)S(1)}, u32[]{:S(2)}, u32[]{:S(2)}) collective-permute-start(f32[2,2,128,128]{3,2,1,0:T(8,128)} %get-tuple-element.46), channel_id=1, source_target_pairs={{0,96},{32,0},{64,32},{96,64},{1,97},{33,1},{65,33},{97,65},{2,98}... | collective-permute-start | bytes 786440 | tf_op jit(solution)/shard_map/ppermute | solution.py:485
  85.7 10.5 %collective-permute-done.3.c1 = f32[2,2,128,128]{3,2,1,0:T(8,128)S(1)} collective-permute-done((f32[2,2,128,128]{3,2,1,0:T(8,128)}, f32[2,2,128,128]{3,2,1,0:T(8,128)S(1)}, u32[]{:S(2)}, u32[]{:S(2)}) %collective-permute-start.3) | collective-permute-done | bytes 262176 | tf_op jit(solution)/shard_map/ppermute | solution.py:485
  96.2 3.3 %collective-permute-done.5.c3 = f32[2,2,128,128]{3,2,1,0:T(8,128)S(1)} collective-permute-done((f32[2,2,128,128]{3,2,1,0:T(8,128)}, f32[2,2,128,128]{3,2,1,0:T(8,128)S(1)}, u32[]{:S(2)}, u32[]{:S(2)}) %collective-permute-start.5) | collective-permute-done | bytes 262176 | tf_op jit(solution)/shard_map/ppermute | solution.py:485
  102.2 9.0 %local_part.5 = (f32[16,2,128,128]{3,2,1,0:T(8,128)S(1)}, f32[32,2,128,128]{3,2,1,0:T(8,128)}, f32[16,2,128,128]{3,2,1,0:T(8,128)S(1)}) custom-call(s32[128]{0:T(128)S(1)} %reshape.155.tab, f32[176]{0:T(256)S(1)} %reshape.156.wts, f32[16,2,128,128]{3,2,1,0:T(8,128)S(1)} %copy-done, f32[2,2,128,128]{3,2,1,0:T(8,128)S(1)} %collective-permute-done.3.c1, ...), custom_call_target="tpu_custom_call" | custom-call | flops 5368709120 | bytes 8388608 | tf_op jit(solution)/shard_map/local_part/pallas_call | solution.py:156
  113.9 11.4 %all-to-all-done.1.recv = f32[32,2,128,128]{3,2,1,0:T(8,128)} async-done(((f32[32,2,128,128]{3,2,1,0:T(8,128)}), f32[32,2,128,128]{3,2,1,0:T(8,128)}, u32[]{:S(2)}, u32[]{:S(2)}) %all-to-all-start.1) | async-done | bytes 4194336 | tf_op jit(solution)/shard_map/all_to_all | solution.py:477
  126.7 4.9 %all-to-all-start.2 = ((f32[32,2,128,128]{3,2,1,0:T(8,128)}), f32[32,2,128,128]{3,2,1,0:T(8,128)}, u32[]{:S(2)}, u32[]{:S(2)}) async-start(f32[32,2,128,128]{3,2,1,0:T(8,128)} %get-tuple-element.51), calls=%async_computation.2 | async-start | bytes 8388608 | tf_op jit(solution)/shard_map/all_to_all | solution.py:477
  131.6 7.9 %row_part.5.z_ref.rest_0_ = f32[16,2,128,128]{3,2,1,0:T(8,128)} custom-call(s32[128]{0:T(128)S(1)} %reshape.155.tab, f32[176]{0:T(256)S(1)} %reshape.156.wts, s32[1]{0:T(128)} %get-tuple-element.52.token, f32[32,2,128,128]{3,2,1,0:T(8,128)} %all-to-all-done.1.recv, f32[16,2,128,128]{3,2,1,0:T(8,128)} %copy-done.6, bf16[256,256]{1,0:T(8,128)(2,1)S(1)} %copy-done.7, ...), custom_call_target="tpu_custom_call" | custom-call | flops 2147483648 | bytes 10485760 | tf_op jit(solution)/shard_map/row_part/pallas_call | solution.py:411
  139.5 2.6 %pack_columns.6 = (f32[2,2,128,128]{3,2,1,0:T(8,128)}, f32[2,2,128,128]{3,2,1,0:T(8,128)}, f32[2,2,128,128]{3,2,1,0:T(8,128)}) custom-call(s32[6]{0:T(128)} %select_reduce_fusion.ctab, f32[16,2,128,128]{3,2,1,0:T(8,128)} %row_part.5.z_ref.rest_0_), custom_call_target="tpu_custom_call" | custom-call | bytes 1048576 | tf_op jit(solution)/shard_map/pack_columns/pallas_call | solution.py:189
  142.1 4.3 %collective-permute-start.6 = (f32[2,2,128,128]{3,2,1,0:T(8,128)}, f32[2,2,128,128]{3,2,1,0:T(8,128)S(1)}, u32[]{:S(2)}, u32[]{:S(2)}) collective-permute-start(f32[2,2,128,128]{3,2,1,0:T(8,128)} %get-tuple-element.53), channel_id=1, source_target_pairs={{0,96},{32,0},{64,32},{96,64},{1,97},{33,1},{65,33},{97,65},{2,98}... | collective-permute-start | bytes 786440 | tf_op jit(solution)/shard_map/ppermute | solution.py:485
  147.7 10.5 %collective-permute-done.6.c1 = f32[2,2,128,128]{3,2,1,0:T(8,128)S(1)} collective-permute-done((f32[2,2,128,128]{3,2,1,0:T(8,128)}, f32[2,2,128,128]{3,2,1,0:T(8,128)S(1)}, u32[]{:S(2)}, u32[]{:S(2)}) %collective-permute-start.6) | collective-permute-done | bytes 262176 | tf_op jit(solution)/shard_map/ppermute | solution.py:485
  158.2 3.3 %collective-permute-done.8.c3 = f32[2,2,128,128]{3,2,1,0:T(8,128)S(1)} collective-permute-done((f32[2,2,128,128]{3,2,1,0:T(8,128)}, f32[2,2,128,128]{3,2,1,0:T(8,128)S(1)}, u32[]{:S(2)}, u32[]{:S(2)}) %collective-permute-start.8) | collective-permute-done | bytes 262176 | tf_op jit(solution)/shard_map/ppermute | solution.py:485
  164.7 9.0 %local_part.6 = (f32[16,2,128,128]{3,2,1,0:T(8,128)S(1)}, f32[32,2,128,128]{3,2,1,0:T(8,128)}, f32[16,2,128,128]{3,2,1,0:T(8,128)S(1)}) custom-call(s32[128]{0:T(128)S(1)} %reshape.155.tab, f32[176]{0:T(256)S(1)} %reshape.156.wts, f32[16,2,128,128]{3,2,1,0:T(8,128)S(1)} %copy-done.2, f32[2,2,128,128]{3,2,1,0:T(8,128)S(1)} %collective-permute-done.6.c1, ...), custom_call_target="tpu_custom_call" | custom-call | flops 5368709120 | bytes 8388608 | tf_op jit(solution)/shard_map/local_part/pallas_call | solution.py:156
  176.4 9.2 %all-to-all-done.2.recv = f32[32,2,128,128]{3,2,1,0:T(8,128)} async-done(((f32[32,2,128,128]{3,2,1,0:T(8,128)}), f32[32,2,128,128]{3,2,1,0:T(8,128)}, u32[]{:S(2)}, u32[]{:S(2)}) %all-to-all-start.2) | async-done | bytes 4194336 | tf_op jit(solution)/shard_map/all_to_all | solution.py:477
  186.9 4.9 %all-to-all-start.3 = ((f32[32,2,128,128]{3,2,1,0:T(8,128)}), f32[32,2,128,128]{3,2,1,0:T(8,128)}, u32[]{:S(2)}, u32[]{:S(2)}) async-start(f32[32,2,128,128]{3,2,1,0:T(8,128)} %get-tuple-element.60), calls=%async_computation.3 | async-start | bytes 8388608 | tf_op jit(solution)/shard_map/all_to_all | solution.py:477
  191.8 7.9 %row_part.6.z_ref = f32[16,2,128,128]{3,2,1,0:T(8,128)} custom-call(s32[128]{0:T(128)S(1)} %reshape.155.tab, f32[176]{0:T(256)S(1)} %reshape.156.wts, s32[1]{0:T(128)} %get-tuple-element.59.token, f32[32,2,128,128]{3,2,1,0:T(8,128)} %all-to-all-done.2.recv, f32[16,2,128,128]{3,2,1,0:T(8,128)} %copy-done.5, bf16[256,256]{1,0:T(8,128)(2,1)S(1)} %copy-done.7, ...), custom_call_target="tpu_custom_call" | custom-call | flops 2147483648 | bytes 10485760 | tf_op jit(solution)/shard_map/row_part/pallas_call | solution.py:411
  199.7 2.6 %pack_columns.7 = (f32[2,2,128,128]{3,2,1,0:T(8,128)}, f32[2,2,128,128]{3,2,1,0:T(8,128)}, f32[2,2,128,128]{3,2,1,0:T(8,128)}) custom-call(s32[6]{0:T(128)} %select_reduce_fusion.ctab, f32[16,2,128,128]{3,2,1,0:T(8,128)} %row_part.6.z_ref), custom_call_target="tpu_custom_call" | custom-call | bytes 1048576 | tf_op jit(solution)/shard_map/pack_columns/pallas_call | solution.py:189
  202.3 4.3 %collective-permute-start.9 = (f32[2,2,128,128]{3,2,1,0:T(8,128)}, f32[2,2,128,128]{3,2,1,0:T(8,128)S(1)}, u32[]{:S(2)}, u32[]{:S(2)}) collective-permute-start(f32[2,2,128,128]{3,2,1,0:T(8,128)} %get-tuple-element.61), channel_id=1, source_target_pairs={{0,96},{32,0},{64,32},{96,64},{1,97},{33,1},{65,33},{97,65},{2,98}... | collective-permute-start | bytes 786440 | tf_op jit(solution)/shard_map/ppermute | solution.py:485
  207.9 10.5 %collective-permute-done.9.c1 = f32[2,2,128,128]{3,2,1,0:T(8,128)S(1)} collective-permute-done((f32[2,2,128,128]{3,2,1,0:T(8,128)}, f32[2,2,128,128]{3,2,1,0:T(8,128)S(1)}, u32[]{:S(2)}, u32[]{:S(2)}) %collective-permute-start.9) | collective-permute-done | bytes 262176 | tf_op jit(solution)/shard_map/ppermute | solution.py:485
  218.4 3.3 %collective-permute-done.11.c3 = f32[2,2,128,128]{3,2,1,0:T(8,128)S(1)} collective-permute-done((f32[2,2,128,128]{3,2,1,0:T(8,128)}, f32[2,2,128,128]{3,2,1,0:T(8,128)S(1)}, u32[]{:S(2)}, u32[]{:S(2)}) %collective-permute-start.11) | collective-permute-done | bytes 262176 | tf_op jit(solution)/shard_map/ppermute | solution.py:485
  224.9 8.2 %local_part.7.part = f32[16,2,128,128]{3,2,1,0:T(8,128)S(1)} custom-call(s32[128]{0:T(128)S(1)} %reshape.155.tab, f32[176]{0:T(256)S(1)} %reshape.156.wts, f32[16,2,128,128]{3,2,1,0:T(8,128)S(1)} %copy-done.4, f32[2,2,128,128]{3,2,1,0:T(8,128)S(1)} %collective-permute-done.9.c1, f32[2,2,128,128]{3,2,1,0:T(8,128)S(1)} %collective-permute-done.10.c2, ...), custom_call_target="tpu_custom_call" | custom-call | flops 5368709120 | bytes 8388608 | tf_op jit(solution)/shard_map/local_part/pallas_call | solution.py:156
  234.5 11.2 %all-to-all-done.3.recv = f32[32,2,128,128]{3,2,1,0:T(8,128)} async-done(((f32[32,2,128,128]{3,2,1,0:T(8,128)}), f32[32,2,128,128]{3,2,1,0:T(8,128)}, u32[]{:S(2)}, u32[]{:S(2)}) %all-to-all-start.3) | async-done | bytes 4194336 | tf_op jit(solution)/shard_map/all_to_all | solution.py:477
  245.7 7.9 %row_part.7 = f32[16,2,128,128]{3,2,1,0:T(8,128)} custom-call(s32[128]{0:T(128)S(1)} %reshape.155.tab, f32[176]{0:T(256)S(1)} %reshape.156.wts, s32[1]{0:T(128)} %get-tuple-element.59.token, f32[32,2,128,128]{3,2,1,0:T(8,128)} %all-to-all-done.3.recv, f32[16,2,128,128]{3,2,1,0:T(8,128)} %copy-done.9, bf16[256,256]{1,0:T(8,128)(2,1)S(1)} %copy-done.7, ...), custom_call_target="tpu_custom_call" | custom-call | flops 2147483648 | bytes 10485760 | tf_op jit(solution)/shard_map/row_part/pallas_call | solution.py:411
  (98 shorter events, 36.0 us)
Async XLA Ops:
  3.4 7.8 %copy-start.19 = (s32[16,4]{0,1:T(4,128)S(1)}, s32[16,4]{0,1:T(4,128)}, u32[]{:S(2)}) copy-start(s32[16,4]{0,1:T(4,128)} %param.14) | copy-start | bytes 772
  3.4 7.8 %copy-start.20 = (s32[16,4]{0,1:T(4,128)S(1)}, s32[16,4]{0,1:T(4,128)}, u32[]{:S(2)}) copy-start(s32[16,4]{0,1:T(4,128)} %param.13) | copy-start | bytes 772
  3.4 17.3 %copy-start.22 = (f32[2,4]{1,0:T(2,128)S(1)}, f32[2,4]{1,0:T(2,128)}, u32[]{:S(2)}) copy-start(f32[2,4]{1,0:T(2,128)} %param.12) | copy-start | bytes 100
  3.4 17.4 %copy-start.21 = (s32[16,4]{0,1:T(4,128)S(1)}, s32[16,4]{0,1:T(4,128)}, u32[]{:S(2)}) copy-start(s32[16,4]{0,1:T(4,128)} %param.15) | copy-start | bytes 772
  3.4 17.7 %copy-start.23 = (f32[4]{0:T(128)S(1)}, f32[4]{0:T(128)}, u32[]{:S(2)}) copy-start(f32[4]{0:T(128)} %param.11) | copy-start | bytes 52
  3.4 31.1 %copy-start.1 = (f32[16,2,128,128]{3,2,1,0:T(8,128)S(1)}, f32[16,2,128,128]{3,2,1,0:T(8,128)}, u32[]{:S(2)}) copy-start(f32[16,2,128,128]{3,2,1,0:T(8,128)} %rest_0_.5) | copy-start | bytes 6291460
  3.5 61.7 %all-to-all-start = ((f32[32,2,128,128]{3,2,1,0:T(8,128)}), f32[32,2,128,128]{3,2,1,0:T(8,128)}, u32[]{:S(2)}, u32[]{:S(2)}) async-start(f32[32,2,128,128]{3,2,1,0:T(8,128)} %pack_rows.1), calls=%async_computation | async-start | bytes 8388608 | tf_op jit(solution)/shard_map/all_to_all | solution.py:477
  15.2 16.1 %collective-permute-start = (f32[2,2,128,128]{3,2,1,0:T(8,128)}, f32[2,2,128,128]{3,2,1,0:T(8,128)S(1)}, u32[]{:S(2)}, u32[]{:S(2)}) collective-permute-start(f32[2,2,128,128]{3,2,1,0:T(8,128)} %get-tuple-element.35), channel_id=1, source_target_pairs={{0,96},{32,0},{64,32},{96,64},{1,97},{33,1},{65,33},{97,65},{2,98}... | collective-permute-start | bytes 786440 | tf_op jit(solution)/shard_map/ppermute | solution.py:485
  19.4 11.9 %collective-permute-start.1 = (f32[2,2,128,128]{3,2,1,0:T(8,128)}, f32[2,2,128,128]{3,2,1,0:T(8,128)S(1)}, u32[]{:S(2)}, u32[]{:S(2)}) collective-permute-start(f32[2,2,128,128]{3,2,1,0:T(8,128)} %get-tuple-element.36), channel_id=1, source_target_pairs={{0,64},{32,96},{64,0},{96,32},{1,65},{33,97},{65,1},{97,33},{2,66}... | collective-permute-start | bytes 786440 | tf_op jit(solution)/shard_map/ppermute | solution.py:485
  19.4 15.2 %collective-permute-start.2 = (f32[2,2,128,128]{3,2,1,0:T(8,128)}, f32[2,2,128,128]{3,2,1,0:T(8,128)S(1)}, u32[]{:S(2)}, u32[]{:S(2)}) collective-permute-start(f32[2,2,128,128]{3,2,1,0:T(8,128)} %get-tuple-element.37), channel_id=1, source_target_pairs={{0,32},{32,64},{64,96},{96,0},{1,33},{33,65},{65,97},{97,1},{2,34}... | collective-permute-start | bytes 786440 | tf_op jit(solution)/shard_map/ppermute | solution.py:485
  36.8 28.4 %copy-start.7 = (bf16[256,256]{1,0:T(8,128)(2,1)S(1)}, bf16[256,256]{1,0:T(8,128)(2,1)}, u32[]{:S(2)}) copy-start(bf16[256,256]{1,0:T(8,128)(2,1)} %get-tuple-element.42.left) | copy-start | bytes 393220
  36.8 28.4 %copy-start.8 = (bf16[256,256]{1,0:T(8,128)(2,1)S(1)}, bf16[256,256]{1,0:T(8,128)(2,1)}, u32[]{:S(2)}) copy-start(bf16[256,256]{1,0:T(8,128)(2,1)} %get-tuple-element.43.right) | copy-start | bytes 393220
  66.5 58.8 %all-to-all-start.1 = ((f32[32,2,128,128]{3,2,1,0:T(8,128)}), f32[32,2,128,128]{3,2,1,0:T(8,128)}, u32[]{:S(2)}, u32[]{:S(2)}) async-start(f32[32,2,128,128]{3,2,1,0:T(8,128)} %get-tuple-element.44), calls=%async_computation.1 | async-start | bytes 8388608 | tf_op jit(solution)/shard_map/all_to_all | solution.py:477
  71.4 28.2 %copy-start.11 = (bf16[256,1280]{1,0:T(8,128)(2,1)S(1)}, bf16[256,1280]{1,0:T(8,128)(2,1)}, u32[]{:S(2)}) copy-start(bf16[256,1280]{1,0:T(8,128)(2,1)} %get-tuple-element.38.left) | copy-start | bytes 1966084
  80.1 16.1 %collective-permute-start.3 = (f32[2,2,128,128]{3,2,1,0:T(8,128)}, f32[2,2,128,128]{3,2,1,0:T(8,128)S(1)}, u32[]{:S(2)}, u32[]{:S(2)}) collective-permute-start(f32[2,2,128,128]{3,2,1,0:T(8,128)} %get-tuple-element.46), channel_id=1, source_target_pairs={{0,96},{32,0},{64,32},{96,64},{1,97},{33,1},{65,33},{97,65},{2,98}... | collective-permute-start | bytes 786440 | tf_op jit(solution)/shard_map/ppermute | solution.py:485
  84.4 11.8 %collective-permute-start.4 = (f32[2,2,128,128]{3,2,1,0:T(8,128)}, f32[2,2,128,128]{3,2,1,0:T(8,128)S(1)}, u32[]{:S(2)}, u32[]{:S(2)}) collective-permute-start(f32[2,2,128,128]{3,2,1,0:T(8,128)} %get-tuple-element.47), channel_id=1, source_target_pairs={{0,64},{32,96},{64,0},{96,32},{1,65},{33,97},{65,1},{97,33},{2,66}... | collective-permute-start | bytes 786440 | tf_op jit(solution)/shard_map/ppermute | solution.py:485
  84.4 15.1 %collective-permute-start.5 = (f32[2,2,128,128]{3,2,1,0:T(8,128)}, f32[2,2,128,128]{3,2,1,0:T(8,128)S(1)}, u32[]{:S(2)}, u32[]{:S(2)}) collective-permute-start(f32[2,2,128,128]{3,2,1,0:T(8,128)} %get-tuple-element.48), channel_id=1, source_target_pairs={{0,32},{32,64},{64,96},{96,0},{1,33},{33,65},{65,97},{97,1},{2,34}... | collective-permute-start | bytes 786440 | tf_op jit(solution)/shard_map/ppermute | solution.py:485
  99.6 1.6 copy-start
  126.7 58.8 %all-to-all-start.2 = ((f32[32,2,128,128]{3,2,1,0:T(8,128)}), f32[32,2,128,128]{3,2,1,0:T(8,128)}, u32[]{:S(2)}, u32[]{:S(2)}) async-start(f32[32,2,128,128]{3,2,1,0:T(8,128)} %get-tuple-element.51), calls=%async_computation.2 | async-start | bytes 8388608 | tf_op jit(solution)/shard_map/all_to_all | solution.py:477
  131.6 30.0 %copy-start.14 = (bf16[1280,256]{1,0:T(8,128)(2,1)S(1)}, bf16[1280,256]{1,0:T(8,128)(2,1)}, u32[]{:S(2)}) copy-start(bf16[1280,256]{1,0:T(8,128)(2,1)} %get-tuple-element.39.right) | copy-start | bytes 1966084
  142.1 16.1 %collective-permute-start.6 = (f32[2,2,128,128]{3,2,1,0:T(8,128)}, f32[2,2,128,128]{3,2,1,0:T(8,128)S(1)}, u32[]{:S(2)}, u32[]{:S(2)}) collective-permute-start(f32[2,2,128,128]{3,2,1,0:T(8,128)} %get-tuple-element.53), channel_id=1, source_target_pairs={{0,96},{32,0},{64,32},{96,64},{1,97},{33,1},{65,33},{97,65},{2,98}... | collective-permute-start | bytes 786440 | tf_op jit(solution)/shard_map/ppermute | solution.py:485
  146.4 11.8 %collective-permute-start.7 = (f32[2,2,128,128]{3,2,1,0:T(8,128)}, f32[2,2,128,128]{3,2,1,0:T(8,128)S(1)}, u32[]{:S(2)}, u32[]{:S(2)}) collective-permute-start(f32[2,2,128,128]{3,2,1,0:T(8,128)} %get-tuple-element.54), channel_id=1, source_target_pairs={{0,64},{32,96},{64,0},{96,32},{1,65},{33,97},{65,1},{97,33},{2,66}... | collective-permute-start | bytes 786440 | tf_op jit(solution)/shard_map/ppermute | solution.py:485
  146.4 15.1 %collective-permute-start.8 = (f32[2,2,128,128]{3,2,1,0:T(8,128)}, f32[2,2,128,128]{3,2,1,0:T(8,128)S(1)}, u32[]{:S(2)}, u32[]{:S(2)}) collective-permute-start(f32[2,2,128,128]{3,2,1,0:T(8,128)} %get-tuple-element.55), channel_id=1, source_target_pairs={{0,32},{32,64},{64,96},{96,0},{1,33},{33,65},{65,97},{97,1},{2,34}... | collective-permute-start | bytes 786440 | tf_op jit(solution)/shard_map/ppermute | solution.py:485
  161.5 1.6 copy-start.2
  163.1 1.6 copy-start.18
  186.9 58.8 %all-to-all-start.3 = ((f32[32,2,128,128]{3,2,1,0:T(8,128)}), f32[32,2,128,128]{3,2,1,0:T(8,128)}, u32[]{:S(2)}, u32[]{:S(2)}) async-start(f32[32,2,128,128]{3,2,1,0:T(8,128)} %get-tuple-element.60), calls=%async_computation.3 | async-start | bytes 8388608 | tf_op jit(solution)/shard_map/all_to_all | solution.py:477
  202.3 16.1 %collective-permute-start.9 = (f32[2,2,128,128]{3,2,1,0:T(8,128)}, f32[2,2,128,128]{3,2,1,0:T(8,128)S(1)}, u32[]{:S(2)}, u32[]{:S(2)}) collective-permute-start(f32[2,2,128,128]{3,2,1,0:T(8,128)} %get-tuple-element.61), channel_id=1, source_target_pairs={{0,96},{32,0},{64,32},{96,64},{1,97},{33,1},{65,33},{97,65},{2,98}... | collective-permute-start | bytes 786440 | tf_op jit(solution)/shard_map/ppermute | solution.py:485
  206.6 11.8 %collective-permute-start.10 = (f32[2,2,128,128]{3,2,1,0:T(8,128)}, f32[2,2,128,128]{3,2,1,0:T(8,128)S(1)}, u32[]{:S(2)}, u32[]{:S(2)}) collective-permute-start(f32[2,2,128,128]{3,2,1,0:T(8,128)} %get-tuple-element.62), channel_id=1, source_target_pairs={{0,64},{32,96},{64,0},{96,32},{1,65},{33,97},{65,1},{97,33},{2,66}... | collective-permute-start | bytes 786440 | tf_op jit(solution)/shard_map/ppermute | solution.py:485
  206.6 15.1 %collective-permute-start.11 = (f32[2,2,128,128]{3,2,1,0:T(8,128)}, f32[2,2,128,128]{3,2,1,0:T(8,128)S(1)}, u32[]{:S(2)}, u32[]{:S(2)}) collective-permute-start(f32[2,2,128,128]{3,2,1,0:T(8,128)} %get-tuple-element.63), channel_id=1, source_target_pairs={{0,32},{32,64},{64,96},{96,0},{1,33},{33,65},{65,97},{97,1},{2,34}... | collective-permute-start | bytes 786440 | tf_op jit(solution)/shard_map/ppermute | solution.py:485
  221.7 1.6 copy-start.4
  223.3 1.6 copy-start.16
  233.2 1.3 copy-start.9
  (8 other events, 9.9 us)

commit v4 on v3

--- a/solution.py
+++ b/solution.py
@@ -325,7 +325,7 @@
     )(tab, wts, *in_hbm(recv, part, slots), left, right, *olds)
 
 
-def row_kernel(tab, wts, token, recv, part, left, right, *rest, scale, back, last):
+def row_kernel(tab, wts, token, recv, part, left, right, *rest, scale, back, last, own_only):
     del token
     count, _, n, _ = part.shape
     if back is not None:
@@ -333,6 +333,8 @@
     z_out, xbuf, ybuf, wbuf, zbuf, sem_x, sem_y, sem_w, sem_g, sem_z = rest
 
     def fetch(g, go):
+        if own_only:
+            return
         slot, low = first_slot(tab, g), tab[g * 8 + 1]
         when_copy(slot >= 0, recv.at[jnp.maximum(slot, 0)], xbuf.at[g], sem_x.at[g], go)
         when_copy(two_links(tab, g), recv.at[jnp.maximum(low, 0)], ybuf.at[g], sem_y.at[g], go)
@@ -362,7 +364,7 @@
 
     def linked(group, buf, above):
         both = [weights(wts, g, a) for g, a in zip(group, above)]
-        values = [(buf[g, 0], buf[g, 1]) for g in group]
+        values = [(0.0, 0.0) if own_only else (buf[g, 0], buf[g, 1]) for g in group]
         if back is not None:
             own = [(wbuf[g, 0], wbuf[g, 1]) for g in group]
             terms = product(
@@ -404,12 +406,12 @@
         keep(step).wait()
 
 
-def row_part(tab, wts, token, recv, part, prev, left, right, scale, back, last):
+def row_part(tab, wts, token, recv, part, prev, left, right, scale, back, last, own_only=False):
     count, _, n, _ = part.shape
     out = jax.ShapeDtypeStruct(part.shape, f32) if last else pltpu.HBM(part.shape, f32)
     olds = [] if back is None else in_hbm(prev)
     return pl.pallas_call(
-        functools.partial(row_kernel, scale=scale, back=back, last=last),
+        functools.partial(row_kernel, scale=scale, back=back, last=last, own_only=own_only),
         out_shape=out,
         in_specs=[SMEM, SMEM, SMEM, HBM, HBM, VMEM, VMEM] + [HBM] * len(olds),
         out_specs=HBM,
@@ -486,17 +488,22 @@
             for s in range(1, along_x)
         ]
         scale = step_size / (level + 1)
+        back = step_size / level if level else None
+        prev = states[level - 1] if level else None
+        mats = (row_left, row_right)
+        if last:
+            acc = row_part(tab, wts, token, prev, acc, prev, *mats, scale, back, True, own_only=True)
+            scale_row, back = scale * back, None
+        else:
+            scale_row = scale
         parts = local_part(
             tab, wts, z, arrived[::-1], left, right, acc, along_y, scale if last else None
         )
         acc = densities if level == 0 else None if last else parts[2]
-        back = step_size / level if level else None
-        prev = states[level - 1] if level else None
-        mats = (row_left, row_right)
         if not last:
             slots, token = fix_slots(tab, wts, recv, parts[0], parts[1], prev, *mats, back)
             following = exchange(slots)
-        new = row_part(tab, wts, token, recv, parts[0], prev, *mats, scale, back, last)
+        new = row_part(tab, wts, token, recv, parts[0], prev, *mats, scale_row, back, last)
         if last:
             return new
         states.append(new)

time: 255 us -> 253 us (level)
  Pallas kernels: 84.9 us -> 89.8 us
  local copies, waits for them, and re-layouts: 20.6 us -> 17 us
  waiting for transfers between devices: 102 us -> 98.9 us
    ppermute x12, waiting for transfers between devices: 51.8 us -> 44.7 us  [local(): lax.ppermute(col_send[s - 1], 'gx', [(x, (x + s) % along_x) for x in rang...]
    pallas_call x4 -> x5, Pallas kernels: 29.9 us -> 34.4 us  [row_part(): pl.pallas_call(functools.partial(row_kernel, scale=scale, back=back, last...]
    all_to_all x4, waiting for transfers between devices: 50.3 us -> 54.2 us  [local(): lax.all_to_all(a, 'gy', split_axis=0, concat_axis=0, tiled=True)]
    unnamed x48 -> x50, local copies, waits for them, and re-layouts: 19.2 us -> 15.6 us
  transfers between devices with their start and end apart: 16 -> 16, of which waited for: 12 -> 12; matrix products, arithmetic and copies ran while one was open for 1% -> 1% of each run, Pallas kernels for 27% -> 30%
where the time goes in v4:
time: 253 us; the launch traced here: 252 us
  waiting for transfers between devices  98.9 us (39%)
  Pallas kernels  89.8 us (35%)
  starting transfers between devices  44.2 us (17%)
  local copies, waits for them, and re-layouts  17 us (7%)
    all_to_all x4, waiting for transfers between devices, local(): lax.all_to_all(a, 'gy', split_axis=0, concat_axis=0, tiled=True)  54.2 us
    ppermute x12, waiting for transfers between devices, local(): lax.ppermute(col_send[s - 1], 'gx', [(x, (x + s) % along_x) for x in rang...  44.7 us
    pallas_call x4, Pallas kernels, local_part(): pl.pallas_call(functools.partial(local_kernel, with_sum=with_sum, last_sc...  34.9 us
    pallas_call x5, Pallas kernels, row_part(): pl.pallas_call(functools.partial(row_kernel, scale=scale, back=back, last...  34.4 us
    all_to_all x4, starting transfers between devices, local(): lax.all_to_all(a, 'gy', split_axis=0, concat_axis=0, tiled=True)  22.2 us
    ppermute x12, starting transfers between devices, local(): lax.ppermute(col_send[s - 1], 'gx', [(x, (x + s) % along_x) for x in rang...  22 us
    unnamed x50, local copies, waits for them, and re-layouts  15.6 us
    pallas_call x4, Pallas kernels, pack_columns(): pl.pallas_call(pack_columns_kernel, out_shape=[pltpu.HBM((XCAP, 2, n, n),...  10.7 us
  transfers between devices with their start and end apart: 16, of which 12 were waited for; matrix products, arithmetic and copies ran while one was open for 1% of the time, Pallas kernels for 30%

profile of v4, /device:TPU:0, one launch (start us, length us, event | category | flops | bytes accessed | tf_op | source)
XLA Modules:
  0.0 251.8 jit_solution(1803149153759722866)
XLA Ops:
  0.0 3.3 %pack_rows.1 = f32[32,2,128,128]{3,2,1,0:T(8,128)} custom-call(s32[4,16]{1,0:T(4,128)} %bitcast.22, s32[4,16]{1,0:T(4,128)} %bitcast.18, f32[16,2,128,128]{3,2,1,0:T(8,128)} %rest_0_.5), custom_call_target="tpu_custom_call" | custom-call | tf_op jit(solution)/shard_map/pack_rows/pallas_call | solution.py:437
  3.4 7.6 %all-to-all-start = ((f32[32,2,128,128]{3,2,1,0:T(8,128)}), f32[32,2,128,128]{3,2,1,0:T(8,128)}, u32[]{:S(2)}, u32[]{:S(2)}) async-start(f32[32,2,128,128]{3,2,1,0:T(8,128)} %pack_rows.1), calls=%async_computation | async-start | bytes 8388608 | tf_op jit(solution)/shard_map/all_to_all | solution.py:479
  15.2 4.1 %collective-permute-start = (f32[2,2,128,128]{3,2,1,0:T(8,128)}, f32[2,2,128,128]{3,2,1,0:T(8,128)S(1)}, u32[]{:S(2)}, u32[]{:S(2)}) collective-permute-start(f32[2,2,128,128]{3,2,1,0:T(8,128)} %get-tuple-element.35), channel_id=1, source_target_pairs={{0,96},{32,0},{64,32},{96,64},{1,97},{33,1},{65,33},{97,65},{2,98}... | collective-permute-start | bytes 786440 | tf_op jit(solution)/shard_map/ppermute | solution.py:487
  24.3 6.9 %collective-permute-done.c1 = f32[2,2,128,128]{3,2,1,0:T(8,128)S(1)} collective-permute-done((f32[2,2,128,128]{3,2,1,0:T(8,128)}, f32[2,2,128,128]{3,2,1,0:T(8,128)S(1)}, u32[]{:S(2)}, u32[]{:S(2)}) %collective-permute-start) | collective-permute-done | bytes 262176 | tf_op jit(solution)/shard_map/ppermute | solution.py:487
  31.2 3.4 %collective-permute-done.2.c3 = f32[2,2,128,128]{3,2,1,0:T(8,128)S(1)} collective-permute-done((f32[2,2,128,128]{3,2,1,0:T(8,128)}, f32[2,2,128,128]{3,2,1,0:T(8,128)S(1)}, u32[]{:S(2)}, u32[]{:S(2)}) %collective-permute-start.2) | collective-permute-done | bytes 262176 | tf_op jit(solution)/shard_map/ppermute | solution.py:487
  36.7 8.5 %local_part.4 = (f32[16,2,128,128]{3,2,1,0:T(8,128)S(1)}, f32[32,2,128,128]{3,2,1,0:T(8,128)}) custom-call(s32[128]{0:T(128)S(1)} %reshape.155.tab, f32[176]{0:T(256)S(1)} %reshape.156.wts, f32[16,2,128,128]{3,2,1,0:T(8,128)S(1)} %copy-done.2, f32[2,2,128,128]{3,2,1,0:T(8,128)S(1)} %collective-permute-done.c1, ...), custom_call_target="tpu_custom_call" | custom-call | flops 5368709120 | bytes 8388608 | tf_op jit(solution)/shard_map/local_part/pallas_call | solution.py:156
  46.5 18.4 %all-to-all-done.recv = f32[32,2,128,128]{3,2,1,0:T(8,128)} async-done(((f32[32,2,128,128]{3,2,1,0:T(8,128)}), f32[32,2,128,128]{3,2,1,0:T(8,128)}, u32[]{:S(2)}, u32[]{:S(2)}) %all-to-all-start) | async-done | bytes 4194336 | tf_op jit(solution)/shard_map/all_to_all | solution.py:479
  66.3 4.9 %all-to-all-start.1 = ((f32[32,2,128,128]{3,2,1,0:T(8,128)}), f32[32,2,128,128]{3,2,1,0:T(8,128)}, u32[]{:S(2)}, u32[]{:S(2)}) async-start(f32[32,2,128,128]{3,2,1,0:T(8,128)} %get-tuple-element.44), calls=%async_computation.1 | async-start | bytes 8388608 | tf_op jit(solution)/shard_map/all_to_all | solution.py:479
  71.2 6.1 %row_part.5.z_ref.rest_0_ = f32[16,2,128,128]{3,2,1,0:T(8,128)} custom-call(s32[128]{0:T(128)S(1)} %reshape.155.tab, f32[176]{0:T(256)S(1)} %reshape.156.wts, s32[1]{0:T(128)} %get-tuple-element.45.token, f32[32,2,128,128]{3,2,1,0:T(8,128)} %all-to-all-done.recv, f32[16,2,128,128]{3,2,1,0:T(8,128)} %copy-done.6, bf16[256,256]{1,0:T(8,128)(2,1)S(1)} %copy-done.4, ...), custom_call_target="tpu_custom_call" | custom-call | flops 2147483648 | bytes 10485760 | tf_op jit(solution)/shard_map/row_part/pallas_call | solution.py:413
  77.3 2.8 %pack_columns.5 = (f32[2,2,128,128]{3,2,1,0:T(8,128)}, f32[2,2,128,128]{3,2,1,0:T(8,128)}, f32[2,2,128,128]{3,2,1,0:T(8,128)}) custom-call(s32[6]{0:T(128)} %select_reduce_fusion.ctab, f32[16,2,128,128]{3,2,1,0:T(8,128)} %row_part.5.z_ref.rest_0_), custom_call_target="tpu_custom_call" | custom-call | bytes 1048576 | tf_op jit(solution)/shard_map/pack_columns/pallas_call | solution.py:189
  80.1 4.2 %collective-permute-start.3 = (f32[2,2,128,128]{3,2,1,0:T(8,128)}, f32[2,2,128,128]{3,2,1,0:T(8,128)S(1)}, u32[]{:S(2)}, u32[]{:S(2)}) collective-permute-start(f32[2,2,128,128]{3,2,1,0:T(8,128)} %get-tuple-element.46), channel_id=1, source_target_pairs={{0,96},{32,0},{64,32},{96,64},{1,97},{33,1},{65,33},{97,65},{2,98}... | collective-permute-start | bytes 786440 | tf_op jit(solution)/shard_map/ppermute | solution.py:487
  85.6 10.4 %collective-permute-done.3.c1 = f32[2,2,128,128]{3,2,1,0:T(8,128)S(1)} collective-permute-done((f32[2,2,128,128]{3,2,1,0:T(8,128)}, f32[2,2,128,128]{3,2,1,0:T(8,128)S(1)}, u32[]{:S(2)}, u32[]{:S(2)}) %collective-permute-start.3) | collective-permute-done | bytes 262176 | tf_op jit(solution)/shard_map/ppermute | solution.py:487
  96.0 3.3 %collective-permute-done.5.c3 = f32[2,2,128,128]{3,2,1,0:T(8,128)S(1)} collective-permute-done((f32[2,2,128,128]{3,2,1,0:T(8,128)}, f32[2,2,128,128]{3,2,1,0:T(8,128)S(1)}, u32[]{:S(2)}, u32[]{:S(2)}) %collective-permute-start.5) | collective-permute-done | bytes 262176 | tf_op jit(solution)/shard_map/ppermute | solution.py:487
  102.0 9.0 %local_part.5 = (f32[16,2,128,128]{3,2,1,0:T(8,128)S(1)}, f32[32,2,128,128]{3,2,1,0:T(8,128)}, f32[16,2,128,128]{3,2,1,0:T(8,128)S(1)}) custom-call(s32[128]{0:T(128)S(1)} %reshape.155.tab, f32[176]{0:T(256)S(1)} %reshape.156.wts, f32[16,2,128,128]{3,2,1,0:T(8,128)S(1)} %copy-done.1, f32[2,2,128,128]{3,2,1,0:T(8,128)S(1)} %collective-permute-done.3.c1, ...), custom_call_target="tpu_custom_call" | custom-call | flops 5368709120 | bytes 8388608 | tf_op jit(solution)/shard_map/local_part/pallas_call | solution.py:156
  113.7 11.4 %all-to-all-done.1.recv = f32[32,2,128,128]{3,2,1,0:T(8,128)} async-done(((f32[32,2,128,128]{3,2,1,0:T(8,128)}), f32[32,2,128,128]{3,2,1,0:T(8,128)}, u32[]{:S(2)}, u32[]{:S(2)}) %all-to-all-start.1) | async-done | bytes 4194336 | tf_op jit(solution)/shard_map/all_to_all | solution.py:479
  126.5 4.9 %all-to-all-start.2 = ((f32[32,2,128,128]{3,2,1,0:T(8,128)}), f32[32,2,128,128]{3,2,1,0:T(8,128)}, u32[]{:S(2)}, u32[]{:S(2)}) async-start(f32[32,2,128,128]{3,2,1,0:T(8,128)} %get-tuple-element.51), calls=%async_computation.2 | async-start | bytes 8388608 | tf_op jit(solution)/shard_map/all_to_all | solution.py:479
  131.4 7.8 %row_part.6.z_ref.recv.rest_0_ = f32[16,2,128,128]{3,2,1,0:T(8,128)} custom-call(s32[128]{0:T(128)S(1)} %reshape.155.tab, f32[176]{0:T(256)S(1)} %reshape.156.wts, s32[1]{0:T(128)} %get-tuple-element.52.token, f32[32,2,128,128]{3,2,1,0:T(8,128)} %all-to-all-done.1.recv, f32[16,2,128,128]{3,2,1,0:T(8,128)} %copy-done.9, bf16[256,256]{1,0:T(8,128)(2,1)S(1)} %copy-done.4, ...), custom_call_target="tpu_custom_call" | custom-call | flops 2147483648 | bytes 10485760 | tf_op jit(solution)/shard_map/row_part/pallas_call | solution.py:413
  139.2 2.7 %pack_columns.6 = (f32[2,2,128,128]{3,2,1,0:T(8,128)}, f32[2,2,128,128]{3,2,1,0:T(8,128)}, f32[2,2,128,128]{3,2,1,0:T(8,128)}) custom-call(s32[6]{0:T(128)} %select_reduce_fusion.ctab, f32[16,2,128,128]{3,2,1,0:T(8,128)} %row_part.6.z_ref.recv.rest_0_), custom_call_target="tpu_custom_call" | custom-call | bytes 1048576 | tf_op jit(solution)/shard_map/pack_columns/pallas_call | solution.py:189
  141.9 4.2 %collective-permute-start.6 = (f32[2,2,128,128]{3,2,1,0:T(8,128)}, f32[2,2,128,128]{3,2,1,0:T(8,128)S(1)}, u32[]{:S(2)}, u32[]{:S(2)}) collective-permute-start(f32[2,2,128,128]{3,2,1,0:T(8,128)} %get-tuple-element.53), channel_id=1, source_target_pairs={{0,96},{32,0},{64,32},{96,64},{1,97},{33,1},{65,33},{97,65},{2,98}... | collective-permute-start | bytes 786440 | tf_op jit(solution)/shard_map/ppermute | solution.py:487
  147.4 10.5 %collective-permute-done.6.c1 = f32[2,2,128,128]{3,2,1,0:T(8,128)S(1)} collective-permute-done((f32[2,2,128,128]{3,2,1,0:T(8,128)}, f32[2,2,128,128]{3,2,1,0:T(8,128)S(1)}, u32[]{:S(2)}, u32[]{:S(2)}) %collective-permute-start.6) | collective-permute-done | bytes 262176 | tf_op jit(solution)/shard_map/ppermute | solution.py:487
  157.9 3.3 %collective-permute-done.8.c3 = f32[2,2,128,128]{3,2,1,0:T(8,128)S(1)} collective-permute-done((f32[2,2,128,128]{3,2,1,0:T(8,128)}, f32[2,2,128,128]{3,2,1,0:T(8,128)S(1)}, u32[]{:S(2)}, u32[]{:S(2)}) %collective-permute-start.8) | collective-permute-done | bytes 262176 | tf_op jit(solution)/shard_map/ppermute | solution.py:487
  163.9 9.0 %local_part.6 = (f32[16,2,128,128]{3,2,1,0:T(8,128)S(1)}, f32[32,2,128,128]{3,2,1,0:T(8,128)}, f32[16,2,128,128]{3,2,1,0:T(8,128)S(1)}) custom-call(s32[128]{0:T(128)S(1)} %reshape.155.tab, f32[176]{0:T(256)S(1)} %reshape.156.wts, f32[16,2,128,128]{3,2,1,0:T(8,128)S(1)} %copy-done, f32[2,2,128,128]{3,2,1,0:T(8,128)S(1)} %collective-permute-done.6.c1, ...), custom_call_target="tpu_custom_call" | custom-call | flops 5368709120 | bytes 8388608 | tf_op jit(solution)/shard_map/local_part/pallas_call | solution.py:156
  175.6 9.8 %all-to-all-done.2.recv = f32[32,2,128,128]{3,2,1,0:T(8,128)} async-done(((f32[32,2,128,128]{3,2,1,0:T(8,128)}), f32[32,2,128,128]{3,2,1,0:T(8,128)}, u32[]{:S(2)}, u32[]{:S(2)}) %all-to-all-start.2) | async-done | bytes 4194336 | tf_op jit(solution)/shard_map/all_to_all | solution.py:479
  186.7 4.9 %all-to-all-start.3 = ((f32[32,2,128,128]{3,2,1,0:T(8,128)}), f32[32,2,128,128]{3,2,1,0:T(8,128)}, u32[]{:S(2)}, u32[]{:S(2)}) async-start(f32[32,2,128,128]{3,2,1,0:T(8,128)} %get-tuple-element.60), calls=%async_computation.3 | async-start | bytes 8388608 | tf_op jit(solution)/shard_map/all_to_all | solution.py:479
  191.6 7.8 %row_part.7.z_ref = f32[16,2,128,128]{3,2,1,0:T(8,128)} custom-call(s32[128]{0:T(128)S(1)} %reshape.155.tab, f32[176]{0:T(256)S(1)} %reshape.156.wts, s32[1]{0:T(128)} %get-tuple-element.59.token, f32[32,2,128,128]{3,2,1,0:T(8,128)} %all-to-all-done.2.recv, f32[16,2,128,128]{3,2,1,0:T(8,128)} %copy-done.8, bf16[256,256]{1,0:T(8,128)(2,1)S(1)} %copy-done.4, ...), custom_call_target="tpu_custom_call" | custom-call | flops 2147483648 | bytes 10485760 | tf_op jit(solution)/shard_map/row_part/pallas_call | solution.py:413
  202.0 4.2 %collective-permute-start.9 = (f32[2,2,128,128]{3,2,1,0:T(8,128)}, f32[2,2,128,128]{3,2,1,0:T(8,128)S(1)}, u32[]{:S(2)}, u32[]{:S(2)}) collective-permute-start(f32[2,2,128,128]{3,2,1,0:T(8,128)} %get-tuple-element.61), channel_id=1, source_target_pairs={{0,96},{32,0},{64,32},{96,64},{1,97},{33,1},{65,33},{97,65},{2,98}... | collective-permute-start | bytes 786440 | tf_op jit(solution)/shard_map/ppermute | solution.py:487
  207.5 6.8 %row_part.8.rest_0_ = f32[16,2,128,128]{3,2,1,0:T(8,128)S(1)} custom-call(s32[128]{0:T(128)S(1)} %reshape.155.tab, f32[176]{0:T(256)S(1)} %reshape.156.wts, s32[1]{0:T(128)} %get-tuple-element.59.token, f32[16,2,128,128]{3,2,1,0:T(8,128)} %row_part.6.z_ref.recv.rest_0_, f32[16,2,128,128]{3,2,1,0:T(8,128)} %copy-done.10, bf16[256,256]{1,0:T(8,128)(2,1)S(1)} %copy-done.4, ...), custom_call_target="tpu_custom_call" | custom-call | flops 2147483648 | bytes 10485760 | tf_op jit(solution)/shard_map/row_part/pallas_call | solution.py:413
  214.3 3.7 %collective-permute-done.9.c1 = f32[2,2,128,128]{3,2,1,0:T(8,128)S(1)} collective-permute-done((f32[2,2,128,128]{3,2,1,0:T(8,128)}, f32[2,2,128,128]{3,2,1,0:T(8,128)S(1)}, u32[]{:S(2)}, u32[]{:S(2)}) %collective-permute-start.9) | collective-permute-done | bytes 262176 | tf_op jit(solution)/shard_map/ppermute | solution.py:487
  218.0 3.3 %collective-permute-done.11.c3 = f32[2,2,128,128]{3,2,1,0:T(8,128)S(1)} collective-permute-done((f32[2,2,128,128]{3,2,1,0:T(8,128)}, f32[2,2,128,128]{3,2,1,0:T(8,128)S(1)}, u32[]{:S(2)}, u32[]{:S(2)}) %collective-permute-start.11) | collective-permute-done | bytes 262176 | tf_op jit(solution)/shard_map/ppermute | solution.py:487
  221.3 8.4 %local_part.7.part = f32[16,2,128,128]{3,2,1,0:T(8,128)S(1)} custom-call(s32[128]{0:T(128)S(1)} %reshape.155.tab, f32[176]{0:T(256)S(1)} %reshape.156.wts, f32[16,2,128,128]{3,2,1,0:T(8,128)S(1)} %copy-done.7, f32[2,2,128,128]{3,2,1,0:T(8,128)S(1)} %collective-permute-done.9.c1, f32[2,2,128,128]{3,2,1,0:T(8,128)S(1)} %collective-permute-done.10.c2, ...), custom_call_target="tpu_custom_call" | custom-call | flops 5368709120 | bytes 8388608 | tf_op jit(solution)/shard_map/local_part/pallas_call | solution.py:156
  231.1 14.5 %all-to-all-done.3.recv = f32[32,2,128,128]{3,2,1,0:T(8,128)} async-done(((f32[32,2,128,128]{3,2,1,0:T(8,128)}), f32[32,2,128,128]{3,2,1,0:T(8,128)}, u32[]{:S(2)}, u32[]{:S(2)}) %all-to-all-start.3) | async-done | bytes 4194336 | tf_op jit(solution)/shard_map/all_to_all | solution.py:479
  245.6 6.0 %row_part.9 = f32[16,2,128,128]{3,2,1,0:T(8,128)} custom-call(s32[128]{0:T(128)S(1)} %reshape.155.tab, f32[176]{0:T(256)S(1)} %reshape.156.wts, s32[1]{0:T(128)} %get-tuple-element.59.token, f32[32,2,128,128]{3,2,1,0:T(8,128)} %all-to-all-done.3.recv, f32[16,2,128,128]{3,2,1,0:T(8,128)} %copy-done.11, bf16[256,256]{1,0:T(8,128)(2,1)S(1)} %copy-done.4, ...), custom_call_target="tpu_custom_call" | custom-call | flops 2147483648 | bytes 10485760 | tf_op jit(solution)/shard_map/row_part/pallas_call | solution.py:413
  (101 shorter events, 35.3 us)
Async XLA Ops:
  3.3 7.7 %copy-start.20 = (s32[16,4]{0,1:T(4,128)S(1)}, s32[16,4]{0,1:T(4,128)}, u32[]{:S(2)}) copy-start(s32[16,4]{0,1:T(4,128)} %param.14) | copy-start | bytes 772
  3.3 7.7 %copy-start.21 = (s32[16,4]{0,1:T(4,128)S(1)}, s32[16,4]{0,1:T(4,128)}, u32[]{:S(2)}) copy-start(s32[16,4]{0,1:T(4,128)} %param.13) | copy-start | bytes 772
  3.4 61.6 %all-to-all-start = ((f32[32,2,128,128]{3,2,1,0:T(8,128)}), f32[32,2,128,128]{3,2,1,0:T(8,128)}, u32[]{:S(2)}, u32[]{:S(2)}) async-start(f32[32,2,128,128]{3,2,1,0:T(8,128)} %pack_rows.1), calls=%async_computation | async-start | bytes 8388608 | tf_op jit(solution)/shard_map/all_to_all | solution.py:479
  11.0 9.7 %copy-start.23 = (f32[2,4]{1,0:T(2,128)S(1)}, f32[2,4]{1,0:T(2,128)}, u32[]{:S(2)}) copy-start(f32[2,4]{1,0:T(2,128)} %param.12) | copy-start | bytes 100
  11.0 9.9 %copy-start.22 = (s32[16,4]{0,1:T(4,128)S(1)}, s32[16,4]{0,1:T(4,128)}, u32[]{:S(2)}) copy-start(s32[16,4]{0,1:T(4,128)} %param.15) | copy-start | bytes 772
  11.0 10.1 %copy-start.24 = (f32[4]{0:T(128)S(1)}, f32[4]{0:T(128)}, u32[]{:S(2)}) copy-start(f32[4]{0:T(128)} %param.11) | copy-start | bytes 52
  11.0 23.5 %copy-start.2 = (f32[16,2,128,128]{3,2,1,0:T(8,128)S(1)}, f32[16,2,128,128]{3,2,1,0:T(8,128)}, u32[]{:S(2)}) copy-start(f32[16,2,128,128]{3,2,1,0:T(8,128)} %rest_0_.5) | copy-start | bytes 6291460
  15.2 16.0 %collective-permute-start = (f32[2,2,128,128]{3,2,1,0:T(8,128)}, f32[2,2,128,128]{3,2,1,0:T(8,128)S(1)}, u32[]{:S(2)}, u32[]{:S(2)}) collective-permute-start(f32[2,2,128,128]{3,2,1,0:T(8,128)} %get-tuple-element.35), channel_id=1, source_target_pairs={{0,96},{32,0},{64,32},{96,64},{1,97},{33,1},{65,33},{97,65},{2,98}... | collective-permute-start | bytes 786440 | tf_op jit(solution)/shard_map/ppermute | solution.py:487
  19.3 11.9 %collective-permute-start.1 = (f32[2,2,128,128]{3,2,1,0:T(8,128)}, f32[2,2,128,128]{3,2,1,0:T(8,128)S(1)}, u32[]{:S(2)}, u32[]{:S(2)}) collective-permute-start(f32[2,2,128,128]{3,2,1,0:T(8,128)} %get-tuple-element.36), channel_id=1, source_target_pairs={{0,64},{32,96},{64,0},{96,32},{1,65},{33,97},{65,1},{97,33},{2,66}... | collective-permute-start | bytes 786440 | tf_op jit(solution)/shard_map/ppermute | solution.py:487
  19.4 15.2 %collective-permute-start.2 = (f32[2,2,128,128]{3,2,1,0:T(8,128)}, f32[2,2,128,128]{3,2,1,0:T(8,128)S(1)}, u32[]{:S(2)}, u32[]{:S(2)}) collective-permute-start(f32[2,2,128,128]{3,2,1,0:T(8,128)} %get-tuple-element.37), channel_id=1, source_target_pairs={{0,32},{32,64},{64,96},{96,0},{1,33},{33,65},{65,97},{97,1},{2,34}... | collective-permute-start | bytes 786440 | tf_op jit(solution)/shard_map/ppermute | solution.py:487
  36.7 28.2 %copy-start.4 = (bf16[256,256]{1,0:T(8,128)(2,1)S(1)}, bf16[256,256]{1,0:T(8,128)(2,1)}, u32[]{:S(2)}) copy-start(bf16[256,256]{1,0:T(8,128)(2,1)} %get-tuple-element.42.left) | copy-start | bytes 393220
  36.7 28.2 %copy-start.5 = (bf16[256,256]{1,0:T(8,128)(2,1)S(1)}, bf16[256,256]{1,0:T(8,128)(2,1)}, u32[]{:S(2)}) copy-start(bf16[256,256]{1,0:T(8,128)(2,1)} %get-tuple-element.43.right) | copy-start | bytes 393220
  66.3 58.8 %all-to-all-start.1 = ((f32[32,2,128,128]{3,2,1,0:T(8,128)}), f32[32,2,128,128]{3,2,1,0:T(8,128)}, u32[]{:S(2)}, u32[]{:S(2)}) async-start(f32[32,2,128,128]{3,2,1,0:T(8,128)} %get-tuple-element.44), calls=%async_computation.1 | async-start | bytes 8388608 | tf_op jit(solution)/shard_map/all_to_all | solution.py:479
  71.2 28.1 %copy-start.13 = (bf16[256,1280]{1,0:T(8,128)(2,1)S(1)}, bf16[256,1280]{1,0:T(8,128)(2,1)}, u32[]{:S(2)}) copy-start(bf16[256,1280]{1,0:T(8,128)(2,1)} %get-tuple-element.38.left) | copy-start | bytes 1966084
  77.3 22.0 %copy-start.1 = (f32[16,2,128,128]{3,2,1,0:T(8,128)S(1)}, f32[16,2,128,128]{3,2,1,0:T(8,128)}, u32[]{:S(2)}) copy-start(f32[16,2,128,128]{3,2,1,0:T(8,128)} %row_part.5.z_ref.rest_0_) | copy-start | bytes 6291460
  80.1 15.9 %collective-permute-start.3 = (f32[2,2,128,128]{3,2,1,0:T(8,128)}, f32[2,2,128,128]{3,2,1,0:T(8,128)S(1)}, u32[]{:S(2)}, u32[]{:S(2)}) collective-permute-start(f32[2,2,128,128]{3,2,1,0:T(8,128)} %get-tuple-element.46), channel_id=1, source_target_pairs={{0,96},{32,0},{64,32},{96,64},{1,97},{33,1},{65,33},{97,65},{2,98}... | collective-permute-start | bytes 786440 | tf_op jit(solution)/shard_map/ppermute | solution.py:487
  84.3 11.8 %collective-permute-start.4 = (f32[2,2,128,128]{3,2,1,0:T(8,128)}, f32[2,2,128,128]{3,2,1,0:T(8,128)S(1)}, u32[]{:S(2)}, u32[]{:S(2)}) collective-permute-start(f32[2,2,128,128]{3,2,1,0:T(8,128)} %get-tuple-element.47), channel_id=1, source_target_pairs={{0,64},{32,96},{64,0},{96,32},{1,65},{33,97},{65,1},{97,33},{2,66}... | collective-permute-start | bytes 786440 | tf_op jit(solution)/shard_map/ppermute | solution.py:487
  84.3 15.1 %collective-permute-start.5 = (f32[2,2,128,128]{3,2,1,0:T(8,128)}, f32[2,2,128,128]{3,2,1,0:T(8,128)S(1)}, u32[]{:S(2)}, u32[]{:S(2)}) collective-permute-start(f32[2,2,128,128]{3,2,1,0:T(8,128)} %get-tuple-element.48), channel_id=1, source_target_pairs={{0,32},{32,64},{64,96},{96,0},{1,33},{33,65},{65,97},{97,1},{2,34}... | collective-permute-start | bytes 786440 | tf_op jit(solution)/shard_map/ppermute | solution.py:487
  99.4 1.6 copy-start.3
  112.3 1.4 copy-start.18
  126.5 58.8 %all-to-all-start.2 = ((f32[32,2,128,128]{3,2,1,0:T(8,128)}), f32[32,2,128,128]{3,2,1,0:T(8,128)}, u32[]{:S(2)}, u32[]{:S(2)}) async-start(f32[32,2,128,128]{3,2,1,0:T(8,128)} %get-tuple-element.51), calls=%async_computation.2 | async-start | bytes 8388608 | tf_op jit(solution)/shard_map/all_to_all | solution.py:479
  139.2 22.0 %copy-start = (f32[16,2,128,128]{3,2,1,0:T(8,128)S(1)}, f32[16,2,128,128]{3,2,1,0:T(8,128)}, u32[]{:S(2)}) copy-start(f32[16,2,128,128]{3,2,1,0:T(8,128)} %row_part.6.z_ref.recv.rest_0_) | copy-start | bytes 6291460
  141.9 16.0 %collective-permute-start.6 = (f32[2,2,128,128]{3,2,1,0:T(8,128)}, f32[2,2,128,128]{3,2,1,0:T(8,128)S(1)}, u32[]{:S(2)}, u32[]{:S(2)}) collective-permute-start(f32[2,2,128,128]{3,2,1,0:T(8,128)} %get-tuple-element.53), channel_id=1, source_target_pairs={{0,96},{32,0},{64,32},{96,64},{1,97},{33,1},{65,33},{97,65},{2,98}... | collective-permute-start | bytes 786440 | tf_op jit(solution)/shard_map/ppermute | solution.py:487
  146.1 11.8 %collective-permute-start.7 = (f32[2,2,128,128]{3,2,1,0:T(8,128)}, f32[2,2,128,128]{3,2,1,0:T(8,128)S(1)}, u32[]{:S(2)}, u32[]{:S(2)}) collective-permute-start(f32[2,2,128,128]{3,2,1,0:T(8,128)} %get-tuple-element.54), channel_id=1, source_target_pairs={{0,64},{32,96},{64,0},{96,32},{1,65},{33,97},{65,1},{97,33},{2,66}... | collective-permute-start | bytes 786440 | tf_op jit(solution)/shard_map/ppermute | solution.py:487
  146.1 15.1 %collective-permute-start.8 = (f32[2,2,128,128]{3,2,1,0:T(8,128)}, f32[2,2,128,128]{3,2,1,0:T(8,128)S(1)}, u32[]{:S(2)}, u32[]{:S(2)}) collective-permute-start(f32[2,2,128,128]{3,2,1,0:T(8,128)} %get-tuple-element.55), channel_id=1, source_target_pairs={{0,32},{32,64},{64,96},{96,0},{1,33},{33,65},{65,97},{97,1},{2,34}... | collective-permute-start | bytes 786440 | tf_op jit(solution)/shard_map/ppermute | solution.py:487
  162.3 1.6 copy-start.19
  186.7 58.8 %all-to-all-start.3 = ((f32[32,2,128,128]{3,2,1,0:T(8,128)}), f32[32,2,128,128]{3,2,1,0:T(8,128)}, u32[]{:S(2)}, u32[]{:S(2)}) async-start(f32[32,2,128,128]{3,2,1,0:T(8,128)} %get-tuple-element.60), calls=%async_computation.3 | async-start | bytes 8388608 | tf_op jit(solution)/shard_map/all_to_all | solution.py:479
  202.0 16.0 %collective-permute-start.9 = (f32[2,2,128,128]{3,2,1,0:T(8,128)}, f32[2,2,128,128]{3,2,1,0:T(8,128)S(1)}, u32[]{:S(2)}, u32[]{:S(2)}) collective-permute-start(f32[2,2,128,128]{3,2,1,0:T(8,128)} %get-tuple-element.61), channel_id=1, source_target_pairs={{0,96},{32,0},{64,32},{96,64},{1,97},{33,1},{65,33},{97,65},{2,98}... | collective-permute-start | bytes 786440 | tf_op jit(solution)/shard_map/ppermute | solution.py:487
  206.2 11.8 %collective-permute-start.10 = (f32[2,2,128,128]{3,2,1,0:T(8,128)}, f32[2,2,128,128]{3,2,1,0:T(8,128)S(1)}, u32[]{:S(2)}, u32[]{:S(2)}) collective-permute-start(f32[2,2,128,128]{3,2,1,0:T(8,128)} %get-tuple-element.62), channel_id=1, source_target_pairs={{0,64},{32,96},{64,0},{96,32},{1,65},{33,97},{65,1},{97,33},{2,66}... | collective-permute-start | bytes 786440 | tf_op jit(solution)/shard_map/ppermute | solution.py:487
  206.2 15.1 %collective-permute-start.11 = (f32[2,2,128,128]{3,2,1,0:T(8,128)}, f32[2,2,128,128]{3,2,1,0:T(8,128)S(1)}, u32[]{:S(2)}, u32[]{:S(2)}) collective-permute-start(f32[2,2,128,128]{3,2,1,0:T(8,128)} %get-tuple-element.63), channel_id=1, source_target_pairs={{0,32},{32,64},{64,96},{96,0},{1,33},{33,65},{65,97},{97,1},{2,34}... | collective-permute-start | bytes 786440 | tf_op jit(solution)/shard_map/ppermute | solution.py:487
  207.5 13.8 %copy-start.7 = (f32[16,2,128,128]{3,2,1,0:T(8,128)S(1)}, f32[16,2,128,128]{3,2,1,0:T(8,128)}, u32[]{:S(2)}) copy-start(f32[16,2,128,128]{3,2,1,0:T(8,128)} %row_part.7.z_ref) | copy-start | bytes 6291460
  207.5 13.8 %copy-start.17 = (bf16[1280,256]{1,0:T(8,128)(2,1)S(1)}, bf16[1280,256]{1,0:T(8,128)(2,1)}, u32[]{:S(2)}) copy-start(bf16[1280,256]{1,0:T(8,128)(2,1)} %get-tuple-element.39.right) | copy-start | bytes 1966084
  (9 other events, 11.0 us)

commit v5 on v4

--- a/solution.py
+++ b/solution.py
@@ -352,9 +352,8 @@
         for copy in copies:
             copy.start() if go else copy.wait()
 
-    def keep(step):
-        group = pl.ds(step * WIDTH, WIDTH)
-        return pltpu.make_async_copy(zbuf.at[group], z_out.at[group], sem_z.at[step])
+    def keep(g):
+        return pltpu.make_async_copy(zbuf.at[g], z_out.at[g], sem_z.at[g])
 
     @pl.loop(0, count // WIDTH)
     def _(step):
@@ -399,11 +398,12 @@
                 for p in range(2):
                     zbuf[g, p] = zbuf[g, p] + scale * term[p]
 
-        keep(step).start()
-
-    @pl.loop(0, count // WIDTH)
-    def _(step):
-        keep(step).wait()
+        for g in group:
+            keep(g).start()
+
+    @pl.loop(0, count)
+    def _(g):
+        keep(g).wait()
 
 
 def row_part(tab, wts, token, recv, part, prev, left, right, scale, back, last, own_only=False):

time: 253 us -> 253 us (level)
  Pallas kernels: 89.8 us -> 92.8 us
    pallas_call x5, Pallas kernels: 34.4 us -> 37.3 us  [row_part(): pl.pallas_call(functools.partial(row_kernel, scale=scale, back=back, last...]
    ppermute x12, waiting for transfers between devices: 44.7 us -> 42 us  [local(): lax.ppermute(col_send[s - 1], 'gx', [(x, (x + s) % along_x) for x in rang...]
  transfers between devices with their start and end apart: 16 -> 16, of which waited for: 12 -> 12; matrix products, arithmetic and copies ran while one was open for 1% -> 1% of each run, Pallas kernels for 30% -> 31%
where the time goes in v5:
time: 253 us; the launch traced here: 252 us
  waiting for transfers between devices  96.7 us (38%)
  Pallas kernels  92.8 us (37%)
  starting transfers between devices  43.6 us (17%)
  local copies, waits for them, and re-layouts  17 us (7%)
    all_to_all x4, waiting for transfers between devices, local(): lax.all_to_all(a, 'gy', split_axis=0, concat_axis=0, tiled=True)  54.7 us
    ppermute x12, waiting for transfers between devices, local(): lax.ppermute(col_send[s - 1], 'gx', [(x, (x + s) % along_x) for x in rang...  42 us
    pallas_call x5, Pallas kernels, row_part(): pl.pallas_call(functools.partial(row_kernel, scale=scale, back=back, last...  37.3 us
    pallas_call x4, Pallas kernels, local_part(): pl.pallas_call(functools.partial(local_kernel, with_sum=with_sum, last_sc...  35 us
    all_to_all x4, starting transfers between devices, local(): lax.all_to_all(a, 'gy', split_axis=0, concat_axis=0, tiled=True)  22.2 us
    ppermute x12, starting transfers between devices, local(): lax.ppermute(col_send[s - 1], 'gx', [(x, (x + s) % along_x) for x in rang...  21.4 us
    unnamed x50, local copies, waits for them, and re-layouts  15.6 us
    pallas_call x4, Pallas kernels, pack_columns(): pl.pallas_call(pack_columns_kernel, out_shape=[pltpu.HBM((XCAP, 2, n, n),...  10.6 us
  transfers between devices with their start and end apart: 16, of which 12 were waited for; matrix products, arithmetic and copies ran while one was open for 1% of the time, Pallas kernels for 31%

profile of v5, /device:TPU:0, one launch (start us, length us, event | category | flops | bytes accessed | tf_op | source)
XLA Modules:
  0.0 252.0 jit_solution(11294519707369874580)
XLA Ops:
  0.0 3.5 %pack_rows.1 = f32[32,2,128,128]{3,2,1,0:T(8,128)} custom-call(s32[4,16]{1,0:T(4,128)} %bitcast.22, s32[4,16]{1,0:T(4,128)} %bitcast.18, f32[16,2,128,128]{3,2,1,0:T(8,128)} %rest_0_.5), custom_call_target="tpu_custom_call" | custom-call | tf_op jit(solution)/shard_map/pack_rows/pallas_call | solution.py:437
  3.5 7.6 %all-to-all-start = ((f32[32,2,128,128]{3,2,1,0:T(8,128)}), f32[32,2,128,128]{3,2,1,0:T(8,128)}, u32[]{:S(2)}, u32[]{:S(2)}) async-start(f32[32,2,128,128]{3,2,1,0:T(8,128)} %pack_rows.1), calls=%async_computation | async-start | bytes 8388608 | tf_op jit(solution)/shard_map/all_to_all | solution.py:479
  12.7 2.6 %pack_columns.4 = (f32[2,2,128,128]{3,2,1,0:T(8,128)}, f32[2,2,128,128]{3,2,1,0:T(8,128)}, f32[2,2,128,128]{3,2,1,0:T(8,128)}) custom-call(s32[6]{0:T(128)} %select_reduce_fusion.ctab, f32[16,2,128,128]{3,2,1,0:T(8,128)} %rest_0_.5), custom_call_target="tpu_custom_call" | custom-call | bytes 1048576 | tf_op jit(solution)/shard_map/pack_columns/pallas_call | solution.py:189
  15.3 4.1 %collective-permute-start = (f32[2,2,128,128]{3,2,1,0:T(8,128)}, f32[2,2,128,128]{3,2,1,0:T(8,128)S(1)}, u32[]{:S(2)}, u32[]{:S(2)}) collective-permute-start(f32[2,2,128,128]{3,2,1,0:T(8,128)} %get-tuple-element.35), channel_id=1, source_target_pairs={{0,96},{32,0},{64,32},{96,64},{1,97},{33,1},{65,33},{97,65},{2,98}... | collective-permute-start | bytes 786440 | tf_op jit(solution)/shard_map/ppermute | solution.py:487
  24.3 6.9 %collective-permute-done.c1 = f32[2,2,128,128]{3,2,1,0:T(8,128)S(1)} collective-permute-done((f32[2,2,128,128]{3,2,1,0:T(8,128)}, f32[2,2,128,128]{3,2,1,0:T(8,128)S(1)}, u32[]{:S(2)}, u32[]{:S(2)}) %collective-permute-start) | collective-permute-done | bytes 262176 | tf_op jit(solution)/shard_map/ppermute | solution.py:487
  31.2 3.3 %collective-permute-done.2.c3 = f32[2,2,128,128]{3,2,1,0:T(8,128)S(1)} collective-permute-done((f32[2,2,128,128]{3,2,1,0:T(8,128)}, f32[2,2,128,128]{3,2,1,0:T(8,128)S(1)}, u32[]{:S(2)}, u32[]{:S(2)}) %collective-permute-start.2) | collective-permute-done | bytes 262176 | tf_op jit(solution)/shard_map/ppermute | solution.py:487
  36.7 8.6 %local_part.4 = (f32[16,2,128,128]{3,2,1,0:T(8,128)S(1)}, f32[32,2,128,128]{3,2,1,0:T(8,128)}) custom-call(s32[128]{0:T(128)S(1)} %reshape.155.tab, f32[176]{0:T(256)S(1)} %reshape.156.wts, f32[16,2,128,128]{3,2,1,0:T(8,128)S(1)} %copy-done.2, f32[2,2,128,128]{3,2,1,0:T(8,128)S(1)} %collective-permute-done.c1, ...), custom_call_target="tpu_custom_call" | custom-call | flops 5368709120 | bytes 8388608 | tf_op jit(solution)/shard_map/local_part/pallas_call | solution.py:156
  46.6 18.5 %all-to-all-done.recv = f32[32,2,128,128]{3,2,1,0:T(8,128)} async-done(((f32[32,2,128,128]{3,2,1,0:T(8,128)}), f32[32,2,128,128]{3,2,1,0:T(8,128)}, u32[]{:S(2)}, u32[]{:S(2)}) %all-to-all-start) | async-done | bytes 4194336 | tf_op jit(solution)/shard_map/all_to_all | solution.py:479
  66.5 4.9 %all-to-all-start.1 = ((f32[32,2,128,128]{3,2,1,0:T(8,128)}), f32[32,2,128,128]{3,2,1,0:T(8,128)}, u32[]{:S(2)}, u32[]{:S(2)}) async-start(f32[32,2,128,128]{3,2,1,0:T(8,128)} %get-tuple-element.44), calls=%async_computation.1 | async-start | bytes 8388608 | tf_op jit(solution)/shard_map/all_to_all | solution.py:479
  71.4 6.2 %row_part.5.z_ref.rest_0_ = f32[16,2,128,128]{3,2,1,0:T(8,128)} custom-call(s32[128]{0:T(128)S(1)} %reshape.155.tab, f32[176]{0:T(256)S(1)} %reshape.156.wts, s32[1]{0:T(128)} %get-tuple-element.45.token, f32[32,2,128,128]{3,2,1,0:T(8,128)} %all-to-all-done.recv, f32[16,2,128,128]{3,2,1,0:T(8,128)} %copy-done.6, bf16[256,256]{1,0:T(8,128)(2,1)S(1)} %copy-done.4, ...), custom_call_target="tpu_custom_call" | custom-call | flops 2147483648 | bytes 10485760 | tf_op jit(solution)/shard_map/row_part/pallas_call | solution.py:413
  77.6 2.7 %pack_columns.5 = (f32[2,2,128,128]{3,2,1,0:T(8,128)}, f32[2,2,128,128]{3,2,1,0:T(8,128)}, f32[2,2,128,128]{3,2,1,0:T(8,128)}) custom-call(s32[6]{0:T(128)} %select_reduce_fusion.ctab, f32[16,2,128,128]{3,2,1,0:T(8,128)} %row_part.5.z_ref.rest_0_), custom_call_target="tpu_custom_call" | custom-call | bytes 1048576 | tf_op jit(solution)/shard_map/pack_columns/pallas_call | solution.py:189
  80.3 4.1 %collective-permute-start.3 = (f32[2,2,128,128]{3,2,1,0:T(8,128)}, f32[2,2,128,128]{3,2,1,0:T(8,128)S(1)}, u32[]{:S(2)}, u32[]{:S(2)}) collective-permute-start(f32[2,2,128,128]{3,2,1,0:T(8,128)} %get-tuple-element.46), channel_id=1, source_target_pairs={{0,96},{32,0},{64,32},{96,64},{1,97},{33,1},{65,33},{97,65},{2,98}... | collective-permute-start | bytes 786440 | tf_op jit(solution)/shard_map/ppermute | solution.py:487
  85.6 10.4 %collective-permute-done.3.c1 = f32[2,2,128,128]{3,2,1,0:T(8,128)S(1)} collective-permute-done((f32[2,2,128,128]{3,2,1,0:T(8,128)}, f32[2,2,128,128]{3,2,1,0:T(8,128)S(1)}, u32[]{:S(2)}, u32[]{:S(2)}) %collective-permute-start.3) | collective-permute-done | bytes 262176 | tf_op jit(solution)/shard_map/ppermute | solution.py:487
  96.0 3.4 %collective-permute-done.5.c3 = f32[2,2,128,128]{3,2,1,0:T(8,128)S(1)} collective-permute-done((f32[2,2,128,128]{3,2,1,0:T(8,128)}, f32[2,2,128,128]{3,2,1,0:T(8,128)S(1)}, u32[]{:S(2)}, u32[]{:S(2)}) %collective-permute-start.5) | collective-permute-done | bytes 262176 | tf_op jit(solution)/shard_map/ppermute | solution.py:487
  102.0 9.0 %local_part.5 = (f32[16,2,128,128]{3,2,1,0:T(8,128)S(1)}, f32[32,2,128,128]{3,2,1,0:T(8,128)}, f32[16,2,128,128]{3,2,1,0:T(8,128)S(1)}) custom-call(s32[128]{0:T(128)S(1)} %reshape.155.tab, f32[176]{0:T(256)S(1)} %reshape.156.wts, f32[16,2,128,128]{3,2,1,0:T(8,128)S(1)} %copy-done.1, f32[2,2,128,128]{3,2,1,0:T(8,128)S(1)} %collective-permute-done.3.c1, ...), custom_call_target="tpu_custom_call" | custom-call | flops 5368709120 | bytes 8388608 | tf_op jit(solution)/shard_map/local_part/pallas_call | solution.py:156
  113.7 11.6 %all-to-all-done.1.recv = f32[32,2,128,128]{3,2,1,0:T(8,128)} async-done(((f32[32,2,128,128]{3,2,1,0:T(8,128)}), f32[32,2,128,128]{3,2,1,0:T(8,128)}, u32[]{:S(2)}, u32[]{:S(2)}) %all-to-all-start.1) | async-done | bytes 4194336 | tf_op jit(solution)/shard_map/all_to_all | solution.py:479
  126.7 4.9 %all-to-all-start.2 = ((f32[32,2,128,128]{3,2,1,0:T(8,128)}), f32[32,2,128,128]{3,2,1,0:T(8,128)}, u32[]{:S(2)}, u32[]{:S(2)}) async-start(f32[32,2,128,128]{3,2,1,0:T(8,128)} %get-tuple-element.51), calls=%async_computation.2 | async-start | bytes 8388608 | tf_op jit(solution)/shard_map/all_to_all | solution.py:479
  131.6 7.8 %row_part.6.z_ref.recv.rest_0_ = f32[16,2,128,128]{3,2,1,0:T(8,128)} custom-call(s32[128]{0:T(128)S(1)} %reshape.155.tab, f32[176]{0:T(256)S(1)} %reshape.156.wts, s32[1]{0:T(128)} %get-tuple-element.52.token, f32[32,2,128,128]{3,2,1,0:T(8,128)} %all-to-all-done.1.recv, f32[16,2,128,128]{3,2,1,0:T(8,128)} %copy-done.9, bf16[256,256]{1,0:T(8,128)(2,1)S(1)} %copy-done.4, ...), custom_call_target="tpu_custom_call" | custom-call | flops 2147483648 | bytes 10485760 | tf_op jit(solution)/shard_map/row_part/pallas_call | solution.py:413
  139.4 2.7 %pack_columns.6 = (f32[2,2,128,128]{3,2,1,0:T(8,128)}, f32[2,2,128,128]{3,2,1,0:T(8,128)}, f32[2,2,128,128]{3,2,1,0:T(8,128)}) custom-call(s32[6]{0:T(128)} %select_reduce_fusion.ctab, f32[16,2,128,128]{3,2,1,0:T(8,128)} %row_part.6.z_ref.recv.rest_0_), custom_call_target="tpu_custom_call" | custom-call | bytes 1048576 | tf_op jit(solution)/shard_map/pack_columns/pallas_call | solution.py:189
  142.1 4.0 %collective-permute-start.6 = (f32[2,2,128,128]{3,2,1,0:T(8,128)}, f32[2,2,128,128]{3,2,1,0:T(8,128)S(1)}, u32[]{:S(2)}, u32[]{:S(2)}) collective-permute-start(f32[2,2,128,128]{3,2,1,0:T(8,128)} %get-tuple-element.53), channel_id=1, source_target_pairs={{0,96},{32,0},{64,32},{96,64},{1,97},{33,1},{65,33},{97,65},{2,98}... | collective-permute-start | bytes 786440 | tf_op jit(solution)/shard_map/ppermute | solution.py:487
  147.5 10.4 %collective-permute-done.6.c1 = f32[2,2,128,128]{3,2,1,0:T(8,128)S(1)} collective-permute-done((f32[2,2,128,128]{3,2,1,0:T(8,128)}, f32[2,2,128,128]{3,2,1,0:T(8,128)S(1)}, u32[]{:S(2)}, u32[]{:S(2)}) %collective-permute-start.6) | collective-permute-done | bytes 262176 | tf_op jit(solution)/shard_map/ppermute | solution.py:487
  157.8 3.4 %collective-permute-done.8.c3 = f32[2,2,128,128]{3,2,1,0:T(8,128)S(1)} collective-permute-done((f32[2,2,128,128]{3,2,1,0:T(8,128)}, f32[2,2,128,128]{3,2,1,0:T(8,128)S(1)}, u32[]{:S(2)}, u32[]{:S(2)}) %collective-permute-start.8) | collective-permute-done | bytes 262176 | tf_op jit(solution)/shard_map/ppermute | solution.py:487
  163.9 9.0 %local_part.6 = (f32[16,2,128,128]{3,2,1,0:T(8,128)S(1)}, f32[32,2,128,128]{3,2,1,0:T(8,128)}, f32[16,2,128,128]{3,2,1,0:T(8,128)S(1)}) custom-call(s32[128]{0:T(128)S(1)} %reshape.155.tab, f32[176]{0:T(256)S(1)} %reshape.156.wts, f32[16,2,128,128]{3,2,1,0:T(8,128)S(1)} %copy-done, f32[2,2,128,128]{3,2,1,0:T(8,128)S(1)} %collective-permute-done.6.c1, ...), custom_call_target="tpu_custom_call" | custom-call | flops 5368709120 | bytes 8388608 | tf_op jit(solution)/shard_map/local_part/pallas_call | solution.py:156
  175.6 9.9 %all-to-all-done.2.recv = f32[32,2,128,128]{3,2,1,0:T(8,128)} async-done(((f32[32,2,128,128]{3,2,1,0:T(8,128)}), f32[32,2,128,128]{3,2,1,0:T(8,128)}, u32[]{:S(2)}, u32[]{:S(2)}) %all-to-all-start.2) | async-done | bytes 4194336 | tf_op jit(solution)/shard_map/all_to_all | solution.py:479
  186.9 4.9 %all-to-all-start.3 = ((f32[32,2,128,128]{3,2,1,0:T(8,128)}), f32[32,2,128,128]{3,2,1,0:T(8,128)}, u32[]{:S(2)}, u32[]{:S(2)}) async-start(f32[32,2,128,128]{3,2,1,0:T(8,128)} %get-tuple-element.60), calls=%async_computation.3 | async-start | bytes 8388608 | tf_op jit(solution)/shard_map/all_to_all | solution.py:479
  191.8 7.8 %row_part.7.z_ref = f32[16,2,128,128]{3,2,1,0:T(8,128)} custom-call(s32[128]{0:T(128)S(1)} %reshape.155.tab, f32[176]{0:T(256)S(1)} %reshape.156.wts, s32[1]{0:T(128)} %get-tuple-element.59.token, f32[32,2,128,128]{3,2,1,0:T(8,128)} %all-to-all-done.2.recv, f32[16,2,128,128]{3,2,1,0:T(8,128)} %copy-done.8, bf16[256,256]{1,0:T(8,128)(2,1)S(1)} %copy-done.4, ...), custom_call_target="tpu_custom_call" | custom-call | flops 2147483648 | bytes 10485760 | tf_op jit(solution)/shard_map/row_part/pallas_call | solution.py:413
  202.2 4.0 %collective-permute-start.9 = (f32[2,2,128,128]{3,2,1,0:T(8,128)}, f32[2,2,128,128]{3,2,1,0:T(8,128)S(1)}, u32[]{:S(2)}, u32[]{:S(2)}) collective-permute-start(f32[2,2,128,128]{3,2,1,0:T(8,128)} %get-tuple-element.61), channel_id=1, source_target_pairs={{0,96},{32,0},{64,32},{96,64},{1,97},{33,1},{65,33},{97,65},{2,98}... | collective-permute-start | bytes 786440 | tf_op jit(solution)/shard_map/ppermute | solution.py:487
  207.6 9.4 %row_part.8.rest_0_ = f32[16,2,128,128]{3,2,1,0:T(8,128)S(1)} custom-call(s32[128]{0:T(128)S(1)} %reshape.155.tab, f32[176]{0:T(256)S(1)} %reshape.156.wts, s32[1]{0:T(128)} %get-tuple-element.59.token, f32[16,2,128,128]{3,2,1,0:T(8,128)} %row_part.6.z_ref.recv.rest_0_, f32[16,2,128,128]{3,2,1,0:T(8,128)} %copy-done.10, bf16[256,256]{1,0:T(8,128)(2,1)S(1)} %copy-done.4, ...), custom_call_target="tpu_custom_call" | custom-call | flops 2147483648 | bytes 10485760 | tf_op jit(solution)/shard_map/row_part/pallas_call | solution.py:413
  217.9 3.4 %collective-permute-done.11.c3 = f32[2,2,128,128]{3,2,1,0:T(8,128)S(1)} collective-permute-done((f32[2,2,128,128]{3,2,1,0:T(8,128)}, f32[2,2,128,128]{3,2,1,0:T(8,128)S(1)}, u32[]{:S(2)}, u32[]{:S(2)}) %collective-permute-start.11) | collective-permute-done | bytes 262176 | tf_op jit(solution)/shard_map/ppermute | solution.py:487
  221.3 8.4 %local_part.7.part = f32[16,2,128,128]{3,2,1,0:T(8,128)S(1)} custom-call(s32[128]{0:T(128)S(1)} %reshape.155.tab, f32[176]{0:T(256)S(1)} %reshape.156.wts, f32[16,2,128,128]{3,2,1,0:T(8,128)S(1)} %copy-done.7, f32[2,2,128,128]{3,2,1,0:T(8,128)S(1)} %collective-permute-done.9.c1, f32[2,2,128,128]{3,2,1,0:T(8,128)S(1)} %collective-permute-done.10.c2, ...), custom_call_target="tpu_custom_call" | custom-call | flops 5368709120 | bytes 8388608 | tf_op jit(solution)/shard_map/local_part/pallas_call | solution.py:156
  231.1 14.7 %all-to-all-done.3.recv = f32[32,2,128,128]{3,2,1,0:T(8,128)} async-done(((f32[32,2,128,128]{3,2,1,0:T(8,128)}), f32[32,2,128,128]{3,2,1,0:T(8,128)}, u32[]{:S(2)}, u32[]{:S(2)}) %all-to-all-start.3) | async-done | bytes 4194336 | tf_op jit(solution)/shard_map/all_to_all | solution.py:479
  245.7 6.1 %row_part.9 = f32[16,2,128,128]{3,2,1,0:T(8,128)} custom-call(s32[128]{0:T(128)S(1)} %reshape.155.tab, f32[176]{0:T(256)S(1)} %reshape.156.wts, s32[1]{0:T(128)} %get-tuple-element.59.token, f32[32,2,128,128]{3,2,1,0:T(8,128)} %all-to-all-done.3.recv, f32[16,2,128,128]{3,2,1,0:T(8,128)} %copy-done.11, bf16[256,256]{1,0:T(8,128)(2,1)S(1)} %copy-done.4, ...), custom_call_target="tpu_custom_call" | custom-call | flops 2147483648 | bytes 10485760 | tf_op jit(solution)/shard_map/row_part/pallas_call | solution.py:413
  (101 shorter events, 33.5 us)
Async XLA Ops:
  3.5 7.7 %copy-start.20 = (s32[16,4]{0,1:T(4,128)S(1)}, s32[16,4]{0,1:T(4,128)}, u32[]{:S(2)}) copy-start(s32[16,4]{0,1:T(4,128)} %param.14) | copy-start | bytes 772
  3.5 7.7 %copy-start.21 = (s32[16,4]{0,1:T(4,128)S(1)}, s32[16,4]{0,1:T(4,128)}, u32[]{:S(2)}) copy-start(s32[16,4]{0,1:T(4,128)} %param.13) | copy-start | bytes 772
  3.5 61.6 %all-to-all-start = ((f32[32,2,128,128]{3,2,1,0:T(8,128)}), f32[32,2,128,128]{3,2,1,0:T(8,128)}, u32[]{:S(2)}, u32[]{:S(2)}) async-start(f32[32,2,128,128]{3,2,1,0:T(8,128)} %pack_rows.1), calls=%async_computation | async-start | bytes 8388608 | tf_op jit(solution)/shard_map/all_to_all | solution.py:479
  11.1 9.5 %copy-start.23 = (f32[2,4]{1,0:T(2,128)S(1)}, f32[2,4]{1,0:T(2,128)}, u32[]{:S(2)}) copy-start(f32[2,4]{1,0:T(2,128)} %param.12) | copy-start | bytes 100
  11.2 9.7 %copy-start.22 = (s32[16,4]{0,1:T(4,128)S(1)}, s32[16,4]{0,1:T(4,128)}, u32[]{:S(2)}) copy-start(s32[16,4]{0,1:T(4,128)} %param.15) | copy-start | bytes 772
  11.2 9.9 %copy-start.24 = (f32[4]{0:T(128)S(1)}, f32[4]{0:T(128)}, u32[]{:S(2)}) copy-start(f32[4]{0:T(128)} %param.11) | copy-start | bytes 52
  11.2 23.3 %copy-start.2 = (f32[16,2,128,128]{3,2,1,0:T(8,128)S(1)}, f32[16,2,128,128]{3,2,1,0:T(8,128)}, u32[]{:S(2)}) copy-start(f32[16,2,128,128]{3,2,1,0:T(8,128)} %rest_0_.5) | copy-start | bytes 6291460
  15.3 15.9 %collective-permute-start = (f32[2,2,128,128]{3,2,1,0:T(8,128)}, f32[2,2,128,128]{3,2,1,0:T(8,128)S(1)}, u32[]{:S(2)}, u32[]{:S(2)}) collective-permute-start(f32[2,2,128,128]{3,2,1,0:T(8,128)} %get-tuple-element.35), channel_id=1, source_target_pairs={{0,96},{32,0},{64,32},{96,64},{1,97},{33,1},{65,33},{97,65},{2,98}... | collective-permute-start | bytes 786440 | tf_op jit(solution)/shard_map/ppermute | solution.py:487
  19.4 11.8 %collective-permute-start.1 = (f32[2,2,128,128]{3,2,1,0:T(8,128)}, f32[2,2,128,128]{3,2,1,0:T(8,128)S(1)}, u32[]{:S(2)}, u32[]{:S(2)}) collective-permute-start(f32[2,2,128,128]{3,2,1,0:T(8,128)} %get-tuple-element.36), channel_id=1, source_target_pairs={{0,64},{32,96},{64,0},{96,32},{1,65},{33,97},{65,1},{97,33},{2,66}... | collective-permute-start | bytes 786440 | tf_op jit(solution)/shard_map/ppermute | solution.py:487
  19.4 15.1 %collective-permute-start.2 = (f32[2,2,128,128]{3,2,1,0:T(8,128)}, f32[2,2,128,128]{3,2,1,0:T(8,128)S(1)}, u32[]{:S(2)}, u32[]{:S(2)}) collective-permute-start(f32[2,2,128,128]{3,2,1,0:T(8,128)} %get-tuple-element.37), channel_id=1, source_target_pairs={{0,32},{32,64},{64,96},{96,0},{1,33},{33,65},{65,97},{97,1},{2,34}... | collective-permute-start | bytes 786440 | tf_op jit(solution)/shard_map/ppermute | solution.py:487
  36.7 28.5 %copy-start.4 = (bf16[256,256]{1,0:T(8,128)(2,1)S(1)}, bf16[256,256]{1,0:T(8,128)(2,1)}, u32[]{:S(2)}) copy-start(bf16[256,256]{1,0:T(8,128)(2,1)} %get-tuple-element.42.left) | copy-start | bytes 393220
  36.7 28.5 %copy-start.5 = (bf16[256,256]{1,0:T(8,128)(2,1)S(1)}, bf16[256,256]{1,0:T(8,128)(2,1)}, u32[]{:S(2)}) copy-start(bf16[256,256]{1,0:T(8,128)(2,1)} %get-tuple-element.43.right) | copy-start | bytes 393220
  66.5 58.8 %all-to-all-start.1 = ((f32[32,2,128,128]{3,2,1,0:T(8,128)}), f32[32,2,128,128]{3,2,1,0:T(8,128)}, u32[]{:S(2)}, u32[]{:S(2)}) async-start(f32[32,2,128,128]{3,2,1,0:T(8,128)} %get-tuple-element.44), calls=%async_computation.1 | async-start | bytes 8388608 | tf_op jit(solution)/shard_map/all_to_all | solution.py:479
  71.4 28.0 %copy-start.13 = (bf16[256,1280]{1,0:T(8,128)(2,1)S(1)}, bf16[256,1280]{1,0:T(8,128)(2,1)}, u32[]{:S(2)}) copy-start(bf16[256,1280]{1,0:T(8,128)(2,1)} %get-tuple-element.38.left) | copy-start | bytes 1966084
  77.6 21.8 %copy-start.1 = (f32[16,2,128,128]{3,2,1,0:T(8,128)S(1)}, f32[16,2,128,128]{3,2,1,0:T(8,128)}, u32[]{:S(2)}) copy-start(f32[16,2,128,128]{3,2,1,0:T(8,128)} %row_part.5.z_ref.rest_0_) | copy-start | bytes 6291460
  80.3 15.7 %collective-permute-start.3 = (f32[2,2,128,128]{3,2,1,0:T(8,128)}, f32[2,2,128,128]{3,2,1,0:T(8,128)S(1)}, u32[]{:S(2)}, u32[]{:S(2)}) collective-permute-start(f32[2,2,128,128]{3,2,1,0:T(8,128)} %get-tuple-element.46), channel_id=1, source_target_pairs={{0,96},{32,0},{64,32},{96,64},{1,97},{33,1},{65,33},{97,65},{2,98}... | collective-permute-start | bytes 786440 | tf_op jit(solution)/shard_map/ppermute | solution.py:487
  84.3 11.7 %collective-permute-start.4 = (f32[2,2,128,128]{3,2,1,0:T(8,128)}, f32[2,2,128,128]{3,2,1,0:T(8,128)S(1)}, u32[]{:S(2)}, u32[]{:S(2)}) collective-permute-start(f32[2,2,128,128]{3,2,1,0:T(8,128)} %get-tuple-element.47), channel_id=1, source_target_pairs={{0,64},{32,96},{64,0},{96,32},{1,65},{33,97},{65,1},{97,33},{2,66}... | collective-permute-start | bytes 786440 | tf_op jit(solution)/shard_map/ppermute | solution.py:487
  84.4 15.0 %collective-permute-start.5 = (f32[2,2,128,128]{3,2,1,0:T(8,128)}, f32[2,2,128,128]{3,2,1,0:T(8,128)S(1)}, u32[]{:S(2)}, u32[]{:S(2)}) collective-permute-start(f32[2,2,128,128]{3,2,1,0:T(8,128)} %get-tuple-element.48), channel_id=1, source_target_pairs={{0,32},{32,64},{64,96},{96,0},{1,33},{33,65},{65,97},{97,1},{2,34}... | collective-permute-start | bytes 786440 | tf_op jit(solution)/shard_map/ppermute | solution.py:487
  99.4 1.6 copy-start.3
  112.4 1.4 copy-start.18
  126.7 58.8 %all-to-all-start.2 = ((f32[32,2,128,128]{3,2,1,0:T(8,128)}), f32[32,2,128,128]{3,2,1,0:T(8,128)}, u32[]{:S(2)}, u32[]{:S(2)}) async-start(f32[32,2,128,128]{3,2,1,0:T(8,128)} %get-tuple-element.51), calls=%async_computation.2 | async-start | bytes 8388608 | tf_op jit(solution)/shard_map/all_to_all | solution.py:479
  139.4 21.8 %copy-start = (f32[16,2,128,128]{3,2,1,0:T(8,128)S(1)}, f32[16,2,128,128]{3,2,1,0:T(8,128)}, u32[]{:S(2)}) copy-start(f32[16,2,128,128]{3,2,1,0:T(8,128)} %row_part.6.z_ref.recv.rest_0_) | copy-start | bytes 6291460
  142.1 15.7 %collective-permute-start.6 = (f32[2,2,128,128]{3,2,1,0:T(8,128)}, f32[2,2,128,128]{3,2,1,0:T(8,128)S(1)}, u32[]{:S(2)}, u32[]{:S(2)}) collective-permute-start(f32[2,2,128,128]{3,2,1,0:T(8,128)} %get-tuple-element.53), channel_id=1, source_target_pairs={{0,96},{32,0},{64,32},{96,64},{1,97},{33,1},{65,33},{97,65},{2,98}... | collective-permute-start | bytes 786440 | tf_op jit(solution)/shard_map/ppermute | solution.py:487
  146.2 11.7 %collective-permute-start.7 = (f32[2,2,128,128]{3,2,1,0:T(8,128)}, f32[2,2,128,128]{3,2,1,0:T(8,128)S(1)}, u32[]{:S(2)}, u32[]{:S(2)}) collective-permute-start(f32[2,2,128,128]{3,2,1,0:T(8,128)} %get-tuple-element.54), channel_id=1, source_target_pairs={{0,64},{32,96},{64,0},{96,32},{1,65},{33,97},{65,1},{97,33},{2,66}... | collective-permute-start | bytes 786440 | tf_op jit(solution)/shard_map/ppermute | solution.py:487
  146.2 15.0 %collective-permute-start.8 = (f32[2,2,128,128]{3,2,1,0:T(8,128)}, f32[2,2,128,128]{3,2,1,0:T(8,128)S(1)}, u32[]{:S(2)}, u32[]{:S(2)}) collective-permute-start(f32[2,2,128,128]{3,2,1,0:T(8,128)} %get-tuple-element.55), channel_id=1, source_target_pairs={{0,32},{32,64},{64,96},{96,0},{1,33},{33,65},{65,97},{97,1},{2,34}... | collective-permute-start | bytes 786440 | tf_op jit(solution)/shard_map/ppermute | solution.py:487
  162.3 1.6 copy-start.19
  186.9 58.8 %all-to-all-start.3 = ((f32[32,2,128,128]{3,2,1,0:T(8,128)}), f32[32,2,128,128]{3,2,1,0:T(8,128)}, u32[]{:S(2)}, u32[]{:S(2)}) async-start(f32[32,2,128,128]{3,2,1,0:T(8,128)} %get-tuple-element.60), calls=%async_computation.3 | async-start | bytes 8388608 | tf_op jit(solution)/shard_map/all_to_all | solution.py:479
  202.2 15.7 %collective-permute-start.9 = (f32[2,2,128,128]{3,2,1,0:T(8,128)}, f32[2,2,128,128]{3,2,1,0:T(8,128)S(1)}, u32[]{:S(2)}, u32[]{:S(2)}) collective-permute-start(f32[2,2,128,128]{3,2,1,0:T(8,128)} %get-tuple-element.61), channel_id=1, source_target_pairs={{0,96},{32,0},{64,32},{96,64},{1,97},{33,1},{65,33},{97,65},{2,98}... | collective-permute-start | bytes 786440 | tf_op jit(solution)/shard_map/ppermute | solution.py:487
  206.3 11.7 %collective-permute-start.10 = (f32[2,2,128,128]{3,2,1,0:T(8,128)}, f32[2,2,128,128]{3,2,1,0:T(8,128)S(1)}, u32[]{:S(2)}, u32[]{:S(2)}) collective-permute-start(f32[2,2,128,128]{3,2,1,0:T(8,128)} %get-tuple-element.62), channel_id=1, source_target_pairs={{0,64},{32,96},{64,0},{96,32},{1,65},{33,97},{65,1},{97,33},{2,66}... | collective-permute-start | bytes 786440 | tf_op jit(solution)/shard_map/ppermute | solution.py:487
  206.3 15.0 %collective-permute-start.11 = (f32[2,2,128,128]{3,2,1,0:T(8,128)}, f32[2,2,128,128]{3,2,1,0:T(8,128)S(1)}, u32[]{:S(2)}, u32[]{:S(2)}) collective-permute-start(f32[2,2,128,128]{3,2,1,0:T(8,128)} %get-tuple-element.63), channel_id=1, source_target_pairs={{0,32},{32,64},{64,96},{96,0},{1,33},{33,65},{65,97},{97,1},{2,34}... | collective-permute-start | bytes 786440 | tf_op jit(solution)/shard_map/ppermute | solution.py:487
  207.6 13.7 %copy-start.7 = (f32[16,2,128,128]{3,2,1,0:T(8,128)S(1)}, f32[16,2,128,128]{3,2,1,0:T(8,128)}, u32[]{:S(2)}) copy-start(f32[16,2,128,128]{3,2,1,0:T(8,128)} %row_part.7.z_ref) | copy-start | bytes 6291460
  207.6 13.7 %copy-start.17 = (bf16[1280,256]{1,0:T(8,128)(2,1)S(1)}, bf16[1280,256]{1,0:T(8,128)(2,1)}, u32[]{:S(2)}) copy-start(bf16[1280,256]{1,0:T(8,128)(2,1)} %get-tuple-element.39.right) | copy-start | bytes 1966084
  (9 other events, 11.0 us)
